TPU v7x, 256 devices: a whole 4x4x8 slice. The times are simulated.
256 devices in a mesh: row: 16 (over y, z_hi), col: 16 (over x, z_lo, core).
Axes of the slice: x: 4, y: 4, z: 8 (z_hi: 4, z_lo: 2; z = z_hi * 2 + z_lo), core: 2. Of those that a mesh axis runs over, the one named last changes fastest.
Arguments:
- fit_tiles: bfloat16 [32, 96, 128, 128], P('row', 'col'), may hold values from -6 to 6
- aux_list: int32 [32, 96], P('row', 'col'), may hold values from 0 to 11, as said below
- aux_count: int32 [32, 16], P('row', 'col'), may hold values from 1 to 6, as said below
- metric: bfloat16 [192, 128, 128], P('col', 'row'), may hold values from -0.5 to 0.5
Outputs:
- exchange: float32 [4096, 4096], P('col', 'row')
Inputs may be any that keep to these rules, and one draw needn't show every extreme that they name: `aux_list`: within one atom block and one col shard, the first 6 slots name distinct auxiliary blocks. `aux_count`: counts follow a density per atom block; the largest is reached in every draw.
All inputs are finite; a program needn't handle non-finite values.
Results may differ from a plain program's by a relative error of at most 0.0015.
Values may be sent and summed in bfloat16 or wider, within the bound.
No kernel may reach another device: no remote copies, remote signals or barrier semaphores. Data moves between devices by JAX's collectives and lax.ppermute only.
A program may use at most 64 MiB of HBM per device.

v0:
```python
import jax
import jax.numpy as jnp
from jax import lax
from jax.sharding import PartitionSpec as P

AUXB = 128
QS = 6


def expand(fitted, marked, local_aux):
    onehot = (marked[:, :, None] == jnp.arange(local_aux, dtype=jnp.int32)[None, None, :]).astype(
        jnp.bfloat16
    )
    dense = jnp.einsum("asq,asmn->amqn", onehot, fitted, preferred_element_type=jnp.float32).astype(
        jnp.bfloat16
    )
    return dense.reshape(fitted.shape[0] * fitted.shape[2], local_aux * fitted.shape[3])


def local(fit_tiles, aux_list, aux_count, metric):
    slots = fit_tiles.shape[1]
    local_aux = metric.shape[0]
    full_metric = lax.all_gather(metric, "row", axis=1, tiled=True)
    alive = jnp.arange(slots, dtype=jnp.int32)[None, :] < aux_count
    marked = jnp.where(alive, aux_list, local_aux)
    picked = full_metric[aux_list]
    fitted = jnp.einsum(
        "asmk,askn->asmn", fit_tiles, picked, preferred_element_type=jnp.float32
    ).astype(jnp.bfloat16)
    dense = expand(fitted, marked, local_aux)
    factor = 1.0 / (QS * lax.axis_size("col") * AUXB) ** 0.5
    gathered = lax.all_gather(dense, "row", axis=0, tiled=True)
    summed = lax.psum_scatter(
        jnp.dot(gathered, dense.T, preferred_element_type=jnp.float32),
        "col",
        scatter_dimension=0,
        tiled=True,
    )
    return summed * factor


def solution(mesh):
    placed = (P("row", "col", None, None), P("row", "col"), P("row", "col"), P("col", "row", None))
    return jax.shard_map(
        local, mesh=mesh, in_specs=placed, out_specs=P("col", "row"), check_vma=False
    )
```

profile of v0, /device:TPU:8, one launch (start us, length us, event | category | flops | bytes accessed | tf_op | source)
XLA Modules:
  0.0 312.3 jit_solution(8098111673905659290)
XLA Ops:
  6.5 0.0 copy-start
  6.5 0.0 all-gather.2.cloned.1.call-start
  6.5 0.8 compare_select_fusion.1
  7.3 0.1 reshape.7
  7.4 44.8 %all_gather.6 = bf16[12,128,128]{2,1,0:T(8,128)(2,1)S(1)} all-gather(bf16[12,8,128]{2,1,0:T(8,128)(2,1)} %param.7), channel_id=1, replica_groups=mesh['row'=16,'col'=16] {'row'}, dimensions={1}, use_global_device_ids=true | all-gather | bytes 417792 | tf_op jit(solution)/shard_map/all_gather | solution.py:23
  52.2 0.6 gather_fusion
  52.8 0.0 copy-done
  52.8 0.4 fusion.5
  53.3 0.3 copy.6
  53.6 0.6 convolution_convert_fusion
  54.1 0.2 copy.11
  54.3 1.2 copy.8
  55.6 0.0 all-gather.2.cloned.1.call-update
  55.6 0.0 reduce-scatter.2.cloned.1.call-start
  55.6 149.9 %all-gather.2.cloned.1.call-done = bf16[4096,1536]{0,1:T(8,128)(2,1)} async-done(((bf16[256,1536]{0,1:T(8,128)(2,1)}), bf16[4096,1536]{0,1:T(8,128)(2,1)}) %all-gather.2.cloned.1.call-update) | async-done | bytes 12582928 | tf_op jit(solution)/shard_map/all_gather | solution.py:32
  205.5 10.2 %fusion.6 = f32[4096,256]{1,0:T(8,128)} fusion(bf16[4096,1536]{0,1:T(8,128)(2,1)} %all-gather.2.cloned.1.call-done, bf16[256,1536]{1,0:T(8,128)(2,1)S(1)} %bitcast.22), kind=kOutput, calls=%fused_computation.13 | convolution fusion | flops 3221225472 | bytes 17563648 | tf_op jit(solution)/shard_map/dot_general | solution.py:34
  215.8 0.0 reduce-scatter.2.cloned.1.call-update
  215.8 88.0 %reduce-scatter.2.cloned.1.call-done = f32[256,256]{1,0:T(8,128)} async-done(((f32[4096,256]{1,0:T(8,128)}), f32[256,256]{1,0:T(8,128)}) %reduce-scatter.2.cloned.1.call-update) | async-done | bytes 262160 | tf_op jit(solution)/shard_map/reduce_scatter | solution.py:33
  303.8 1.7 broadcast_multiply_fusion
  (1 shorter events, 0.0 us)
Async XLA Ops:
  6.5 46.3 %copy-start = (bf16[2,6,128,128]{3,2,1,0:T(8,128)(2,1)S(1)}, bf16[2,6,128,128]{3,2,1,0:T(8,128)(2,1)}, u32[]{:S(2)}) copy-start(bf16[2,6,128,128]{3,2,1,0:T(8,128)(2,1)} %param.4) | copy-start | bytes 1179652
  6.5 199.0 %all-gather.2.cloned.1.call-start = ((), (), s32[]{:S(2)}) async-start(), calls=%async_computation.1 | async-start | bytes 13369344 | tf_op jit(solution)/shard_map/all_gather | solution.py:32
  55.6 248.2 %reduce-scatter.2.cloned.1.call-start = ((), (), s32[]{:S(2)}) async-start(), calls=%async_computation.2 | async-start | bytes 4456448 | tf_op jit(solution)/shard_map/reduce_scatter | solution.py:33
Sparse Core Ops, SparseCore 0:
  55.7 149.7 all-gather.1
  215.9 87.8 reduce-scatter.1
where the time goes:
time: 313 us; the launch traced here: 312 us
  waiting for transfers between devices  238 us (76%)
  blocking collectives  44.8 us (14%)
  between operations  13.4 us (4%)
  matrix products  11.2 us (4%)
    all_gather x1, waiting for transfers between devices, local(): gathered = lax.all_gather(dense, 'row', axis=0, tiled=True)  150 us
    reduce_scatter x1, waiting for transfers between devices, local(): lax.psum_scatter(jnp.dot(gathered, dense.T, preferred_element_type=jnp.fl...  88 us
    all_gather x1, blocking collectives, local(): full_metric = lax.all_gather(metric, 'row', axis=1, tiled=True)  44.8 us
    dot_general x1, matrix products, local(): jnp.dot(gathered, dense.T, preferred_element_type=jnp.float32)  10.2 us
  transfers between devices with their start and end apart: 2, of which 2 were waited for; matrix products, arithmetic and copies ran while one was open for 0% of the time, Pallas kernels for 0%

commit v1 on v0

v1 whole, which is shorter than its diff:
```python
import functools

import jax
import jax.numpy as jnp
from jax import lax
from jax.experimental import pallas as pl
from jax.experimental.pallas import tpu as pltpu
from jax.sharding import Mesh, PartitionSpec as P


AUXB = 128
BS = 128
QS = 6
QB = 12
NA = 2
ROWS = NA * BS
WIDE = (QB + 1) * AUXB
USED = QB * AUXB
MROWS = 8
HALF = QS * BS
LISTS = 16
SECOND = HALF + LISTS
PAY = SECOND + HALF
F32 = jnp.float32
BF16 = jnp.bfloat16

SMEM = pl.BlockSpec(memory_space=pltpu.SMEM)
VMEM = pl.BlockSpec(memory_space=pltpu.VMEM)
PARAMS = pltpu.CompilerParams(vmem_limit_bytes=14 << 20)


def ring(n, k):
    return [(i, (i + k) % n) for i in range(n)]


def back(i, k):
    return lax.rem(i - k + 4, 4)


def pack_kernel(lists, counts, tiles, out):
    out[0:HALF, :] = tiles[0:HALF, :]
    out[SECOND:PAY, :] = tiles[HALF : 2 * HALF, :]
    lane = lax.broadcasted_iota(jnp.int32, (LISTS, AUXB), 1)
    row = jnp.full((LISTS, AUXB), QB, jnp.int32)
    for a in range(NA):
        for s in range(QS):
            q = jnp.where(s < counts[a, 0], lists[a, s], QB)
            row = jnp.where(lane == a * QS + s, q, row)
    out[HALF:SECOND, :] = row.astype(F32).astype(BF16)


def pack(aux_list, aux_count, tiles):
    return pl.pallas_call(
        pack_kernel,
        out_shape=jax.ShapeDtypeStruct((PAY, AUXB), BF16),
        in_specs=[SMEM, SMEM, VMEM],
        out_specs=VMEM,
        compiler_params=PARAMS,
        name="pack",
    )(aux_list, aux_count, tiles)


def line_kernel(sc_ref, m0, m1, m2, m3, out):
    zh = sc_ref[1]
    for src in range(4):
        k = back(zh, src)
        near = jnp.where(k == 0, m0[...].astype(F32), m1[...].astype(F32))
        far = jnp.where(k == 2, m2[...].astype(F32), m3[...].astype(F32))
        part = jnp.where(k < 2, near, far)
        out[:, src * MROWS : (src + 1) * MROWS, :] = part.astype(BF16)


def line(sc, parts):
    return pl.pallas_call(
        line_kernel,
        out_shape=jax.ShapeDtypeStruct((QB, 4 * MROWS, AUXB), BF16),
        in_specs=[SMEM] + [VMEM] * 4,
        out_specs=VMEM,
        compiler_params=PARAMS,
        name="line",
    )(sc, *parts)


def fill(tiles, start, met, lists, row, first, dense, base):
    for i in range(QS):
        q = lists[row, first + i]
        at = start + i * BS
        fitted = jnp.dot(tiles[at : at + BS, :], met[q], preferred_element_type=F32)
        cols = pl.ds(pl.multiple_of(q * AUXB, AUXB), AUXB)
        dense[pl.ds(pl.multiple_of(base, BS), BS), cols] = fitted.astype(BF16)


def fill_block(tiles, met, lists, row, dense, base):
    fill(tiles, 0, met, lists, row, 0, dense, base)
    fill(tiles, SECOND, met, lists, row, QS, dense, base + BS)


def list_row(tiles, at):
    return tiles[at : at + LISTS, :].astype(F32)[0:1, :].astype(jnp.int32)


def build_kernel(sc_ref, t0, t1, t2, t3, z1, z3, s0, s1, s2, s3, dy, dz, met, lv, ls, sem):
    y, zh = sc_ref[0], sc_ref[1]
    for n, t in enumerate((t0, t1, t2, t3, z1, z3)):
        lv[n : n + 1, :] = list_row(t, HALF)
    copy = pltpu.make_async_copy(lv, ls, sem)
    copy.start()
    for k, s in enumerate((s0, s1, s2, s3)):
        at = pl.multiple_of(back(y, k) * 4 * MROWS, 4 * MROWS)
        met[0:QB, pl.ds(at, 4 * MROWS), :] = s[...]
    dy[...] = jnp.zeros_like(dy)
    dz[...] = jnp.zeros_like(dz)
    copy.wait()
    fill_block(t0, met, ls, 0, dy, y * ROWS)
    mine = dy[pl.ds(pl.multiple_of(y * ROWS, ROWS), ROWS), :]
    dz[pl.ds(pl.multiple_of(zh * ROWS, ROWS), ROWS), :] = mine
    for k, t in ((1, t1), (2, t2), (3, t3)):
        fill_block(t, met, ls, k, dy, back(y, k) * ROWS)
    for n, k, t in ((4, 1, z1), (5, 3, z3)):
        fill_block(t, met, ls, n, dz, back(zh, k) * ROWS)


def build(sc, tiles, zs, smalls):
    dense = jax.ShapeDtypeStruct((4 * ROWS, WIDE), BF16)
    return pl.pallas_call(
        build_kernel,
        out_shape=(dense, dense, jax.ShapeDtypeStruct((QB + 1, AUXB, AUXB), BF16)),
        in_specs=[SMEM] + [VMEM] * 10,
        out_specs=(VMEM,) * 3,
        scratch_shapes=[
            pltpu.VMEM((8, 128), jnp.int32),
            pltpu.SMEM((8, 128), jnp.int32),
            pltpu.SemaphoreType.DMA,
        ],
        compiler_params=PARAMS,
        name="build",
    )(sc, *tiles, *zs, *smalls)


def gram_kernel(flip, h, sc_ref, dy, dz, met, f1, f3, out, far, lv, ls, sem):
    zh, co = sc_ref[1], sc_ref[2]
    p = 2 * h + (1 - co if flip else co)
    opposite = back(zh, 2)
    factor = 1.0 / (QS * 16 * AUXB) ** 0.5

    def product(rhs):
        for q in range(4):
            lhs = dy[q * ROWS : (q + 1) * ROWS, 0:USED]
            prod = lax.dot_general(
                lhs, rhs, (((1,), (1,)), ((), ())), preferred_element_type=F32
            )
            out[q] = prod * factor

    @pl.when(p == opposite)
    def _():
        lv[0:1, :] = list_row(f1, HALF)
        copy = pltpu.make_async_copy(lv, ls, sem)
        copy.start()
        far[...] = jnp.zeros_like(far)
        copy.wait()
        fill(f1, 0, met, ls, 0, 0, far, 0)
        fill(f3, LISTS, met, ls, 0, QS, far, BS)
        product(far[:, 0:USED])

    @pl.when(p != opposite)
    def _():
        product(dz[pl.ds(pl.multiple_of(p * ROWS, ROWS), ROWS), 0:USED])


def gram(flip, h, sc, dy, dz, met, f1, f3):
    return pl.pallas_call(
        functools.partial(gram_kernel, flip, h),
        out_shape=jax.ShapeDtypeStruct((4, ROWS, ROWS), F32),
        in_specs=[SMEM] + [VMEM] * 5,
        out_specs=VMEM,
        scratch_shapes=[
            pltpu.VMEM((ROWS, WIDE), BF16),
            pltpu.VMEM((8, 128), jnp.int32),
            pltpu.SMEM((8, 128), jnp.int32),
            pltpu.SemaphoreType.DMA,
        ],
        compiler_params=PARAMS,
    )(sc, dy, dz, met, f1, f3)


def share_kernel(sc_ref, keep, got, own, out1, out2, out3):
    x = sc_ref[3]
    for k, out in ((0, own), (1, out1), (2, out2), (3, out3)):
        i = lax.rem(x + k, 4)
        out[...] = (keep[i] + got[i]).astype(out.dtype)


def share(sc, keep, got):
    piece = (ROWS, ROWS)
    return pl.pallas_call(
        share_kernel,
        out_shape=(jax.ShapeDtypeStruct(piece, F32),) + (jax.ShapeDtypeStruct(piece, BF16),) * 3,
        in_specs=[SMEM, VMEM, VMEM],
        out_specs=(VMEM,) * 4,
        compiler_params=PARAMS,
        name="share",
    )(sc, keep, got)


def fold_kernel(sc_ref, a0, a1, a2, a3, b0, b1, b2, b3, mine, other):
    low = sc_ref[4] == 0
    first = a0[...] + a1[...].astype(F32) + a2[...].astype(F32) + a3[...].astype(F32)
    second = b0[...] + b1[...].astype(F32) + b2[...].astype(F32) + b3[...].astype(F32)
    mine[...] = jnp.where(low, first, second)
    other[...] = jnp.where(low, second, first).astype(BF16)


def fold(sc, first, second):
    piece = (ROWS, ROWS)
    return pl.pallas_call(
        fold_kernel,
        out_shape=(jax.ShapeDtypeStruct(piece, F32), jax.ShapeDtypeStruct(piece, BF16)),
        in_specs=[SMEM] + [VMEM] * 8,
        out_specs=(VMEM,) * 2,
        compiler_params=PARAMS,
        name="fold",
    )(sc, *first, *second)


def shift(v, axis, perm):
    return lax.ppermute(v, axis, perm)


def local(fit_tiles, aux_list, aux_count, metric):
    sc = jnp.stack([lax.axis_index(n) for n in ("y", "zh", "co", "x", "zl")]).astype(jnp.int32)
    mz = [metric] + [shift(metric, "zh", ring(4, k)) for k in (1, 2, 3)]
    pay = pack(aux_list, aux_count, fit_tiles.reshape(2 * HALF, AUXB))
    z1 = shift(pay, "zh", ring(4, 1))
    z3 = shift(pay, "zh", ring(4, 3))
    ys = [pay] + [shift(pay, "y", ring(4, k)) for k in (1, 2, 3)]
    small = line(sc, mz)
    smalls = [small] + [shift(small, "y", ring(4, k)) for k in (1, 2, 3)]
    f1 = shift(z1[:SECOND], "zh", ring(4, 1))
    f3 = shift(z3[HALF:], "zh", ring(4, 3))

    dy, dz, met = build(sc, ys, [z1, z3], smalls)
    sums = []
    for h in range(2):
        send = gram(True, h, sc, dy, dz, met, f1, f3)
        got = shift(send, "co", ring(2, 1))
        keep = gram(False, h, sc, dy, dz, met, f1, f3)
        own, *shares = share(sc, keep, got)
        sums.append([own] + [shift(shares[k - 1], "x", ring(4, k)) for k in (1, 2, 3)])
    mine, other = fold(sc, *sums)
    total = mine + shift(other, "zl", ring(2, 1)).astype(F32)
    swap = [(a * 4 + b, b * 4 + a) for a in range(4) for b in range(4)]
    return shift(total, ("zh", "zl", "co"), swap)


def solution(mesh):
    fine = Mesh(mesh.devices.reshape(4, 4, 4, 2, 2), ("y", "zh", "x", "zl", "co"))
    row, col = ("y", "zh"), ("x", "zl", "co")
    placed = (P(row, col, None, None), P(row, col), P(row, col), P(col, row, None))

    return jax.shard_map(local, mesh=fine, in_specs=placed, out_specs=P(col, row), check_vma=False)
```

time: 313 us -> 115 us (0.37)
  the two profiles are of different devices: /device:TPU:8 before, /device:TPU:32 now
where the time goes in v1:
time: 115 us
  waiting for transfers between devices  49.1 us (43%)
  starting transfers between devices  48.8 us (42%)
  Pallas kernels  13.1 us (11%)
  local copies, waits for them, and re-layouts  3.97 us (3%)
    ppermute x23, waiting for transfers between devices, shift(): return lax.ppermute(v, axis, perm)  49.1 us
    ppermute x23, starting transfers between devices, shift(): return lax.ppermute(v, axis, perm)  48.8 us
    pallas_call x4, Pallas kernels, gram(): pl.pallas_call(functools.partial(gram_kernel, flip, h), out_shape=jax.Sha...  7.4 us
    unnamed x8, local copies, waits for them, and re-layouts  3.85 us
    pallas_call x1, Pallas kernels, build(): pl.pallas_call(build_kernel, out_shape=(dense, dense, jax.ShapeDtypeStruc...  2.58 us
  transfers between devices with their start and end apart: 23, of which 9 were waited for; matrix products, arithmetic and copies ran while one was open for 0% of the time, Pallas kernels for 9%

profile of v1, /device:TPU:32, one launch (start us, length us, event | category | flops | bytes accessed | tf_op | source)
XLA Modules:
  0.0 115.2 jit_solution(7833489271769346882)
XLA Ops:
  0.0 0.7 copy.5.counts
  0.7 1.0 copy-done
  3.0 3.3 %collective-permute-start.3 = (bf16[1552,128]{1,0:T(8,128)(2,1)S(1)}, bf16[1552,128]{1,0:T(8,128)(2,1)S(1)}, u32[]{:S(2)}, u32[]{:S(2)}) collective-permute-start(bf16[1552,128]{1,0:T(8,128)(2,1)S(1)} %pack.1.t0), channel_id=1, source_target_pairs={{0,16},{16,32},{32,48},{48,0},{1,17},{17,33},{33,49},{49,1},{2,18}... | collective-permute-start | bytes 1191944 | tf_op jit(solution)/shard_map/ppermute | solution.py:226
  6.4 2.2 %collective-permute-start.4 = (bf16[1552,128]{1,0:T(8,128)(2,1)S(1)}, bf16[1552,128]{1,0:T(8,128)(2,1)S(1)}, u32[]{:S(2)}, u32[]{:S(2)}) collective-permute-start(bf16[1552,128]{1,0:T(8,128)(2,1)S(1)} %pack.1.t0), channel_id=1, source_target_pairs={{0,48},{16,0},{32,16},{48,32},{1,49},{17,1},{33,17},{49,33},{2,50}... | collective-permute-start | bytes 1191944 | tf_op jit(solution)/shard_map/ppermute | solution.py:226
  8.6 1.4 %collective-permute-start.5 = (bf16[12,8,128]{2,1,0:T(8,128)(2,1)}, bf16[12,8,128]{2,1,0:T(8,128)(2,1)S(1)}, u32[]{:S(2)}, u32[]{:S(2)}) collective-permute-start(bf16[12,8,128]{2,1,0:T(8,128)(2,1)} %m0.1), channel_id=1, source_target_pairs={{0,16},{16,32},{32,48},{48,0},{1,17},{17,33},{33,49},{49,1},{2,18}... | collective-permute-start | bytes 73736 | tf_op jit(solution)/shard_map/ppermute | solution.py:226
  9.9 3.8 %collective-permute-start.6 = (bf16[12,8,128]{2,1,0:T(8,128)(2,1)}, bf16[12,8,128]{2,1,0:T(8,128)(2,1)S(1)}, u32[]{:S(2)}, u32[]{:S(2)}) collective-permute-start(bf16[12,8,128]{2,1,0:T(8,128)(2,1)} %m0.1), channel_id=1, source_target_pairs={{0,32},{16,48},{32,0},{48,16},{1,33},{17,49},{33,1},{49,17},{2,34}... | collective-permute-start | bytes 73736 | tf_op jit(solution)/shard_map/ppermute | solution.py:226
  13.8 3.9 %collective-permute-start.7 = (bf16[12,8,128]{2,1,0:T(8,128)(2,1)}, bf16[12,8,128]{2,1,0:T(8,128)(2,1)S(1)}, u32[]{:S(2)}, u32[]{:S(2)}) collective-permute-start(bf16[12,8,128]{2,1,0:T(8,128)(2,1)} %m0.1), channel_id=1, source_target_pairs={{0,48},{16,0},{32,16},{48,32},{1,49},{17,1},{33,17},{49,33},{2,50}... | collective-permute-start | bytes 73736 | tf_op jit(solution)/shard_map/ppermute | solution.py:226
  17.7 10.6 %collective-permute-done.5.m1 = bf16[12,8,128]{2,1,0:T(8,128)(2,1)S(1)} collective-permute-done((bf16[12,8,128]{2,1,0:T(8,128)(2,1)}, bf16[12,8,128]{2,1,0:T(8,128)(2,1)S(1)}, u32[]{:S(2)}, u32[]{:S(2)}) %collective-permute-start.5) | collective-permute-done | bytes 24608 | tf_op jit(solution)/shard_map/ppermute | solution.py:226
  28.3 0.7 copy-done.1
  29.7 3.1 %collective-permute-start.10 = (bf16[12,32,128]{2,1,0:T(8,128)(2,1)S(1)}, bf16[12,32,128]{2,1,0:T(8,128)(2,1)S(1)}, u32[]{:S(2)}, u32[]{:S(2)}) collective-permute-start(bf16[12,32,128]{2,1,0:T(8,128)(2,1)S(1)} %line.1.s0), channel_id=1, source_target_pairs={{0,192},{64,0},{128,64},{192,128},{1,193},{65,1},{129,65},{193,129... | collective-permute-start | bytes 294920 | tf_op jit(solution)/shard_map/ppermute | solution.py:226
  32.7 2.2 %collective-permute-start.1 = (bf16[1552,128]{1,0:T(8,128)(2,1)S(1)}, bf16[1552,128]{1,0:T(8,128)(2,1)S(1)}, u32[]{:S(2)}, u32[]{:S(2)}) collective-permute-start(bf16[1552,128]{1,0:T(8,128)(2,1)S(1)} %pack.1.t0), channel_id=1, source_target_pairs={{0,128},{64,192},{128,0},{192,64},{1,129},{65,193},{129,1},{193,65... | collective-permute-start | bytes 1191944 | tf_op jit(solution)/shard_map/ppermute | solution.py:226
  35.0 3.6 %collective-permute-start.2 = (bf16[1552,128]{1,0:T(8,128)(2,1)S(1)}, bf16[1552,128]{1,0:T(8,128)(2,1)S(1)}, u32[]{:S(2)}, u32[]{:S(2)}) collective-permute-start(bf16[1552,128]{1,0:T(8,128)(2,1)S(1)} %pack.1.t0), channel_id=1, source_target_pairs={{0,192},{64,0},{128,64},{192,128},{1,193},{65,1},{129,65},{193,129... | collective-permute-start | bytes 1191944 | tf_op jit(solution)/shard_map/ppermute | solution.py:226
  38.6 1.5 %collective-permute-start.9 = (bf16[12,32,128]{2,1,0:T(8,128)(2,1)S(1)}, bf16[12,32,128]{2,1,0:T(8,128)(2,1)S(1)}, u32[]{:S(2)}, u32[]{:S(2)}) collective-permute-start(bf16[12,32,128]{2,1,0:T(8,128)(2,1)S(1)} %line.1.s0), channel_id=1, source_target_pairs={{0,128},{64,192},{128,0},{192,64},{1,129},{65,193},{129,1},{193,65... | collective-permute-start | bytes 294920 | tf_op jit(solution)/shard_map/ppermute | solution.py:226
  40.1 17.0 %collective-permute-done.8.s1 = bf16[12,32,128]{2,1,0:T(8,128)(2,1)S(1)} collective-permute-done((bf16[12,32,128]{2,1,0:T(8,128)(2,1)S(1)}, bf16[12,32,128]{2,1,0:T(8,128)(2,1)S(1)}, u32[]{:S(2)}, u32[]{:S(2)}) %collective-permute-start.8) | collective-permute-done | bytes 98336 | tf_op jit(solution)/shard_map/ppermute | solution.py:226
  57.6 3.6 %collective-permute-start.12 = (bf16[784,128]{1,0:T(8,128)(2,1)S(1)}, bf16[784,128]{1,0:T(8,128)(2,1)S(1)}, u32[]{:S(2)}, u32[]{:S(2)}) collective-permute-start(bf16[784,128]{1,0:T(8,128)(2,1)S(1)} %slice.9), channel_id=1, source_target_pairs={{0,48},{16,0},{32,16},{48,32},{1,49},{17,1},{33,17},{49,33},{2,50}... | collective-permute-start | bytes 602120 | tf_op jit(solution)/shard_map/ppermute | solution.py:226
  61.2 2.6 %build.1 = (bf16[1024,1664]{1,0:T(8,128)(2,1)S(1)}, bf16[1024,1664]{1,0:T(8,128)(2,1)S(1)}, bf16[13,128,128]{2,1,0:T(8,128)(2,1)S(1)}) custom-call(s32[5]{0:T(128)S(1)} %stack.23.sc_ref, bf16[1552,128]{1,0:T(8,128)(2,1)S(1)} %pack.1.t0, bf16[1552,128]{1,0:T(8,128)(2,1)S(1)} %collective-permute-done.t1, bf16[1552,128]{1,0:T(8,128)(2,1)S(1)} %collective-permute-done.1.t2, ...), custom_call_target="tpu_custom_call" | custom-call | tf_op jit(solution)/shard_map/build/pallas_call | solution.py:125
  63.8 2.2 %collective-permute-done.11.f1 = bf16[784,128]{1,0:T(8,128)(2,1)S(1)} collective-permute-done((bf16[784,128]{1,0:T(8,128)(2,1)S(1)}, bf16[784,128]{1,0:T(8,128)(2,1)S(1)}, u32[]{:S(2)}, u32[]{:S(2)}) %collective-permute-start.11) | collective-permute-done | bytes 200736 | tf_op jit(solution)/shard_map/ppermute | solution.py:226
  66.4 1.8 %shard_map.49 = f32[4,256,256]{2,1,0:T(8,128)S(1)} custom-call(s32[5]{0:T(128)S(1)} %stack.23.sc_ref, bf16[1024,1664]{1,0:T(8,128)(2,1)S(1)} %get-tuple-element.18.dy, bf16[1024,1664]{1,0:T(8,128)(2,1)S(1)} %get-tuple-element.19.dz, bf16[13,128,128]{2,1,0:T(8,128)(2,1)S(1)} %get-tuple-element.20.met, bf16[784,128]{1,0:T(8,128)(2,1)S(1)} %collective-permute-done.11.f1, ...), custom_call_target="tpu_custom_call" | custom-call | tf_op jit(solution)/shard_map/pallas_call | solution.py:171
  68.3 1.6 %shard_map.47 = f32[4,256,256]{2,1,0:T(8,128)S(1)} custom-call(s32[5]{0:T(128)S(1)} %stack.23.sc_ref, bf16[1024,1664]{1,0:T(8,128)(2,1)S(1)} %get-tuple-element.18.dy, bf16[1024,1664]{1,0:T(8,128)(2,1)S(1)} %get-tuple-element.19.dz, bf16[13,128,128]{2,1,0:T(8,128)(2,1)S(1)} %get-tuple-element.20.met, bf16[784,128]{1,0:T(8,128)(2,1)S(1)} %collective-permute-done.11.f1, ...), custom_call_target="tpu_custom_call" | custom-call | tf_op jit(solution)/shard_map/pallas_call | solution.py:171
  70.5 2.5 %shard_map.48.keep = f32[4,256,256]{2,1,0:T(8,128)S(1)} custom-call(s32[5]{0:T(128)S(1)} %stack.23.sc_ref, bf16[1024,1664]{1,0:T(8,128)(2,1)S(1)} %get-tuple-element.18.dy, bf16[1024,1664]{1,0:T(8,128)(2,1)S(1)} %get-tuple-element.19.dz, bf16[13,128,128]{2,1,0:T(8,128)(2,1)S(1)} %get-tuple-element.20.met, bf16[784,128]{1,0:T(8,128)(2,1)S(1)} %collective-permute-done.11.f1, ...), custom_call_target="tpu_custom_call" | custom-call | tf_op jit(solution)/shard_map/pallas_call | solution.py:171
  73.6 1.6 %collective-permute-start.18 = (bf16[256,256]{1,0:T(8,128)(2,1)S(1)}, bf16[256,256]{1,0:T(8,128)(2,1)S(1)}, u32[]{:S(2)}, u32[]{:S(2)}) collective-permute-start(bf16[256,256]{1,0:T(8,128)(2,1)S(1)} %get-tuple-element.26), channel_id=1, source_target_pairs={{0,4},{4,8},{8,12},{12,0},{1,5},{5,9},{9,13},{13,1},{2,6},{6,10},{... | collective-permute-start | bytes 393224 | tf_op jit(solution)/shard_map/ppermute | solution.py:226
  75.2 1.6 %shard_map.46.keep = f32[4,256,256]{2,1,0:T(8,128)S(1)} custom-call(s32[5]{0:T(128)S(1)} %stack.23.sc_ref, bf16[1024,1664]{1,0:T(8,128)(2,1)S(1)} %get-tuple-element.18.dy, bf16[1024,1664]{1,0:T(8,128)(2,1)S(1)} %get-tuple-element.19.dz, bf16[13,128,128]{2,1,0:T(8,128)(2,1)S(1)} %get-tuple-element.20.met, bf16[784,128]{1,0:T(8,128)(2,1)S(1)} %collective-permute-done.11.f1, ...), custom_call_target="tpu_custom_call" | custom-call | tf_op jit(solution)/shard_map/pallas_call | solution.py:171
  76.8 2.8 %collective-permute-start.19 = (bf16[256,256]{1,0:T(8,128)(2,1)S(1)}, bf16[256,256]{1,0:T(8,128)(2,1)S(1)}, u32[]{:S(2)}, u32[]{:S(2)}) collective-permute-start(bf16[256,256]{1,0:T(8,128)(2,1)S(1)} %get-tuple-element.27), channel_id=1, source_target_pairs={{0,8},{4,12},{8,0},{12,4},{1,9},{5,13},{9,1},{13,5},{2,10},{6,14},... | collective-permute-start | bytes 393224 | tf_op jit(solution)/shard_map/ppermute | solution.py:226
  79.6 1.4 %collective-permute-start.20 = (bf16[256,256]{1,0:T(8,128)(2,1)S(1)}, bf16[256,256]{1,0:T(8,128)(2,1)S(1)}, u32[]{:S(2)}, u32[]{:S(2)}) collective-permute-start(bf16[256,256]{1,0:T(8,128)(2,1)S(1)} %get-tuple-element.28), channel_id=1, source_target_pairs={{0,12},{4,0},{8,4},{12,8},{1,13},{5,1},{9,5},{13,9},{2,14},{6,2},{... | collective-permute-start | bytes 393224 | tf_op jit(solution)/shard_map/ppermute | solution.py:226
  82.3 0.9 collective-permute-start.15
  83.2 1.9 %collective-permute-start.16 = (bf16[256,256]{1,0:T(8,128)(2,1)S(1)}, bf16[256,256]{1,0:T(8,128)(2,1)S(1)}, u32[]{:S(2)}, u32[]{:S(2)}) collective-permute-start(bf16[256,256]{1,0:T(8,128)(2,1)S(1)} %get-tuple-element.24), channel_id=1, source_target_pairs={{0,12},{4,0},{8,4},{12,8},{1,13},{5,1},{9,5},{13,9},{2,14},{6,2},{... | collective-permute-start | bytes 393224 | tf_op jit(solution)/shard_map/ppermute | solution.py:226
  85.8 4.4 %collective-permute-done.14.a1 = bf16[256,256]{1,0:T(8,128)(2,1)S(1)} collective-permute-done((bf16[256,256]{1,0:T(8,128)(2,1)S(1)}, bf16[256,256]{1,0:T(8,128)(2,1)S(1)}, u32[]{:S(2)}, u32[]{:S(2)}) %collective-permute-start.14) | collective-permute-done | bytes 131104 | tf_op jit(solution)/shard_map/ppermute | solution.py:226
  91.2 3.6 %collective-permute-start.21 = (bf16[256,256]{1,0:T(8,128)(2,1)S(1)}, bf16[256,256]{1,0:T(8,128)(2,1)S(1)}, u32[]{:S(2)}, u32[]{:S(2)}) collective-permute-start(bf16[256,256]{1,0:T(8,128)(2,1)S(1)} %get-tuple-element.30), channel_id=1, source_target_pairs={{0,2},{2,0},{1,3},{3,1},{4,6},{6,4},{5,7},{7,5},{8,10},{10,8},{9,1... | collective-permute-start | bytes 393224 | tf_op jit(solution)/shard_map/ppermute | solution.py:226
  94.9 2.9 %collective-permute-done.21 = bf16[256,256]{1,0:T(8,128)(2,1)S(1)} collective-permute-done((bf16[256,256]{1,0:T(8,128)(2,1)S(1)}, bf16[256,256]{1,0:T(8,128)(2,1)S(1)}, u32[]{:S(2)}, u32[]{:S(2)}) %collective-permute-start.21) | collective-permute-done | bytes 131104 | tf_op jit(solution)/shard_map/ppermute | solution.py:226
  97.8 6.1 %collective-permute-start.22 = (f32[256,256]{1,0:T(8,128)S(1)}, f32[256,256]{1,0:T(8,128)S(1)}, u32[]{:S(2)}, u32[]{:S(2)}) collective-permute-start(f32[256,256]{1,0:T(8,128)S(1)} %convert_add_fusion), channel_id=1, source_target_pairs={{0,0},{1,16},{2,32},{3,48},{16,1},{17,17},{18,33},{19,49},{32,2},{... | collective-permute-start | bytes 786440 | tf_op jit(solution)/shard_map/ppermute | solution.py:226
  103.9 10.6 %collective-permute-done.22 = f32[256,256]{1,0:T(8,128)S(1)} collective-permute-done((f32[256,256]{1,0:T(8,128)S(1)}, f32[256,256]{1,0:T(8,128)S(1)}, u32[]{:S(2)}, u32[]{:S(2)}) %collective-permute-start.22) | collective-permute-done | bytes 262176 | tf_op jit(solution)/shard_map/ppermute | solution.py:226
  114.5 0.7 copy.7
  (36 shorter events, 7.4 us)
Async XLA Ops:
  0.7 1.0 copy-start
  1.7 0.7 copy-start.2
  3.0 35.6 %collective-permute-start.3 = (bf16[1552,128]{1,0:T(8,128)(2,1)S(1)}, bf16[1552,128]{1,0:T(8,128)(2,1)S(1)}, u32[]{:S(2)}, u32[]{:S(2)}) collective-permute-start(bf16[1552,128]{1,0:T(8,128)(2,1)S(1)} %pack.1.t0), channel_id=1, source_target_pairs={{0,16},{16,32},{32,48},{48,0},{1,17},{17,33},{33,49},{49,1},{2,18}... | collective-permute-start | bytes 1191944 | tf_op jit(solution)/shard_map/ppermute | solution.py:226
  6.4 32.2 %collective-permute-start.4 = (bf16[1552,128]{1,0:T(8,128)(2,1)S(1)}, bf16[1552,128]{1,0:T(8,128)(2,1)S(1)}, u32[]{:S(2)}, u32[]{:S(2)}) collective-permute-start(bf16[1552,128]{1,0:T(8,128)(2,1)S(1)} %pack.1.t0), channel_id=1, source_target_pairs={{0,48},{16,0},{32,16},{48,32},{1,49},{17,1},{33,17},{49,33},{2,50}... | collective-permute-start | bytes 1191944 | tf_op jit(solution)/shard_map/ppermute | solution.py:226
  8.6 19.7 %collective-permute-start.5 = (bf16[12,8,128]{2,1,0:T(8,128)(2,1)}, bf16[12,8,128]{2,1,0:T(8,128)(2,1)S(1)}, u32[]{:S(2)}, u32[]{:S(2)}) collective-permute-start(bf16[12,8,128]{2,1,0:T(8,128)(2,1)} %m0.1), channel_id=1, source_target_pairs={{0,16},{16,32},{32,48},{48,0},{1,17},{17,33},{33,49},{49,1},{2,18}... | collective-permute-start | bytes 73736 | tf_op jit(solution)/shard_map/ppermute | solution.py:226
  9.9 18.4 %collective-permute-start.6 = (bf16[12,8,128]{2,1,0:T(8,128)(2,1)}, bf16[12,8,128]{2,1,0:T(8,128)(2,1)S(1)}, u32[]{:S(2)}, u32[]{:S(2)}) collective-permute-start(bf16[12,8,128]{2,1,0:T(8,128)(2,1)} %m0.1), channel_id=1, source_target_pairs={{0,32},{16,48},{32,0},{48,16},{1,33},{17,49},{33,1},{49,17},{2,34}... | collective-permute-start | bytes 73736 | tf_op jit(solution)/shard_map/ppermute | solution.py:226
  13.8 14.5 %collective-permute-start.7 = (bf16[12,8,128]{2,1,0:T(8,128)(2,1)}, bf16[12,8,128]{2,1,0:T(8,128)(2,1)S(1)}, u32[]{:S(2)}, u32[]{:S(2)}) collective-permute-start(bf16[12,8,128]{2,1,0:T(8,128)(2,1)} %m0.1), channel_id=1, source_target_pairs={{0,48},{16,0},{32,16},{48,32},{1,49},{17,1},{33,17},{49,33},{2,50}... | collective-permute-start | bytes 73736 | tf_op jit(solution)/shard_map/ppermute | solution.py:226
  28.3 0.7 copy-start.1
  29.7 5.3 %collective-permute-start.10 = (bf16[12,32,128]{2,1,0:T(8,128)(2,1)S(1)}, bf16[12,32,128]{2,1,0:T(8,128)(2,1)S(1)}, u32[]{:S(2)}, u32[]{:S(2)}) collective-permute-start(bf16[12,32,128]{2,1,0:T(8,128)(2,1)S(1)} %line.1.s0), channel_id=1, source_target_pairs={{0,192},{64,0},{128,64},{192,128},{1,193},{65,1},{129,65},{193,129... | collective-permute-start | bytes 294920 | tf_op jit(solution)/shard_map/ppermute | solution.py:226
  32.7 28.5 %collective-permute-start = (bf16[1552,128]{1,0:T(8,128)(2,1)S(1)}, bf16[1552,128]{1,0:T(8,128)(2,1)S(1)}, u32[]{:S(2)}, u32[]{:S(2)}) collective-permute-start(bf16[1552,128]{1,0:T(8,128)(2,1)S(1)} %pack.1.t0), channel_id=1, source_target_pairs={{0,64},{64,128},{128,192},{192,0},{1,65},{65,129},{129,193},{193,1... | collective-permute-start | bytes 1191944 | tf_op jit(solution)/shard_map/ppermute | solution.py:226
  32.7 28.5 %collective-permute-start.1 = (bf16[1552,128]{1,0:T(8,128)(2,1)S(1)}, bf16[1552,128]{1,0:T(8,128)(2,1)S(1)}, u32[]{:S(2)}, u32[]{:S(2)}) collective-permute-start(bf16[1552,128]{1,0:T(8,128)(2,1)S(1)} %pack.1.t0), channel_id=1, source_target_pairs={{0,128},{64,192},{128,0},{192,64},{1,129},{65,193},{129,1},{193,65... | collective-permute-start | bytes 1191944 | tf_op jit(solution)/shard_map/ppermute | solution.py:226
  35.0 26.3 %collective-permute-start.2 = (bf16[1552,128]{1,0:T(8,128)(2,1)S(1)}, bf16[1552,128]{1,0:T(8,128)(2,1)S(1)}, u32[]{:S(2)}, u32[]{:S(2)}) collective-permute-start(bf16[1552,128]{1,0:T(8,128)(2,1)S(1)} %pack.1.t0), channel_id=1, source_target_pairs={{0,192},{64,0},{128,64},{192,128},{1,193},{65,1},{129,65},{193,129... | collective-permute-start | bytes 1191944 | tf_op jit(solution)/shard_map/ppermute | solution.py:226
  38.6 18.5 %collective-permute-start.8 = (bf16[12,32,128]{2,1,0:T(8,128)(2,1)S(1)}, bf16[12,32,128]{2,1,0:T(8,128)(2,1)S(1)}, u32[]{:S(2)}, u32[]{:S(2)}) collective-permute-start(bf16[12,32,128]{2,1,0:T(8,128)(2,1)S(1)} %line.1.s0), channel_id=1, source_target_pairs={{0,64},{64,128},{128,192},{192,0},{1,65},{65,129},{129,193},{193,1... | collective-permute-start | bytes 294920 | tf_op jit(solution)/shard_map/ppermute | solution.py:226
  38.6 19.0 %collective-permute-start.9 = (bf16[12,32,128]{2,1,0:T(8,128)(2,1)S(1)}, bf16[12,32,128]{2,1,0:T(8,128)(2,1)S(1)}, u32[]{:S(2)}, u32[]{:S(2)}) collective-permute-start(bf16[12,32,128]{2,1,0:T(8,128)(2,1)S(1)} %line.1.s0), channel_id=1, source_target_pairs={{0,128},{64,192},{128,0},{192,64},{1,129},{65,193},{129,1},{193,65... | collective-permute-start | bytes 294920 | tf_op jit(solution)/shard_map/ppermute | solution.py:226
  57.1 8.9 %collective-permute-start.11 = (bf16[784,128]{1,0:T(8,128)(2,1)S(1)}, bf16[784,128]{1,0:T(8,128)(2,1)S(1)}, u32[]{:S(2)}, u32[]{:S(2)}) collective-permute-start(bf16[784,128]{1,0:T(8,128)(2,1)S(1)} %slice.8), channel_id=1, source_target_pairs={{0,16},{16,32},{32,48},{48,0},{1,17},{17,33},{33,49},{49,1},{2,18}... | collective-permute-start | bytes 602120 | tf_op jit(solution)/shard_map/ppermute | solution.py:226
  57.6 8.8 %collective-permute-start.12 = (bf16[784,128]{1,0:T(8,128)(2,1)S(1)}, bf16[784,128]{1,0:T(8,128)(2,1)S(1)}, u32[]{:S(2)}, u32[]{:S(2)}) collective-permute-start(bf16[784,128]{1,0:T(8,128)(2,1)S(1)} %slice.9), channel_id=1, source_target_pairs={{0,48},{16,0},{32,16},{48,32},{1,49},{17,1},{33,17},{49,33},{2,50}... | collective-permute-start | bytes 602120 | tf_op jit(solution)/shard_map/ppermute | solution.py:226
  68.2 4.8 %collective-permute-start.17 = (f32[4,256,256]{2,1,0:T(8,128)S(1)}, f32[4,256,256]{2,1,0:T(8,128)S(1)}, u32[]{:S(2)}, u32[]{:S(2)}) collective-permute-start(f32[4,256,256]{2,1,0:T(8,128)S(1)} %shard_map.49), channel_id=1, source_target_pairs={{0,1},{1,0},{2,3},{3,2},{4,5},{5,4},{6,7},{7,6},{8,9},{9,8},{10,11... | collective-permute-start | bytes 3145736 | tf_op jit(solution)/shard_map/ppermute | solution.py:226
  69.9 11.1 %collective-permute-start.13 = (f32[4,256,256]{2,1,0:T(8,128)S(1)}, f32[4,256,256]{2,1,0:T(8,128)S(1)}, u32[]{:S(2)}, u32[]{:S(2)}) collective-permute-start(f32[4,256,256]{2,1,0:T(8,128)S(1)} %shard_map.47), channel_id=1, source_target_pairs={{0,1},{1,0},{2,3},{3,2},{4,5},{5,4},{6,7},{7,6},{8,9},{9,8},{10,11... | collective-permute-start | bytes 3145736 | tf_op jit(solution)/shard_map/ppermute | solution.py:226
  73.6 9.6 %collective-permute-start.18 = (bf16[256,256]{1,0:T(8,128)(2,1)S(1)}, bf16[256,256]{1,0:T(8,128)(2,1)S(1)}, u32[]{:S(2)}, u32[]{:S(2)}) collective-permute-start(bf16[256,256]{1,0:T(8,128)(2,1)S(1)} %get-tuple-element.26), channel_id=1, source_target_pairs={{0,4},{4,8},{8,12},{12,0},{1,5},{5,9},{9,13},{13,1},{2,6},{6,10},{... | collective-permute-start | bytes 393224 | tf_op jit(solution)/shard_map/ppermute | solution.py:226
  76.8 8.4 %collective-permute-start.19 = (bf16[256,256]{1,0:T(8,128)(2,1)S(1)}, bf16[256,256]{1,0:T(8,128)(2,1)S(1)}, u32[]{:S(2)}, u32[]{:S(2)}) collective-permute-start(bf16[256,256]{1,0:T(8,128)(2,1)S(1)} %get-tuple-element.27), channel_id=1, source_target_pairs={{0,8},{4,12},{8,0},{12,4},{1,9},{5,13},{9,1},{13,5},{2,10},{6,14},... | collective-permute-start | bytes 393224 | tf_op jit(solution)/shard_map/ppermute | solution.py:226
  79.6 6.2 %collective-permute-start.20 = (bf16[256,256]{1,0:T(8,128)(2,1)S(1)}, bf16[256,256]{1,0:T(8,128)(2,1)S(1)}, u32[]{:S(2)}, u32[]{:S(2)}) collective-permute-start(bf16[256,256]{1,0:T(8,128)(2,1)S(1)} %get-tuple-element.28), channel_id=1, source_target_pairs={{0,12},{4,0},{8,4},{12,8},{1,13},{5,1},{9,5},{13,9},{2,14},{6,2},{... | collective-permute-start | bytes 393224 | tf_op jit(solution)/shard_map/ppermute | solution.py:226
  81.7 8.5 %collective-permute-start.14 = (bf16[256,256]{1,0:T(8,128)(2,1)S(1)}, bf16[256,256]{1,0:T(8,128)(2,1)S(1)}, u32[]{:S(2)}, u32[]{:S(2)}) collective-permute-start(bf16[256,256]{1,0:T(8,128)(2,1)S(1)} %get-tuple-element.22), channel_id=1, source_target_pairs={{0,4},{4,8},{8,12},{12,0},{1,5},{5,9},{9,13},{13,1},{2,6},{6,10},{... | collective-permute-start | bytes 393224 | tf_op jit(solution)/shard_map/ppermute | solution.py:226
  82.3 7.8 %collective-permute-start.15 = (bf16[256,256]{1,0:T(8,128)(2,1)S(1)}, bf16[256,256]{1,0:T(8,128)(2,1)S(1)}, u32[]{:S(2)}, u32[]{:S(2)}) collective-permute-start(bf16[256,256]{1,0:T(8,128)(2,1)S(1)} %get-tuple-element.23), channel_id=1, source_target_pairs={{0,8},{4,12},{8,0},{12,4},{1,9},{5,13},{9,1},{13,5},{2,10},{6,14},... | collective-permute-start | bytes 393224 | tf_op jit(solution)/shard_map/ppermute | solution.py:226
  83.2 7.3 %collective-permute-start.16 = (bf16[256,256]{1,0:T(8,128)(2,1)S(1)}, bf16[256,256]{1,0:T(8,128)(2,1)S(1)}, u32[]{:S(2)}, u32[]{:S(2)}) collective-permute-start(bf16[256,256]{1,0:T(8,128)(2,1)S(1)} %get-tuple-element.24), channel_id=1, source_target_pairs={{0,12},{4,0},{8,4},{12,8},{1,13},{5,1},{9,5},{13,9},{2,14},{6,2},{... | collective-permute-start | bytes 393224 | tf_op jit(solution)/shard_map/ppermute | solution.py:226
  91.2 6.6 %collective-permute-start.21 = (bf16[256,256]{1,0:T(8,128)(2,1)S(1)}, bf16[256,256]{1,0:T(8,128)(2,1)S(1)}, u32[]{:S(2)}, u32[]{:S(2)}) collective-permute-start(bf16[256,256]{1,0:T(8,128)(2,1)S(1)} %get-tuple-element.30), channel_id=1, source_target_pairs={{0,2},{2,0},{1,3},{3,1},{4,6},{6,4},{5,7},{7,5},{8,10},{10,8},{9,1... | collective-permute-start | bytes 393224 | tf_op jit(solution)/shard_map/ppermute | solution.py:226
  97.8 16.6 %collective-permute-start.22 = (f32[256,256]{1,0:T(8,128)S(1)}, f32[256,256]{1,0:T(8,128)S(1)}, u32[]{:S(2)}, u32[]{:S(2)}) collective-permute-start(f32[256,256]{1,0:T(8,128)S(1)} %convert_add_fusion), channel_id=1, source_target_pairs={{0,0},{1,16},{2,32},{3,48},{16,1},{17,17},{18,33},{19,49},{32,2},{... | collective-permute-start | bytes 786440 | tf_op jit(solution)/shard_map/ppermute | solution.py:226

commit v2 on v1

v2 whole, which is shorter than its diff:
```python
import functools

import jax
import jax.numpy as jnp
from jax import lax
from jax.experimental import pallas as pl
from jax.experimental.pallas import tpu as pltpu
from jax.sharding import Mesh, PartitionSpec as P


AUXB = 128
BS = 128
QS = 6
QB = 12
NA = 2
ROWS = NA * BS
WIDE = (QB + 1) * AUXB
USED = QB * AUXB
MROWS = 8
HALF = QS * BS
PART = QB * MROWS
LIST0 = 4 * PART
SMALL = LIST0 + 16
F32 = jnp.float32
BF16 = jnp.bfloat16

SMEM = pl.BlockSpec(memory_space=pltpu.SMEM)
VMEM = pl.BlockSpec(memory_space=pltpu.VMEM)
PARAMS = pltpu.CompilerParams(vmem_limit_bytes=14 << 20)


def ring(n, k):
    return [(i, (i + k) % n) for i in range(n)]


def back(i, k):
    return lax.rem(i - k + 4, 4)


def pack_kernel(lists, counts, metric, out):
    out[0:PART, :] = metric[...]
    slot = lax.broadcasted_iota(jnp.int32, (NA, QS), 1)
    marked = jnp.where(slot < counts[...], lists[...], QB)
    tail = jnp.concatenate([marked, jnp.zeros((NA, AUXB - QS), jnp.int32)], axis=1)
    tail = jnp.concatenate([tail, jnp.zeros((8 - NA, AUXB), jnp.int32)], axis=0)
    out[PART : PART + 8, :] = tail.astype(F32).astype(BF16)


def pack(aux_list, aux_count, metric):
    return pl.pallas_call(
        pack_kernel,
        out_shape=jax.ShapeDtypeStruct((PART + 8, AUXB), BF16),
        in_specs=[VMEM] * 3,
        out_specs=VMEM,
        compiler_params=PARAMS,
        name="pack",
    )(aux_list, aux_count, metric)


def line_kernel(sc_ref, m0, m1, m2, m3, out):
    zh = sc_ref[1]
    parts = [m[...].astype(F32) for m in (m0, m1, m2, m3)]
    rows = lax.broadcasted_iota(jnp.int32, (8, AUXB), 0)
    tail = jnp.zeros((8, AUXB), F32)
    for src in range(4):
        k = back(zh, src)
        near = jnp.where(k == 0, parts[0], parts[1])
        far = jnp.where(k == 2, parts[2], parts[3])
        part = jnp.where(k < 2, near, far)
        for q in range(QB):
            at = (4 * q + src) * MROWS
            out[at : at + MROWS, :] = part[q * MROWS : (q + 1) * MROWS, :].astype(BF16)
        for a in range(NA):
            tail = jnp.where(rows == NA * src + a, part[PART + a : PART + a + 1, :], tail)
    both = jnp.concatenate([tail, parts[0][PART : PART + 8, :]], axis=0)
    out[LIST0:SMALL, :] = both.astype(BF16)


def line(sc, parts):
    return pl.pallas_call(
        line_kernel,
        out_shape=jax.ShapeDtypeStruct((SMALL, AUXB), BF16),
        in_specs=[SMEM] + [VMEM] * 4,
        out_specs=VMEM,
        compiler_params=PARAMS,
        name="line",
    )(sc, *parts)


def fill(tiles, start, met, lists, row, dense, base):
    for i in range(QS):
        q = lists[row, i]
        at = start + i * BS
        fitted = jnp.dot(tiles[at : at + BS, :], met[q], preferred_element_type=F32)
        cols = pl.ds(pl.multiple_of(q * AUXB, AUXB), AUXB)
        dense[pl.ds(pl.multiple_of(base, BS), BS), cols] = fitted.astype(BF16)


def fill_block(tiles, met, lists, row, dense, base):
    for a in range(NA):
        fill(tiles, a * HALF, met, lists, row + a, dense, base + a * BS)


def read_lists(small):
    return small[LIST0:SMALL, :].astype(F32).astype(jnp.int32)


def build_kernel(sc_ref, t0, t1, t2, t3, z1, z3, s0, s1, s2, s3, dy, dz, met, lv, ls, sem):
    y, zh = sc_ref[0], sc_ref[1]
    for k, s in enumerate((s0, s1, s2, s3)):
        lv[16 * k : 16 * k + 16, :] = read_lists(s)
    copy = pltpu.make_async_copy(lv, ls, sem)
    copy.start()
    for k, s in enumerate((s0, s1, s2, s3)):
        at = pl.multiple_of(back(y, k) * 4 * MROWS, 4 * MROWS)
        met[0:QB, pl.ds(at, 4 * MROWS), :] = s[0:LIST0, :].reshape(QB, 4 * MROWS, AUXB)
    dy[...] = jnp.zeros_like(dy)
    dz[...] = jnp.zeros_like(dz)
    copy.wait()
    fill_block(t0, met, ls, 8, dy, y * ROWS)
    mine = dy[pl.ds(pl.multiple_of(y * ROWS, ROWS), ROWS), :]
    dz[pl.ds(pl.multiple_of(zh * ROWS, ROWS), ROWS), :] = mine
    for k, t in ((1, t1), (2, t2), (3, t3)):
        fill_block(t, met, ls, 16 * k + 8, dy, back(y, k) * ROWS)
    for k, t in ((1, z1), (3, z3)):
        src = back(zh, k)
        fill_block(t, met, ls, NA * src, dz, src * ROWS)


def build(sc, tiles, zs, smalls):
    dense = jax.ShapeDtypeStruct((4 * ROWS, WIDE), BF16)
    return pl.pallas_call(
        build_kernel,
        out_shape=(dense, dense, jax.ShapeDtypeStruct((QB + 1, AUXB, AUXB), BF16)),
        in_specs=[SMEM] + [VMEM] * 10,
        out_specs=(VMEM,) * 3,
        scratch_shapes=[
            pltpu.VMEM((64, 128), jnp.int32),
            pltpu.SMEM((64, 128), jnp.int32),
            pltpu.SemaphoreType.DMA,
        ],
        compiler_params=PARAMS,
        name="build",
    )(sc, *tiles, *zs, *smalls)


def gram_kernel(flip, sc_ref, dy, dz, met, f1, f3, s0, out, far, lv, ls, sem):
    zh, co = sc_ref[1], sc_ref[2]
    parity = 1 - co if flip else co
    opposite = back(zh, 2)
    factor = 1.0 / (QS * 16 * AUXB) ** 0.5

    @pl.when(lax.rem(zh, 2) == parity)
    def _():
        lv[...] = read_lists(s0)
        copy = pltpu.make_async_copy(lv, ls, sem)
        copy.start()
        far[...] = jnp.zeros_like(far)
        copy.wait()
        fill(f1, 0, met, ls, NA * opposite, far, 0)
        fill(f3, 0, met, ls, NA * opposite + 1, far, BS)

    for h in range(2):
        p = 2 * h + parity

        def product(rhs):
            for q in range(4):
                lhs = dy[q * ROWS : (q + 1) * ROWS, 0:USED]
                prod = lax.dot_general(
                    lhs, rhs, (((1,), (1,)), ((), ())), preferred_element_type=F32
                )
                out[q, h] = prod * factor

        @pl.when(p == opposite)
        def _():
            product(far[:, 0:USED])

        @pl.when(p != opposite)
        def _():
            product(dz[pl.ds(pl.multiple_of(p * ROWS, ROWS), ROWS), 0:USED])


def gram(flip, sc, dy, dz, met, f1, f3, small):
    return pl.pallas_call(
        functools.partial(gram_kernel, flip),
        out_shape=jax.ShapeDtypeStruct((4, 2, ROWS, ROWS), F32),
        in_specs=[SMEM] + [VMEM] * 6,
        out_specs=VMEM,
        scratch_shapes=[
            pltpu.VMEM((ROWS, WIDE), BF16),
            pltpu.VMEM((16, 128), jnp.int32),
            pltpu.SMEM((16, 128), jnp.int32),
            pltpu.SemaphoreType.DMA,
        ],
        compiler_params=PARAMS,
        name="send" if flip else "keep",
    )(sc, dy, dz, met, f1, f3, small)


STEPS = tuple((k, w) for w in range(2) for k in range(4))


def share_kernel(sc_ref, keep, got, own, *outs):
    x, zl = sc_ref[3], sc_ref[4]
    for (k, w), out in zip(STEPS, (own,) + outs):
        q, h = lax.rem(x + k, 4), lax.rem(zl + w, 2)
        out[...] = (keep[q, h] + got[q, h]).astype(out.dtype)


def share(sc, keep, got):
    piece = (ROWS, ROWS)
    return pl.pallas_call(
        share_kernel,
        out_shape=(jax.ShapeDtypeStruct(piece, F32),) + (jax.ShapeDtypeStruct(piece, BF16),) * 7,
        in_specs=[SMEM, VMEM, VMEM],
        out_specs=(VMEM,) * 8,
        compiler_params=PARAMS,
        name="share",
    )(sc, keep, got)


def hop(k, w):
    return [(2 * a + b, 2 * ((a + k) % 4) + (b + w) % 2) for a in range(4) for b in range(2)]


def local(fit_tiles, aux_list, aux_count, metric):
    sc = jnp.stack([lax.axis_index(n) for n in ("y", "zh", "co", "x", "zl")]).astype(jnp.int32)
    part = pack(aux_list, aux_count, metric.reshape(PART, AUXB))
    parts = [part] + [lax.ppermute(part, "zh", ring(4, k)) for k in (1, 2, 3)]
    tiles = fit_tiles.reshape(2 * HALF, AUXB)
    z1 = lax.ppermute(tiles, "zh", ring(4, 1))
    z3 = lax.ppermute(tiles, "zh", ring(4, 3))
    ys = [tiles] + [lax.ppermute(tiles, "y", ring(4, k)) for k in (1, 2, 3)]
    small = line(sc, parts)
    smalls = [small] + [lax.ppermute(small, "y", ring(4, k)) for k in (1, 2, 3)]
    f1 = lax.ppermute(z1[:HALF], "zh", ring(4, 1))
    f3 = lax.ppermute(z3[HALF:], "zh", ring(4, 3))

    dy, dz, met = build(sc, ys, [z1, z3], smalls)
    send = gram(True, sc, dy, dz, met, f1, f3, small)
    got = lax.ppermute(send, "co", ring(2, 1))
    keep = gram(False, sc, dy, dz, met, f1, f3, small)
    total, *shares = share(sc, keep, got)
    for (k, w), piece in zip(STEPS[1:], shares):
        total = total + lax.ppermute(piece, ("x", "zl"), hop(k, w)).astype(F32)
    swap = [(a * 4 + b, b * 4 + a) for a in range(4) for b in range(4)]
    return lax.ppermute(total, ("zh", "zl", "co"), swap)


def solution(mesh):
    fine = Mesh(mesh.devices.reshape(4, 4, 4, 2, 2), ("y", "zh", "x", "zl", "co"))
    row, col = ("y", "zh"), ("x", "zl", "co")
    placed = (P(row, col, None, None), P(row, col), P(row, col), P(col, row, None))

    return jax.shard_map(local, mesh=fine, in_specs=placed, out_specs=P(col, row), check_vma=False)
```

time: 115 us -> 110 us (0.957)
  starting transfers between devices: 48.8 us -> 34.3 us
  waiting for transfers between devices: 49.1 us -> 60.9 us
  Pallas kernels: 13.1 us -> 10.8 us
    ppermute x23 -> x22, starting transfers between devices: 48.8 us -> 34.3 us  [the longest x7 8.11 us: local(): total = total + lax.ppermute(piece, ('x', 'zl'), hop(k, w)).astype(F32)]
    ppermute x23 -> x22, waiting for transfers between devices: 49.1 us -> 60.9 us  [the longest x3 18.4 us: local(): smalls = [small] + [lax.ppermute(small, 'y', ring(4, k)) for k in (1, 2, 3)]]
    pallas_call x7 -> x4, Pallas kernels: 9.24 us -> 7.04 us  [the longest x2 6.38 us: gram(): pl.pallas_call(functools.partial(gram_kernel, flip), out_shape=jax.ShapeD...]
  transfers between devices with their start and end apart: 23 -> 22, of which waited for: 9 -> 13; matrix products, arithmetic and copies ran while one was open for 0% -> 1% of each run, Pallas kernels for 9% -> 7%
where the time goes in v2:
time: 110 us
  waiting for transfers between devices  60.9 us (55%)
  starting transfers between devices  34.3 us (31%)
  Pallas kernels  10.8 us (10%)
  local copies, waits for them, and re-layouts  3.96 us (4%)
    ppermute x3, waiting for transfers between devices, local(): smalls = [small] + [lax.ppermute(small, 'y', ring(4, k)) for k in (1, 2, 3)]  18.4 us
    ppermute x3, waiting for transfers between devices, local(): parts = [part] + [lax.ppermute(part, 'zh', ring(4, k)) for k in (1, 2, 3)]  14.3 us
    ppermute x7, waiting for transfers between devices, local(): total = total + lax.ppermute(piece, ('x', 'zl'), hop(k, w)).astype(F32)  13.1 us
    ppermute x1, waiting for transfers between devices, local(): return lax.ppermute(total, ('zh', 'zl', 'co'), swap)  9.67 us
    ppermute x7, starting transfers between devices, local(): total = total + lax.ppermute(piece, ('x', 'zl'), hop(k, w)).astype(F32)  8.11 us
    ppermute x3, starting transfers between devices, local(): smalls = [small] + [lax.ppermute(small, 'y', ring(4, k)) for k in (1, 2, 3)]  7.2 us
    ppermute x3, starting transfers between devices, local(): parts = [part] + [lax.ppermute(part, 'zh', ring(4, k)) for k in (1, 2, 3)]  6.75 us
    pallas_call x2, Pallas kernels, gram(): pl.pallas_call(functools.partial(gram_kernel, flip), out_shape=jax.ShapeD...  6.38 us
  transfers between devices with their start and end apart: 22, of which 13 were waited for; matrix products, arithmetic and copies ran while one was open for 1% of the time, Pallas kernels for 7%

profile of v2, /device:TPU:32, one launch (start us, length us, event | category | flops | bytes accessed | tf_op | source)
XLA Modules:
  0.0 110.2 jit_solution(7386475951903007897)
XLA Ops:
  0.0 5.4 %collective-permute-start.4 = (bf16[1536,128]{1,0:T(8,128)(2,1)}, bf16[1536,128]{1,0:T(8,128)(2,1)S(1)}, u32[]{:S(2)}, u32[]{:S(2)}) collective-permute-start(bf16[1536,128]{1,0:T(8,128)(2,1)} %bitcast.7), channel_id=1, source_target_pairs={{0,48},{16,0},{32,16},{48,32},{1,49},{17,1},{33,17},{49,33},{2,50}... | collective-permute-start | bytes 1179656 | tf_op jit(solution)/shard_map/ppermute | solution.py:232
  5.4 0.7 copy.5.counts
  6.1 0.7 copy-done.1
  6.9 0.7 copy-done.2
  7.6 4.1 %collective-permute-start.7 = (bf16[104,128]{1,0:T(8,128)(2,1)S(1)}, bf16[104,128]{1,0:T(8,128)(2,1)S(1)}, u32[]{:S(2)}, u32[]{:S(2)}) collective-permute-start(bf16[104,128]{1,0:T(8,128)(2,1)S(1)} %pack.1.m0), channel_id=1, source_target_pairs={{0,48},{16,0},{32,16},{48,32},{1,49},{17,1},{33,17},{49,33},{2,50}... | collective-permute-start | bytes 79880 | tf_op jit(solution)/shard_map/ppermute | solution.py:229
  11.8 1.4 %collective-permute-start.6 = (bf16[104,128]{1,0:T(8,128)(2,1)S(1)}, bf16[104,128]{1,0:T(8,128)(2,1)S(1)}, u32[]{:S(2)}, u32[]{:S(2)}) collective-permute-start(bf16[104,128]{1,0:T(8,128)(2,1)S(1)} %pack.1.m0), channel_id=1, source_target_pairs={{0,32},{16,48},{32,0},{48,16},{1,33},{17,49},{33,1},{49,17},{2,34}... | collective-permute-start | bytes 79880 | tf_op jit(solution)/shard_map/ppermute | solution.py:229
  13.2 1.2 %collective-permute-start.5 = (bf16[104,128]{1,0:T(8,128)(2,1)S(1)}, bf16[104,128]{1,0:T(8,128)(2,1)S(1)}, u32[]{:S(2)}, u32[]{:S(2)}) collective-permute-start(bf16[104,128]{1,0:T(8,128)(2,1)S(1)} %pack.1.m0), channel_id=1, source_target_pairs={{0,16},{16,32},{32,48},{48,0},{1,17},{17,33},{33,49},{49,1},{2,18}... | collective-permute-start | bytes 79880 | tf_op jit(solution)/shard_map/ppermute | solution.py:229
  14.5 8.5 %collective-permute-done.7.m3 = bf16[104,128]{1,0:T(8,128)(2,1)S(1)} collective-permute-done((bf16[104,128]{1,0:T(8,128)(2,1)S(1)}, bf16[104,128]{1,0:T(8,128)(2,1)S(1)}, u32[]{:S(2)}, u32[]{:S(2)}) %collective-permute-start.7) | collective-permute-done | bytes 26656 | tf_op jit(solution)/shard_map/ppermute | solution.py:229
  23.3 5.5 %collective-permute-done.5.m1 = bf16[104,128]{1,0:T(8,128)(2,1)S(1)} collective-permute-done((bf16[104,128]{1,0:T(8,128)(2,1)S(1)}, bf16[104,128]{1,0:T(8,128)(2,1)S(1)}, u32[]{:S(2)}, u32[]{:S(2)}) %collective-permute-start.5) | collective-permute-done | bytes 26656 | tf_op jit(solution)/shard_map/ppermute | solution.py:229
  29.4 3.1 %collective-permute-start.10 = (bf16[400,128]{1,0:T(8,128)(2,1)S(1)}, bf16[400,128]{1,0:T(8,128)(2,1)S(1)}, u32[]{:S(2)}, u32[]{:S(2)}) collective-permute-start(bf16[400,128]{1,0:T(8,128)(2,1)S(1)} %line.1.s0), channel_id=1, source_target_pairs={{0,192},{64,0},{128,64},{192,128},{1,193},{65,1},{129,65},{193,129... | collective-permute-start | bytes 307208 | tf_op jit(solution)/shard_map/ppermute | solution.py:235
  32.5 0.7 collective-permute-start.2
  33.6 2.2 %collective-permute-done.10.s3 = bf16[400,128]{1,0:T(8,128)(2,1)S(1)} collective-permute-done((bf16[400,128]{1,0:T(8,128)(2,1)S(1)}, bf16[400,128]{1,0:T(8,128)(2,1)S(1)}, u32[]{:S(2)}, u32[]{:S(2)}) %collective-permute-start.10) | collective-permute-done | bytes 102432 | tf_op jit(solution)/shard_map/ppermute | solution.py:235
  35.8 1.0 collective-permute-start
  36.8 4.1 %collective-permute-start.9 = (bf16[400,128]{1,0:T(8,128)(2,1)S(1)}, bf16[400,128]{1,0:T(8,128)(2,1)S(1)}, u32[]{:S(2)}, u32[]{:S(2)}) collective-permute-start(bf16[400,128]{1,0:T(8,128)(2,1)S(1)} %line.1.s0), channel_id=1, source_target_pairs={{0,128},{64,192},{128,0},{192,64},{1,129},{65,193},{129,1},{193,65... | collective-permute-start | bytes 307208 | tf_op jit(solution)/shard_map/ppermute | solution.py:235
  41.0 15.8 %collective-permute-done.9.s2 = bf16[400,128]{1,0:T(8,128)(2,1)S(1)} collective-permute-done((bf16[400,128]{1,0:T(8,128)(2,1)S(1)}, bf16[400,128]{1,0:T(8,128)(2,1)S(1)}, u32[]{:S(2)}, u32[]{:S(2)}) %collective-permute-start.9) | collective-permute-done | bytes 102432 | tf_op jit(solution)/shard_map/ppermute | solution.py:235
  57.7 2.0 %collective-permute-start.11 = (bf16[768,128]{1,0:T(8,128)(2,1)S(1)}, bf16[768,128]{1,0:T(8,128)(2,1)S(1)}, u32[]{:S(2)}, u32[]{:S(2)}) collective-permute-start(bf16[768,128]{1,0:T(8,128)(2,1)S(1)} %slice.8), channel_id=1, source_target_pairs={{0,16},{16,32},{32,48},{48,0},{1,17},{17,33},{33,49},{49,1},{2,18}... | collective-permute-start | bytes 589832 | tf_op jit(solution)/shard_map/ppermute | solution.py:236
  59.7 1.0 copy-done
  60.7 3.0 %build.1 = (bf16[1024,1664]{1,0:T(8,128)(2,1)S(1)}, bf16[1024,1664]{1,0:T(8,128)(2,1)S(1)}, bf16[13,128,128]{2,1,0:T(8,128)(2,1)S(1)}) custom-call(s32[5]{0:T(128)S(1)} %stack.23.sc_ref, bf16[1536,128]{1,0:T(8,128)(2,1)S(1)} %bitcast.12, bf16[1536,128]{1,0:T(8,128)(2,1)S(1)} %collective-permute-done.t1, bf16[1536,128]{1,0:T(8,128)(2,1)S(1)} %collective-permute-done.1.t2, ...), custom_call_target="tpu_custom_call" | custom-call | tf_op jit(solution)/shard_map/build/pallas_call | solution.py:132
  64.2 4.6 %collective-permute-done.11.f1 = bf16[768,128]{1,0:T(8,128)(2,1)S(1)} collective-permute-done((bf16[768,128]{1,0:T(8,128)(2,1)S(1)}, bf16[768,128]{1,0:T(8,128)(2,1)S(1)}, u32[]{:S(2)}, u32[]{:S(2)}) %collective-permute-start.11) | collective-permute-done | bytes 196640 | tf_op jit(solution)/shard_map/ppermute | solution.py:236
  68.7 2.8 %send.1 = f32[4,2,256,256]{3,2,1,0:T(8,128)S(1)} custom-call(s32[5]{0:T(128)S(1)} %stack.23.sc_ref, bf16[1024,1664]{1,0:T(8,128)(2,1)S(1)} %get-tuple-element.16.dy, bf16[1024,1664]{1,0:T(8,128)(2,1)S(1)} %get-tuple-element.17.dz, bf16[13,128,128]{2,1,0:T(8,128)(2,1)S(1)} %get-tuple-element.18.met, bf16[768,128]{1,0:T(8,128)(2,1)S(1)} %collective-permute-done.11.f1, ...), custom_call_target="tpu_custom_call" | custom-call | tf_op jit(solution)/shard_map/send/pallas_call | solution.py:184
  71.8 3.6 %keep.1 = f32[4,2,256,256]{3,2,1,0:T(8,128)S(1)} custom-call(s32[5]{0:T(128)S(1)} %stack.23.sc_ref, bf16[1024,1664]{1,0:T(8,128)(2,1)S(1)} %get-tuple-element.16.dy, bf16[1024,1664]{1,0:T(8,128)(2,1)S(1)} %get-tuple-element.17.dz, bf16[13,128,128]{2,1,0:T(8,128)(2,1)S(1)} %get-tuple-element.18.met, bf16[768,128]{1,0:T(8,128)(2,1)S(1)} %collective-permute-done.11.f1, ...), custom_call_target="tpu_custom_call" | custom-call | tf_op jit(solution)/shard_map/keep/pallas_call | solution.py:184
  75.8 0.7 share.1
  76.5 1.6 %collective-permute-start.14 = (bf16[256,256]{1,0:T(8,128)(2,1)S(1)}, bf16[256,256]{1,0:T(8,128)(2,1)S(1)}, u32[]{:S(2)}, u32[]{:S(2)}) collective-permute-start(bf16[256,256]{1,0:T(8,128)(2,1)S(1)} %get-tuple-element.20), channel_id=1, source_target_pairs={{0,4},{2,6},{4,8},{6,10},{8,12},{10,14},{12,0},{14,2},{1,5},{3,7},... | collective-permute-start | bytes 393224 | tf_op jit(solution)/shard_map/ppermute | solution.py:245
  78.1 2.7 %collective-permute-start.15 = (bf16[256,256]{1,0:T(8,128)(2,1)S(1)}, bf16[256,256]{1,0:T(8,128)(2,1)S(1)}, u32[]{:S(2)}, u32[]{:S(2)}) collective-permute-start(bf16[256,256]{1,0:T(8,128)(2,1)S(1)} %get-tuple-element.21), channel_id=1, source_target_pairs={{0,8},{2,10},{4,12},{6,14},{8,0},{10,2},{12,4},{14,6},{1,9},{3,11}... | collective-permute-start | bytes 393224 | tf_op jit(solution)/shard_map/ppermute | solution.py:245
  80.8 1.4 %collective-permute-start.16 = (bf16[256,256]{1,0:T(8,128)(2,1)S(1)}, bf16[256,256]{1,0:T(8,128)(2,1)S(1)}, u32[]{:S(2)}, u32[]{:S(2)}) collective-permute-start(bf16[256,256]{1,0:T(8,128)(2,1)S(1)} %get-tuple-element.22), channel_id=1, source_target_pairs={{0,12},{2,14},{4,0},{6,2},{8,4},{10,6},{12,8},{14,10},{1,13},{3,15... | collective-permute-start | bytes 393224 | tf_op jit(solution)/shard_map/ppermute | solution.py:245
  82.3 2.0 %collective-permute-start.18 = (bf16[256,256]{1,0:T(8,128)(2,1)S(1)}, bf16[256,256]{1,0:T(8,128)(2,1)S(1)}, u32[]{:S(2)}, u32[]{:S(2)}) collective-permute-start(bf16[256,256]{1,0:T(8,128)(2,1)S(1)} %get-tuple-element.24), channel_id=1, source_target_pairs={{0,6},{2,4},{4,10},{6,8},{8,14},{10,12},{12,2},{14,0},{1,7},{3,5},... | collective-permute-start | bytes 393224 | tf_op jit(solution)/shard_map/ppermute | solution.py:245
  84.6 7.3 %collective-permute-done.15 = bf16[256,256]{1,0:T(8,128)(2,1)S(1)} collective-permute-done((bf16[256,256]{1,0:T(8,128)(2,1)S(1)}, bf16[256,256]{1,0:T(8,128)(2,1)S(1)}, u32[]{:S(2)}, u32[]{:S(2)}) %collective-permute-start.15) | collective-permute-done | bytes 131104 | tf_op jit(solution)/shard_map/ppermute | solution.py:245
  91.9 2.0 %collective-permute-done.19 = bf16[256,256]{1,0:T(8,128)(2,1)S(1)} collective-permute-done((bf16[256,256]{1,0:T(8,128)(2,1)S(1)}, bf16[256,256]{1,0:T(8,128)(2,1)S(1)}, u32[]{:S(2)}, u32[]{:S(2)}) %collective-permute-start.19) | collective-permute-done | bytes 131104 | tf_op jit(solution)/shard_map/ppermute | solution.py:245
  94.0 3.8 %collective-permute-done.20 = bf16[256,256]{1,0:T(8,128)(2,1)S(1)} collective-permute-done((bf16[256,256]{1,0:T(8,128)(2,1)S(1)}, bf16[256,256]{1,0:T(8,128)(2,1)S(1)}, u32[]{:S(2)}, u32[]{:S(2)}) %collective-permute-start.20) | collective-permute-done | bytes 131104 | tf_op jit(solution)/shard_map/ppermute | solution.py:245
  97.9 1.9 %collective-permute-start.21 = (f32[256,256]{1,0:T(8,128)S(1)}, f32[256,256]{1,0:T(8,128)S(1)}, u32[]{:S(2)}, u32[]{:S(2)}) collective-permute-start(f32[256,256]{1,0:T(8,128)S(1)} %convert_add_fusion), channel_id=1, source_target_pairs={{0,0},{1,16},{2,32},{3,48},{16,1},{17,17},{18,33},{19,49},{32,2},{... | collective-permute-start | bytes 786440 | tf_op jit(solution)/shard_map/ppermute | solution.py:247
  99.8 9.7 %collective-permute-done.21 = f32[256,256]{1,0:T(8,128)S(1)} collective-permute-done((f32[256,256]{1,0:T(8,128)S(1)}, f32[256,256]{1,0:T(8,128)S(1)}, u32[]{:S(2)}, u32[]{:S(2)}) %collective-permute-start.21) | collective-permute-done | bytes 262176 | tf_op jit(solution)/shard_map/ppermute | solution.py:247
  109.5 0.7 copy.7
  (30 shorter events, 3.9 us)
Async XLA Ops:
  0.0 36.8 %collective-permute-start.4 = (bf16[1536,128]{1,0:T(8,128)(2,1)}, bf16[1536,128]{1,0:T(8,128)(2,1)S(1)}, u32[]{:S(2)}, u32[]{:S(2)}) collective-permute-start(bf16[1536,128]{1,0:T(8,128)(2,1)} %bitcast.7), channel_id=1, source_target_pairs={{0,48},{16,0},{32,16},{48,32},{1,49},{17,1},{33,17},{49,33},{2,50}... | collective-permute-start | bytes 1179656 | tf_op jit(solution)/shard_map/ppermute | solution.py:232
  5.4 35.5 %collective-permute-start.3 = (bf16[1536,128]{1,0:T(8,128)(2,1)}, bf16[1536,128]{1,0:T(8,128)(2,1)S(1)}, u32[]{:S(2)}, u32[]{:S(2)}) collective-permute-start(bf16[1536,128]{1,0:T(8,128)(2,1)} %bitcast.8), channel_id=1, source_target_pairs={{0,16},{16,32},{32,48},{48,0},{1,17},{17,33},{33,49},{49,1},{2,18}... | collective-permute-start | bytes 1179656 | tf_op jit(solution)/shard_map/ppermute | solution.py:231
  6.1 0.7 copy-start.1
  6.9 0.7 copy-start.2
  7.6 15.4 %collective-permute-start.7 = (bf16[104,128]{1,0:T(8,128)(2,1)S(1)}, bf16[104,128]{1,0:T(8,128)(2,1)S(1)}, u32[]{:S(2)}, u32[]{:S(2)}) collective-permute-start(bf16[104,128]{1,0:T(8,128)(2,1)S(1)} %pack.1.m0), channel_id=1, source_target_pairs={{0,48},{16,0},{32,16},{48,32},{1,49},{17,1},{33,17},{49,33},{2,50}... | collective-permute-start | bytes 79880 | tf_op jit(solution)/shard_map/ppermute | solution.py:229
  11.8 11.5 %collective-permute-start.6 = (bf16[104,128]{1,0:T(8,128)(2,1)S(1)}, bf16[104,128]{1,0:T(8,128)(2,1)S(1)}, u32[]{:S(2)}, u32[]{:S(2)}) collective-permute-start(bf16[104,128]{1,0:T(8,128)(2,1)S(1)} %pack.1.m0), channel_id=1, source_target_pairs={{0,32},{16,48},{32,0},{48,16},{1,33},{17,49},{33,1},{49,17},{2,34}... | collective-permute-start | bytes 79880 | tf_op jit(solution)/shard_map/ppermute | solution.py:229
  13.2 15.6 %collective-permute-start.5 = (bf16[104,128]{1,0:T(8,128)(2,1)S(1)}, bf16[104,128]{1,0:T(8,128)(2,1)S(1)}, u32[]{:S(2)}, u32[]{:S(2)}) collective-permute-start(bf16[104,128]{1,0:T(8,128)(2,1)S(1)} %pack.1.m0), channel_id=1, source_target_pairs={{0,16},{16,32},{32,48},{48,0},{1,17},{17,33},{33,49},{49,1},{2,18}... | collective-permute-start | bytes 79880 | tf_op jit(solution)/shard_map/ppermute | solution.py:229
  29.4 6.4 %collective-permute-start.10 = (bf16[400,128]{1,0:T(8,128)(2,1)S(1)}, bf16[400,128]{1,0:T(8,128)(2,1)S(1)}, u32[]{:S(2)}, u32[]{:S(2)}) collective-permute-start(bf16[400,128]{1,0:T(8,128)(2,1)S(1)} %line.1.s0), channel_id=1, source_target_pairs={{0,192},{64,0},{128,64},{192,128},{1,193},{65,1},{129,65},{193,129... | collective-permute-start | bytes 307208 | tf_op jit(solution)/shard_map/ppermute | solution.py:235
  32.5 27.2 %collective-permute-start.2 = (bf16[1536,128]{1,0:T(8,128)(2,1)}, bf16[1536,128]{1,0:T(8,128)(2,1)S(1)}, u32[]{:S(2)}, u32[]{:S(2)}) collective-permute-start(bf16[1536,128]{1,0:T(8,128)(2,1)} %bitcast.9), channel_id=1, source_target_pairs={{0,192},{64,0},{128,64},{192,128},{1,193},{65,1},{129,65},{193,129... | collective-permute-start | bytes 1179656 | tf_op jit(solution)/shard_map/ppermute | solution.py:233
  33.2 26.5 %collective-permute-start.1 = (bf16[1536,128]{1,0:T(8,128)(2,1)}, bf16[1536,128]{1,0:T(8,128)(2,1)S(1)}, u32[]{:S(2)}, u32[]{:S(2)}) collective-permute-start(bf16[1536,128]{1,0:T(8,128)(2,1)} %bitcast.10), channel_id=1, source_target_pairs={{0,128},{64,192},{128,0},{192,64},{1,129},{65,193},{129,1},{193,65... | collective-permute-start | bytes 1179656 | tf_op jit(solution)/shard_map/ppermute | solution.py:233
  35.8 23.9 %collective-permute-start = (bf16[1536,128]{1,0:T(8,128)(2,1)}, bf16[1536,128]{1,0:T(8,128)(2,1)S(1)}, u32[]{:S(2)}, u32[]{:S(2)}) collective-permute-start(bf16[1536,128]{1,0:T(8,128)(2,1)} %bitcast.11), channel_id=1, source_target_pairs={{0,64},{64,128},{128,192},{192,0},{1,65},{65,129},{129,193},{193,1... | collective-permute-start | bytes 1179656 | tf_op jit(solution)/shard_map/ppermute | solution.py:233
  36.8 19.9 %collective-permute-start.9 = (bf16[400,128]{1,0:T(8,128)(2,1)S(1)}, bf16[400,128]{1,0:T(8,128)(2,1)S(1)}, u32[]{:S(2)}, u32[]{:S(2)}) collective-permute-start(bf16[400,128]{1,0:T(8,128)(2,1)S(1)} %line.1.s0), channel_id=1, source_target_pairs={{0,128},{64,192},{128,0},{192,64},{1,129},{65,193},{129,1},{193,65... | collective-permute-start | bytes 307208 | tf_op jit(solution)/shard_map/ppermute | solution.py:235
  40.9 16.8 %collective-permute-start.8 = (bf16[400,128]{1,0:T(8,128)(2,1)S(1)}, bf16[400,128]{1,0:T(8,128)(2,1)S(1)}, u32[]{:S(2)}, u32[]{:S(2)}) collective-permute-start(bf16[400,128]{1,0:T(8,128)(2,1)S(1)} %line.1.s0), channel_id=1, source_target_pairs={{0,64},{64,128},{128,192},{192,0},{1,65},{65,129},{129,193},{193,1... | collective-permute-start | bytes 307208 | tf_op jit(solution)/shard_map/ppermute | solution.py:235
  56.7 7.4 %collective-permute-start.12 = (bf16[768,128]{1,0:T(8,128)(2,1)S(1)}, bf16[768,128]{1,0:T(8,128)(2,1)S(1)}, u32[]{:S(2)}, u32[]{:S(2)}) collective-permute-start(bf16[768,128]{1,0:T(8,128)(2,1)S(1)} %slice.9), channel_id=1, source_target_pairs={{0,48},{16,0},{32,16},{48,32},{1,49},{17,1},{33,17},{49,33},{2,50}... | collective-permute-start | bytes 589832 | tf_op jit(solution)/shard_map/ppermute | solution.py:237
  57.7 11.0 %collective-permute-start.11 = (bf16[768,128]{1,0:T(8,128)(2,1)S(1)}, bf16[768,128]{1,0:T(8,128)(2,1)S(1)}, u32[]{:S(2)}, u32[]{:S(2)}) collective-permute-start(bf16[768,128]{1,0:T(8,128)(2,1)S(1)} %slice.8), channel_id=1, source_target_pairs={{0,16},{16,32},{32,48},{48,0},{1,17},{17,33},{33,49},{49,1},{2,18}... | collective-permute-start | bytes 589832 | tf_op jit(solution)/shard_map/ppermute | solution.py:236
  59.7 1.0 copy-start
  71.5 4.2 %collective-permute-start.13 = (f32[4,2,256,256]{3,2,1,0:T(8,128)S(1)}, f32[4,2,256,256]{3,2,1,0:T(8,128)S(1)}, u32[]{:S(2)}, u32[]{:S(2)}) collective-permute-start(f32[4,2,256,256]{3,2,1,0:T(8,128)S(1)} %send.1), channel_id=1, source_target_pairs={{0,1},{1,0},{2,3},{3,2},{4,5},{5,4},{6,7},{7,6},{8,9},{9,8},{10,11... | collective-permute-start | bytes 6291464 | tf_op jit(solution)/shard_map/ppermute | solution.py:241
  76.5 7.8 %collective-permute-start.14 = (bf16[256,256]{1,0:T(8,128)(2,1)S(1)}, bf16[256,256]{1,0:T(8,128)(2,1)S(1)}, u32[]{:S(2)}, u32[]{:S(2)}) collective-permute-start(bf16[256,256]{1,0:T(8,128)(2,1)S(1)} %get-tuple-element.20), channel_id=1, source_target_pairs={{0,4},{2,6},{4,8},{6,10},{8,12},{10,14},{12,0},{14,2},{1,5},{3,7},... | collective-permute-start | bytes 393224 | tf_op jit(solution)/shard_map/ppermute | solution.py:245
  78.1 13.8 %collective-permute-start.15 = (bf16[256,256]{1,0:T(8,128)(2,1)S(1)}, bf16[256,256]{1,0:T(8,128)(2,1)S(1)}, u32[]{:S(2)}, u32[]{:S(2)}) collective-permute-start(bf16[256,256]{1,0:T(8,128)(2,1)S(1)} %get-tuple-element.21), channel_id=1, source_target_pairs={{0,8},{2,10},{4,12},{6,14},{8,0},{10,2},{12,4},{14,6},{1,9},{3,11}... | collective-permute-start | bytes 393224 | tf_op jit(solution)/shard_map/ppermute | solution.py:245
  80.8 11.1 %collective-permute-start.16 = (bf16[256,256]{1,0:T(8,128)(2,1)S(1)}, bf16[256,256]{1,0:T(8,128)(2,1)S(1)}, u32[]{:S(2)}, u32[]{:S(2)}) collective-permute-start(bf16[256,256]{1,0:T(8,128)(2,1)S(1)} %get-tuple-element.22), channel_id=1, source_target_pairs={{0,12},{2,14},{4,0},{6,2},{8,4},{10,6},{12,8},{14,10},{1,13},{3,15... | collective-permute-start | bytes 393224 | tf_op jit(solution)/shard_map/ppermute | solution.py:245
  82.3 9.6 %collective-permute-start.17 = (bf16[256,256]{1,0:T(8,128)(2,1)S(1)}, bf16[256,256]{1,0:T(8,128)(2,1)S(1)}, u32[]{:S(2)}, u32[]{:S(2)}) collective-permute-start(bf16[256,256]{1,0:T(8,128)(2,1)S(1)} %get-tuple-element.23), channel_id=1, source_target_pairs={{0,2},{2,0},{4,6},{6,4},{8,10},{10,8},{12,14},{14,12},{1,3},{3,1},... | collective-permute-start | bytes 393224 | tf_op jit(solution)/shard_map/ppermute | solution.py:245
  82.3 9.6 %collective-permute-start.18 = (bf16[256,256]{1,0:T(8,128)(2,1)S(1)}, bf16[256,256]{1,0:T(8,128)(2,1)S(1)}, u32[]{:S(2)}, u32[]{:S(2)}) collective-permute-start(bf16[256,256]{1,0:T(8,128)(2,1)S(1)} %get-tuple-element.24), channel_id=1, source_target_pairs={{0,6},{2,4},{4,10},{6,8},{8,14},{10,12},{12,2},{14,0},{1,7},{3,5},... | collective-permute-start | bytes 393224 | tf_op jit(solution)/shard_map/ppermute | solution.py:245
  84.3 9.6 %collective-permute-start.19 = (bf16[256,256]{1,0:T(8,128)(2,1)S(1)}, bf16[256,256]{1,0:T(8,128)(2,1)S(1)}, u32[]{:S(2)}, u32[]{:S(2)}) collective-permute-start(bf16[256,256]{1,0:T(8,128)(2,1)S(1)} %get-tuple-element.25), channel_id=1, source_target_pairs={{0,10},{2,8},{4,14},{6,12},{8,2},{10,0},{12,6},{14,4},{1,11},{3,9}... | collective-permute-start | bytes 393224 | tf_op jit(solution)/shard_map/ppermute | solution.py:245
  91.9 5.9 %collective-permute-start.20 = (bf16[256,256]{1,0:T(8,128)(2,1)S(1)}, bf16[256,256]{1,0:T(8,128)(2,1)S(1)}, u32[]{:S(2)}, u32[]{:S(2)}) collective-permute-start(bf16[256,256]{1,0:T(8,128)(2,1)S(1)} %get-tuple-element.26), channel_id=1, source_target_pairs={{0,14},{2,12},{4,2},{6,0},{8,6},{10,4},{12,10},{14,8},{1,15},{3,13... | collective-permute-start | bytes 393224 | tf_op jit(solution)/shard_map/ppermute | solution.py:245
  97.9 11.6 %collective-permute-start.21 = (f32[256,256]{1,0:T(8,128)S(1)}, f32[256,256]{1,0:T(8,128)S(1)}, u32[]{:S(2)}, u32[]{:S(2)}) collective-permute-start(f32[256,256]{1,0:T(8,128)S(1)} %convert_add_fusion), channel_id=1, source_target_pairs={{0,0},{1,16},{2,32},{3,48},{16,1},{17,17},{18,33},{19,49},{32,2},{... | collective-permute-start | bytes 786440 | tf_op jit(solution)/shard_map/ppermute | solution.py:247

commit v3 on v2

--- a/solution.py
+++ b/solution.py
@@ -58,22 +58,12 @@
 
 
 def line_kernel(sc_ref, m0, m1, m2, m3, out):
-    zh = sc_ref[1]
-    parts = [m[...].astype(F32) for m in (m0, m1, m2, m3)]
-    rows = lax.broadcasted_iota(jnp.int32, (8, AUXB), 0)
-    tail = jnp.zeros((8, AUXB), F32)
-    for src in range(4):
-        k = back(zh, src)
-        near = jnp.where(k == 0, parts[0], parts[1])
-        far = jnp.where(k == 2, parts[2], parts[3])
-        part = jnp.where(k < 2, near, far)
-        for q in range(QB):
-            at = (4 * q + src) * MROWS
-            out[at : at + MROWS, :] = part[q * MROWS : (q + 1) * MROWS, :].astype(BF16)
-        for a in range(NA):
-            tail = jnp.where(rows == NA * src + a, part[PART + a : PART + a + 1, :], tail)
-    both = jnp.concatenate([tail, parts[0][PART : PART + 8, :]], axis=0)
-    out[LIST0:SMALL, :] = both.astype(BF16)
+    y = sc_ref[0]
+    for k, m in enumerate((m0, m1, m2, m3)):
+        at = pl.multiple_of(back(y, k) * PART, 32)
+        out[pl.ds(at, PART), :] = m[0:PART, :]
+    tail = jnp.concatenate([m0[PART : PART + 8, :].astype(F32), jnp.zeros((8, AUXB), F32)], axis=0)
+    out[LIST0:SMALL, :] = tail.astype(BF16)
 
 
 def line(sc, parts):
@@ -101,50 +91,61 @@
         fill(tiles, a * HALF, met, lists, row + a, dense, base + a * BS)
 
 
-def read_lists(small):
-    return small[LIST0:SMALL, :].astype(F32).astype(jnp.int32)
-
-
-def build_kernel(sc_ref, t0, t1, t2, t3, z1, z3, s0, s1, s2, s3, dy, dz, met, lv, ls, sem):
+def read_lists(ref, at):
+    return ref[at : at + 8, :].astype(F32).astype(jnp.int32)
+
+
+def build_kernel(
+    sc_ref, t0, t1, t2, t3, z1, z3, p0, p1, p2, p3, s0, s1, s2, s3, dy, dz, met, lv, ls, sem
+):
     y, zh = sc_ref[0], sc_ref[1]
-    for k, s in enumerate((s0, s1, s2, s3)):
-        lv[16 * k : 16 * k + 16, :] = read_lists(s)
+    for k, p in enumerate((p0, p1, p2, p3)):
+        lv[8 * k : 8 * k + 8, :] = read_lists(p, PART)
+    for n, s in ((4, s1), (5, s3)):
+        lv[8 * n : 8 * n + 8, :] = read_lists(s, LIST0)
     copy = pltpu.make_async_copy(lv, ls, sem)
     copy.start()
-    for k, s in enumerate((s0, s1, s2, s3)):
-        at = pl.multiple_of(back(y, k) * 4 * MROWS, 4 * MROWS)
-        met[0:QB, pl.ds(at, 4 * MROWS), :] = s[0:LIST0, :].reshape(QB, 4 * MROWS, AUXB)
+    lines = [s[0:LIST0, :].astype(F32) for s in (s0, s1, s2, s3)]
+    for src in range(4):
+        k = back(zh, src)
+        near = jnp.where(k == 0, lines[0], lines[1])
+        far = jnp.where(k == 2, lines[2], lines[3])
+        rows = jnp.where(k < 2, near, far)
+        for ysrc in range(4):
+            for q in range(QB):
+                at = ysrc * PART + q * MROWS
+                to = (4 * ysrc + src) * MROWS
+                met[q, to : to + MROWS, :] = rows[at : at + MROWS, :].astype(BF16)
     dy[...] = jnp.zeros_like(dy)
     dz[...] = jnp.zeros_like(dz)
     copy.wait()
-    fill_block(t0, met, ls, 8, dy, y * ROWS)
+    fill_block(t0, met, ls, 0, dy, y * ROWS)
     mine = dy[pl.ds(pl.multiple_of(y * ROWS, ROWS), ROWS), :]
     dz[pl.ds(pl.multiple_of(zh * ROWS, ROWS), ROWS), :] = mine
     for k, t in ((1, t1), (2, t2), (3, t3)):
-        fill_block(t, met, ls, 16 * k + 8, dy, back(y, k) * ROWS)
-    for k, t in ((1, z1), (3, z3)):
-        src = back(zh, k)
-        fill_block(t, met, ls, NA * src, dz, src * ROWS)
-
-
-def build(sc, tiles, zs, smalls):
+        fill_block(t, met, ls, 8 * k, dy, back(y, k) * ROWS)
+    for n, k, t in ((4, 1, z1), (5, 3, z3)):
+        fill_block(t, met, ls, 8 * n, dz, back(zh, k) * ROWS)
+
+
+def build(sc, tiles, zs, parts, smalls):
     dense = jax.ShapeDtypeStruct((4 * ROWS, WIDE), BF16)
     return pl.pallas_call(
         build_kernel,
         out_shape=(dense, dense, jax.ShapeDtypeStruct((QB + 1, AUXB, AUXB), BF16)),
-        in_specs=[SMEM] + [VMEM] * 10,
+        in_specs=[SMEM] + [VMEM] * 14,
         out_specs=(VMEM,) * 3,
         scratch_shapes=[
-            pltpu.VMEM((64, 128), jnp.int32),
-            pltpu.SMEM((64, 128), jnp.int32),
+            pltpu.VMEM((48, 128), jnp.int32),
+            pltpu.SMEM((48, 128), jnp.int32),
             pltpu.SemaphoreType.DMA,
         ],
         compiler_params=PARAMS,
         name="build",
-    )(sc, *tiles, *zs, *smalls)
-
-
-def gram_kernel(flip, sc_ref, dy, dz, met, f1, f3, s0, out, far, lv, ls, sem):
+    )(sc, *tiles, *zs, *parts, *smalls)
+
+
+def gram_kernel(flip, sc_ref, dy, dz, met, f1, f3, s2, out, far, lv, ls, sem):
     zh, co = sc_ref[1], sc_ref[2]
     parity = 1 - co if flip else co
     opposite = back(zh, 2)
@@ -152,13 +153,13 @@
 
     @pl.when(lax.rem(zh, 2) == parity)
     def _():
-        lv[...] = read_lists(s0)
+        lv[...] = read_lists(s2, LIST0)
         copy = pltpu.make_async_copy(lv, ls, sem)
         copy.start()
         far[...] = jnp.zeros_like(far)
         copy.wait()
-        fill(f1, 0, met, ls, NA * opposite, far, 0)
-        fill(f3, 0, met, ls, NA * opposite + 1, far, BS)
+        fill(f1, 0, met, ls, 0, far, 0)
+        fill(f3, 0, met, ls, 1, far, BS)
 
     for h in range(2):
         p = 2 * h + parity
@@ -188,8 +189,8 @@
         out_specs=VMEM,
         scratch_shapes=[
             pltpu.VMEM((ROWS, WIDE), BF16),
-            pltpu.VMEM((16, 128), jnp.int32),
-            pltpu.SMEM((16, 128), jnp.int32),
+            pltpu.VMEM((8, 128), jnp.int32),
+            pltpu.SMEM((8, 128), jnp.int32),
             pltpu.SemaphoreType.DMA,
         ],
         compiler_params=PARAMS,
@@ -226,20 +227,20 @@
 def local(fit_tiles, aux_list, aux_count, metric):
     sc = jnp.stack([lax.axis_index(n) for n in ("y", "zh", "co", "x", "zl")]).astype(jnp.int32)
     part = pack(aux_list, aux_count, metric.reshape(PART, AUXB))
-    parts = [part] + [lax.ppermute(part, "zh", ring(4, k)) for k in (1, 2, 3)]
+    parts = [part] + [lax.ppermute(part, "y", ring(4, k)) for k in (1, 2, 3)]
     tiles = fit_tiles.reshape(2 * HALF, AUXB)
     z1 = lax.ppermute(tiles, "zh", ring(4, 1))
     z3 = lax.ppermute(tiles, "zh", ring(4, 3))
     ys = [tiles] + [lax.ppermute(tiles, "y", ring(4, k)) for k in (1, 2, 3)]
     small = line(sc, parts)
-    smalls = [small] + [lax.ppermute(small, "y", ring(4, k)) for k in (1, 2, 3)]
+    smalls = [small] + [lax.ppermute(small, "zh", ring(4, k)) for k in (1, 2, 3)]
     f1 = lax.ppermute(z1[:HALF], "zh", ring(4, 1))
     f3 = lax.ppermute(z3[HALF:], "zh", ring(4, 3))
 
-    dy, dz, met = build(sc, ys, [z1, z3], smalls)
-    send = gram(True, sc, dy, dz, met, f1, f3, small)
+    dy, dz, met = build(sc, ys, [z1, z3], parts, smalls)
+    send = gram(True, sc, dy, dz, met, f1, f3, smalls[2])
     got = lax.ppermute(send, "co", ring(2, 1))
-    keep = gram(False, sc, dy, dz, met, f1, f3, small)
+    keep = gram(False, sc, dy, dz, met, f1, f3, smalls[2])
     total, *shares = share(sc, keep, got)
     for (k, w), piece in zip(STEPS[1:], shares):
         total = total + lax.ppermute(piece, ("x", "zl"), hop(k, w)).astype(F32)

time: 110 us -> 98.3 us (0.89)
  the two profiles are of different devices: /device:TPU:32 before, /device:TPU:40 now
where the time goes in v3:
time: 98.3 us; the launch traced here: 98.1 us
  starting transfers between devices  45.5 us (46%)
  waiting for transfers between devices  38.3 us (39%)
  Pallas kernels  10.1 us (10%)
  local copies, waits for them, and re-layouts  3.96 us (4%)
    ppermute x7, waiting for transfers between devices, local(): total = total + lax.ppermute(piece, ('x', 'zl'), hop(k, w)).astype(F32)  12.7 us
    ppermute x3, starting transfers between devices, local(): lax.ppermute(small, 'zh', ring(4, k))  11.2 us
    ppermute x3, waiting for transfers between devices, local(): lax.ppermute(small, 'zh', ring(4, k))  8.93 us
    ppermute x7, starting transfers between devices, local(): total = total + lax.ppermute(piece, ('x', 'zl'), hop(k, w)).astype(F32)  8.48 us
    ppermute x1, waiting for transfers between devices, local(): return lax.ppermute(total, ('zh', 'zl', 'co'), swap)  8.29 us
    ppermute x1, starting transfers between devices, local(): return lax.ppermute(total, ('zh', 'zl', 'co'), swap)  6.34 us
    pallas_call x2, Pallas kernels, gram(): pl.pallas_call(functools.partial(gram_kernel, flip), out_shape=jax.ShapeD...  6.3 us
    ppermute x1, waiting for transfers between devices, local(): f1 = lax.ppermute(z1[:HALF], 'zh', ring(4, 1))  5.85 us
  transfers between devices with their start and end apart: 22, of which 11 were waited for; matrix products, arithmetic and copies ran while one was open for 1% of the time, Pallas kernels for 7%

profile of v3, /device:TPU:40, one launch (start us, length us, event | category | flops | bytes accessed | tf_op | source)
XLA Modules:
  0.0 98.1 jit_solution(12940347732439677515)
XLA Ops:
  0.0 5.4 %collective-permute-start.4 = (bf16[1536,128]{1,0:T(8,128)(2,1)}, bf16[1536,128]{1,0:T(8,128)(2,1)S(1)}, u32[]{:S(2)}, u32[]{:S(2)}) collective-permute-start(bf16[1536,128]{1,0:T(8,128)(2,1)} %bitcast.7), channel_id=1, source_target_pairs={{0,48},{16,0},{32,16},{48,32},{1,49},{17,1},{33,17},{49,33},{2,50}... | collective-permute-start | bytes 1179656 | tf_op jit(solution)/shard_map/ppermute | solution.py:233
  5.4 0.7 copy.5.counts
  8.1 2.6 %collective-permute-start.6 = (bf16[104,128]{1,0:T(8,128)(2,1)S(1)}, bf16[104,128]{1,0:T(8,128)(2,1)S(1)}, u32[]{:S(2)}, u32[]{:S(2)}) collective-permute-start(bf16[104,128]{1,0:T(8,128)(2,1)S(1)} %pack.1.m0.p0), channel_id=1, source_target_pairs={{0,128},{64,192},{128,0},{192,64},{1,129},{65,193},{129,1},{193,65... | collective-permute-start | bytes 79880 | tf_op jit(solution)/shard_map/ppermute | solution.py:230
  10.7 1.9 %collective-permute-start.5 = (bf16[104,128]{1,0:T(8,128)(2,1)S(1)}, bf16[104,128]{1,0:T(8,128)(2,1)S(1)}, u32[]{:S(2)}, u32[]{:S(2)}) collective-permute-start(bf16[104,128]{1,0:T(8,128)(2,1)S(1)} %pack.1.m0.p0), channel_id=1, source_target_pairs={{0,64},{64,128},{128,192},{192,0},{1,65},{65,129},{129,193},{193,1... | collective-permute-start | bytes 79880 | tf_op jit(solution)/shard_map/ppermute | solution.py:230
  12.7 0.8 collective-permute-done.6.m2.p2
  13.5 1.1 %collective-permute-done.5.m1.p1 = bf16[104,128]{1,0:T(8,128)(2,1)S(1)} collective-permute-done((bf16[104,128]{1,0:T(8,128)(2,1)S(1)}, bf16[104,128]{1,0:T(8,128)(2,1)S(1)}, u32[]{:S(2)}, u32[]{:S(2)}) %collective-permute-start.5) | collective-permute-done | bytes 26656 | tf_op jit(solution)/shard_map/ppermute | solution.py:230
  15.1 4.2 %collective-permute-start.10 = (bf16[400,128]{1,0:T(8,128)(2,1)S(1)}, bf16[400,128]{1,0:T(8,128)(2,1)S(1)}, u32[]{:S(2)}, u32[]{:S(2)}) collective-permute-start(bf16[400,128]{1,0:T(8,128)(2,1)S(1)} %line.1.s0), channel_id=1, source_target_pairs={{0,48},{16,0},{32,16},{48,32},{1,49},{17,1},{33,17},{49,33},{2,50}... | collective-permute-start | bytes 307208 | tf_op jit(solution)/shard_map/ppermute | solution.py:236
  19.3 2.3 %collective-permute-start.2 = (bf16[1536,128]{1,0:T(8,128)(2,1)}, bf16[1536,128]{1,0:T(8,128)(2,1)S(1)}, u32[]{:S(2)}, u32[]{:S(2)}) collective-permute-start(bf16[1536,128]{1,0:T(8,128)(2,1)} %bitcast.9), channel_id=1, source_target_pairs={{0,192},{64,0},{128,64},{192,128},{1,193},{65,1},{129,65},{193,129... | collective-permute-start | bytes 1179656 | tf_op jit(solution)/shard_map/ppermute | solution.py:234
  21.6 1.1 %collective-permute-start.1 = (bf16[1536,128]{1,0:T(8,128)(2,1)}, bf16[1536,128]{1,0:T(8,128)(2,1)S(1)}, u32[]{:S(2)}, u32[]{:S(2)}) collective-permute-start(bf16[1536,128]{1,0:T(8,128)(2,1)} %bitcast.10), channel_id=1, source_target_pairs={{0,128},{64,192},{128,0},{192,64},{1,129},{65,193},{129,1},{193,65... | collective-permute-start | bytes 1179656 | tf_op jit(solution)/shard_map/ppermute | solution.py:234
  22.7 2.7 %collective-permute-done.10.s3 = bf16[400,128]{1,0:T(8,128)(2,1)S(1)} collective-permute-done((bf16[400,128]{1,0:T(8,128)(2,1)S(1)}, bf16[400,128]{1,0:T(8,128)(2,1)S(1)}, u32[]{:S(2)}, u32[]{:S(2)}) %collective-permute-start.10) | collective-permute-done | bytes 102432 | tf_op jit(solution)/shard_map/ppermute | solution.py:236
  25.4 1.6 %collective-permute-start = (bf16[1536,128]{1,0:T(8,128)(2,1)}, bf16[1536,128]{1,0:T(8,128)(2,1)S(1)}, u32[]{:S(2)}, u32[]{:S(2)}) collective-permute-start(bf16[1536,128]{1,0:T(8,128)(2,1)} %bitcast.11), channel_id=1, source_target_pairs={{0,64},{64,128},{128,192},{192,0},{1,65},{65,129},{129,193},{193,1... | collective-permute-start | bytes 1179656 | tf_op jit(solution)/shard_map/ppermute | solution.py:234
  27.0 4.9 %collective-permute-start.9 = (bf16[400,128]{1,0:T(8,128)(2,1)S(1)}, bf16[400,128]{1,0:T(8,128)(2,1)S(1)}, u32[]{:S(2)}, u32[]{:S(2)}) collective-permute-start(bf16[400,128]{1,0:T(8,128)(2,1)S(1)} %line.1.s0), channel_id=1, source_target_pairs={{0,32},{16,48},{32,0},{48,16},{1,33},{17,49},{33,1},{49,17},{2,34}... | collective-permute-start | bytes 307208 | tf_op jit(solution)/shard_map/ppermute | solution.py:236
  31.9 2.1 %collective-permute-start.8 = (bf16[400,128]{1,0:T(8,128)(2,1)S(1)}, bf16[400,128]{1,0:T(8,128)(2,1)S(1)}, u32[]{:S(2)}, u32[]{:S(2)}) collective-permute-start(bf16[400,128]{1,0:T(8,128)(2,1)S(1)} %line.1.s0), channel_id=1, source_target_pairs={{0,16},{16,32},{32,48},{48,0},{1,17},{17,33},{33,49},{49,1},{2,18}... | collective-permute-start | bytes 307208 | tf_op jit(solution)/shard_map/ppermute | solution.py:236
  34.1 3.6 %collective-permute-done.9.s2 = bf16[400,128]{1,0:T(8,128)(2,1)S(1)} collective-permute-done((bf16[400,128]{1,0:T(8,128)(2,1)S(1)}, bf16[400,128]{1,0:T(8,128)(2,1)S(1)}, u32[]{:S(2)}, u32[]{:S(2)}) %collective-permute-start.9) | collective-permute-done | bytes 102432 | tf_op jit(solution)/shard_map/ppermute | solution.py:236
  37.7 2.5 %collective-permute-start.12 = (bf16[768,128]{1,0:T(8,128)(2,1)S(1)}, bf16[768,128]{1,0:T(8,128)(2,1)S(1)}, u32[]{:S(2)}, u32[]{:S(2)}) collective-permute-start(bf16[768,128]{1,0:T(8,128)(2,1)S(1)} %slice.9), channel_id=1, source_target_pairs={{0,48},{16,0},{32,16},{48,32},{1,49},{17,1},{33,17},{49,33},{2,50}... | collective-permute-start | bytes 589832 | tf_op jit(solution)/shard_map/ppermute | solution.py:238
  40.2 2.6 %collective-permute-done.8.s1 = bf16[400,128]{1,0:T(8,128)(2,1)S(1)} collective-permute-done((bf16[400,128]{1,0:T(8,128)(2,1)S(1)}, bf16[400,128]{1,0:T(8,128)(2,1)S(1)}, u32[]{:S(2)}, u32[]{:S(2)}) %collective-permute-start.8) | collective-permute-done | bytes 102432 | tf_op jit(solution)/shard_map/ppermute | solution.py:236
  42.8 1.6 %collective-permute-start.11 = (bf16[768,128]{1,0:T(8,128)(2,1)S(1)}, bf16[768,128]{1,0:T(8,128)(2,1)S(1)}, u32[]{:S(2)}, u32[]{:S(2)}) collective-permute-start(bf16[768,128]{1,0:T(8,128)(2,1)S(1)} %slice.8), channel_id=1, source_target_pairs={{0,16},{16,32},{32,48},{48,0},{1,17},{17,33},{33,49},{49,1},{2,18}... | collective-permute-start | bytes 589832 | tf_op jit(solution)/shard_map/ppermute | solution.py:237
  44.4 1.0 %copy-done = bf16[2,6,128,128]{3,2,1,0:T(8,128)(2,1)S(1)} copy-done((bf16[2,6,128,128]{3,2,1,0:T(8,128)(2,1)S(1)}, bf16[2,6,128,128]{3,2,1,0:T(8,128)(2,1)}, u32[]{:S(2)}) %copy-start) | copy-done | bytes 393240
  45.4 2.4 %build.1 = (bf16[1024,1664]{1,0:T(8,128)(2,1)S(1)}, bf16[1024,1664]{1,0:T(8,128)(2,1)S(1)}, bf16[13,128,128]{2,1,0:T(8,128)(2,1)S(1)}) custom-call(s32[5]{0:T(128)S(1)} %stack.23.sc_ref, bf16[1536,128]{1,0:T(8,128)(2,1)S(1)} %bitcast.12, bf16[1536,128]{1,0:T(8,128)(2,1)S(1)} %collective-permute-done.t1, bf16[1536,128]{1,0:T(8,128)(2,1)S(1)} %collective-permute-done.1.t2, ...), custom_call_target="tpu_custom_call" | custom-call | tf_op jit(solution)/shard_map/build/pallas_call | solution.py:133
  47.8 5.8 %collective-permute-done.11.f1 = bf16[768,128]{1,0:T(8,128)(2,1)S(1)} collective-permute-done((bf16[768,128]{1,0:T(8,128)(2,1)S(1)}, bf16[768,128]{1,0:T(8,128)(2,1)S(1)}, u32[]{:S(2)}, u32[]{:S(2)}) %collective-permute-start.11) | collective-permute-done | bytes 196640 | tf_op jit(solution)/shard_map/ppermute | solution.py:237
  53.6 2.8 %send.1 = f32[4,2,256,256]{3,2,1,0:T(8,128)S(1)} custom-call(s32[5]{0:T(128)S(1)} %stack.23.sc_ref, bf16[1024,1664]{1,0:T(8,128)(2,1)S(1)} %get-tuple-element.16.dy, bf16[1024,1664]{1,0:T(8,128)(2,1)S(1)} %get-tuple-element.17.dz, bf16[13,128,128]{2,1,0:T(8,128)(2,1)S(1)} %get-tuple-element.18.met, bf16[768,128]{1,0:T(8,128)(2,1)S(1)} %collective-permute-done.11.f1, ...), custom_call_target="tpu_custom_call" | custom-call | tf_op jit(solution)/shard_map/send/pallas_call | solution.py:185
  56.5 3.5 %keep.1 = f32[4,2,256,256]{3,2,1,0:T(8,128)S(1)} custom-call(s32[5]{0:T(128)S(1)} %stack.23.sc_ref, bf16[1024,1664]{1,0:T(8,128)(2,1)S(1)} %get-tuple-element.16.dy, bf16[1024,1664]{1,0:T(8,128)(2,1)S(1)} %get-tuple-element.17.dz, bf16[13,128,128]{2,1,0:T(8,128)(2,1)S(1)} %get-tuple-element.18.met, bf16[768,128]{1,0:T(8,128)(2,1)S(1)} %collective-permute-done.11.f1, ...), custom_call_target="tpu_custom_call" | custom-call | tf_op jit(solution)/shard_map/keep/pallas_call | solution.py:185
  60.7 0.7 share.1
  61.4 1.6 %collective-permute-start.14 = (bf16[256,256]{1,0:T(8,128)(2,1)S(1)}, bf16[256,256]{1,0:T(8,128)(2,1)S(1)}, u32[]{:S(2)}, u32[]{:S(2)}) collective-permute-start(bf16[256,256]{1,0:T(8,128)(2,1)S(1)} %get-tuple-element.20), channel_id=1, source_target_pairs={{0,4},{2,6},{4,8},{6,10},{8,12},{10,14},{12,0},{14,2},{1,5},{3,7},... | collective-permute-start | bytes 393224 | tf_op jit(solution)/shard_map/ppermute | solution.py:246
  63.0 2.7 %collective-permute-start.15 = (bf16[256,256]{1,0:T(8,128)(2,1)S(1)}, bf16[256,256]{1,0:T(8,128)(2,1)S(1)}, u32[]{:S(2)}, u32[]{:S(2)}) collective-permute-start(bf16[256,256]{1,0:T(8,128)(2,1)S(1)} %get-tuple-element.21), channel_id=1, source_target_pairs={{0,8},{2,10},{4,12},{6,14},{8,0},{10,2},{12,4},{14,6},{1,9},{3,11}... | collective-permute-start | bytes 393224 | tf_op jit(solution)/shard_map/ppermute | solution.py:246
  65.7 1.4 %collective-permute-start.16 = (bf16[256,256]{1,0:T(8,128)(2,1)S(1)}, bf16[256,256]{1,0:T(8,128)(2,1)S(1)}, u32[]{:S(2)}, u32[]{:S(2)}) collective-permute-start(bf16[256,256]{1,0:T(8,128)(2,1)S(1)} %get-tuple-element.22), channel_id=1, source_target_pairs={{0,12},{2,14},{4,0},{6,2},{8,4},{10,6},{12,8},{14,10},{1,13},{3,15... | collective-permute-start | bytes 393224 | tf_op jit(solution)/shard_map/ppermute | solution.py:246
  67.2 2.0 %collective-permute-start.18 = (bf16[256,256]{1,0:T(8,128)(2,1)S(1)}, bf16[256,256]{1,0:T(8,128)(2,1)S(1)}, u32[]{:S(2)}, u32[]{:S(2)}) collective-permute-start(bf16[256,256]{1,0:T(8,128)(2,1)S(1)} %get-tuple-element.24), channel_id=1, source_target_pairs={{0,6},{2,4},{4,10},{6,8},{8,14},{10,12},{12,2},{14,0},{1,7},{3,5},... | collective-permute-start | bytes 393224 | tf_op jit(solution)/shard_map/ppermute | solution.py:246
  69.9 6.9 %collective-permute-done.15 = bf16[256,256]{1,0:T(8,128)(2,1)S(1)} collective-permute-done((bf16[256,256]{1,0:T(8,128)(2,1)S(1)}, bf16[256,256]{1,0:T(8,128)(2,1)S(1)}, u32[]{:S(2)}, u32[]{:S(2)}) %collective-permute-start.15) | collective-permute-done | bytes 131104 | tf_op jit(solution)/shard_map/ppermute | solution.py:246
  76.8 2.0 %collective-permute-done.19 = bf16[256,256]{1,0:T(8,128)(2,1)S(1)} collective-permute-done((bf16[256,256]{1,0:T(8,128)(2,1)S(1)}, bf16[256,256]{1,0:T(8,128)(2,1)S(1)}, u32[]{:S(2)}, u32[]{:S(2)}) %collective-permute-start.19) | collective-permute-done | bytes 131104 | tf_op jit(solution)/shard_map/ppermute | solution.py:246
  78.8 3.8 %collective-permute-done.20 = bf16[256,256]{1,0:T(8,128)(2,1)S(1)} collective-permute-done((bf16[256,256]{1,0:T(8,128)(2,1)S(1)}, bf16[256,256]{1,0:T(8,128)(2,1)S(1)}, u32[]{:S(2)}, u32[]{:S(2)}) %collective-permute-start.20) | collective-permute-done | bytes 131104 | tf_op jit(solution)/shard_map/ppermute | solution.py:246
  82.8 6.3 %collective-permute-start.21 = (f32[256,256]{1,0:T(8,128)S(1)}, f32[256,256]{1,0:T(8,128)S(1)}, u32[]{:S(2)}, u32[]{:S(2)}) collective-permute-start(f32[256,256]{1,0:T(8,128)S(1)} %convert_add_fusion), channel_id=1, source_target_pairs={{0,0},{1,16},{2,32},{3,48},{16,1},{17,17},{18,33},{19,49},{32,2},{... | collective-permute-start | bytes 786440 | tf_op jit(solution)/shard_map/ppermute | solution.py:248
  89.1 8.3 %collective-permute-done.21 = f32[256,256]{1,0:T(8,128)S(1)} collective-permute-done((f32[256,256]{1,0:T(8,128)S(1)}, f32[256,256]{1,0:T(8,128)S(1)}, u32[]{:S(2)}, u32[]{:S(2)}) %collective-permute-start.21) | collective-permute-done | bytes 262176 | tf_op jit(solution)/shard_map/ppermute | solution.py:248
  (30 shorter events, 4.9 us)
Async XLA Ops:
  0.0 27.0 %collective-permute-start.4 = (bf16[1536,128]{1,0:T(8,128)(2,1)}, bf16[1536,128]{1,0:T(8,128)(2,1)S(1)}, u32[]{:S(2)}, u32[]{:S(2)}) collective-permute-start(bf16[1536,128]{1,0:T(8,128)(2,1)} %bitcast.7), channel_id=1, source_target_pairs={{0,48},{16,0},{32,16},{48,32},{1,49},{17,1},{33,17},{49,33},{2,50}... | collective-permute-start | bytes 1179656 | tf_op jit(solution)/shard_map/ppermute | solution.py:233
  5.4 26.5 %collective-permute-start.3 = (bf16[1536,128]{1,0:T(8,128)(2,1)}, bf16[1536,128]{1,0:T(8,128)(2,1)S(1)}, u32[]{:S(2)}, u32[]{:S(2)}) collective-permute-start(bf16[1536,128]{1,0:T(8,128)(2,1)} %bitcast.8), channel_id=1, source_target_pairs={{0,16},{16,32},{32,48},{48,0},{1,17},{17,33},{33,49},{49,1},{2,18}... | collective-permute-start | bytes 1179656 | tf_op jit(solution)/shard_map/ppermute | solution.py:232
  6.1 0.7 copy-start.1
  6.9 0.7 copy-start.2
  7.6 5.0 %collective-permute-start.7 = (bf16[104,128]{1,0:T(8,128)(2,1)S(1)}, bf16[104,128]{1,0:T(8,128)(2,1)S(1)}, u32[]{:S(2)}, u32[]{:S(2)}) collective-permute-start(bf16[104,128]{1,0:T(8,128)(2,1)S(1)} %pack.1.m0.p0), channel_id=1, source_target_pairs={{0,192},{64,0},{128,64},{192,128},{1,193},{65,1},{129,65},{193,129... | collective-permute-start | bytes 79880 | tf_op jit(solution)/shard_map/ppermute | solution.py:230
  8.1 5.4 %collective-permute-start.6 = (bf16[104,128]{1,0:T(8,128)(2,1)S(1)}, bf16[104,128]{1,0:T(8,128)(2,1)S(1)}, u32[]{:S(2)}, u32[]{:S(2)}) collective-permute-start(bf16[104,128]{1,0:T(8,128)(2,1)S(1)} %pack.1.m0.p0), channel_id=1, source_target_pairs={{0,128},{64,192},{128,0},{192,64},{1,129},{65,193},{129,1},{193,65... | collective-permute-start | bytes 79880 | tf_op jit(solution)/shard_map/ppermute | solution.py:230
  10.7 3.8 %collective-permute-start.5 = (bf16[104,128]{1,0:T(8,128)(2,1)S(1)}, bf16[104,128]{1,0:T(8,128)(2,1)S(1)}, u32[]{:S(2)}, u32[]{:S(2)}) collective-permute-start(bf16[104,128]{1,0:T(8,128)(2,1)S(1)} %pack.1.m0.p0), channel_id=1, source_target_pairs={{0,64},{64,128},{128,192},{192,0},{1,65},{65,129},{129,193},{193,1... | collective-permute-start | bytes 79880 | tf_op jit(solution)/shard_map/ppermute | solution.py:230
  15.1 10.3 %collective-permute-start.10 = (bf16[400,128]{1,0:T(8,128)(2,1)S(1)}, bf16[400,128]{1,0:T(8,128)(2,1)S(1)}, u32[]{:S(2)}, u32[]{:S(2)}) collective-permute-start(bf16[400,128]{1,0:T(8,128)(2,1)S(1)} %line.1.s0), channel_id=1, source_target_pairs={{0,48},{16,0},{32,16},{48,32},{1,49},{17,1},{33,17},{49,33},{2,50}... | collective-permute-start | bytes 307208 | tf_op jit(solution)/shard_map/ppermute | solution.py:236
  19.3 25.1 %collective-permute-start.2 = (bf16[1536,128]{1,0:T(8,128)(2,1)}, bf16[1536,128]{1,0:T(8,128)(2,1)S(1)}, u32[]{:S(2)}, u32[]{:S(2)}) collective-permute-start(bf16[1536,128]{1,0:T(8,128)(2,1)} %bitcast.9), channel_id=1, source_target_pairs={{0,192},{64,0},{128,64},{192,128},{1,193},{65,1},{129,65},{193,129... | collective-permute-start | bytes 1179656 | tf_op jit(solution)/shard_map/ppermute | solution.py:234
  21.6 22.8 %collective-permute-start.1 = (bf16[1536,128]{1,0:T(8,128)(2,1)}, bf16[1536,128]{1,0:T(8,128)(2,1)S(1)}, u32[]{:S(2)}, u32[]{:S(2)}) collective-permute-start(bf16[1536,128]{1,0:T(8,128)(2,1)} %bitcast.10), channel_id=1, source_target_pairs={{0,128},{64,192},{128,0},{192,64},{1,129},{65,193},{129,1},{193,65... | collective-permute-start | bytes 1179656 | tf_op jit(solution)/shard_map/ppermute | solution.py:234
  25.4 19.0 %collective-permute-start = (bf16[1536,128]{1,0:T(8,128)(2,1)}, bf16[1536,128]{1,0:T(8,128)(2,1)S(1)}, u32[]{:S(2)}, u32[]{:S(2)}) collective-permute-start(bf16[1536,128]{1,0:T(8,128)(2,1)} %bitcast.11), channel_id=1, source_target_pairs={{0,64},{64,128},{128,192},{192,0},{1,65},{65,129},{129,193},{193,1... | collective-permute-start | bytes 1179656 | tf_op jit(solution)/shard_map/ppermute | solution.py:234
  27.0 10.7 %collective-permute-start.9 = (bf16[400,128]{1,0:T(8,128)(2,1)S(1)}, bf16[400,128]{1,0:T(8,128)(2,1)S(1)}, u32[]{:S(2)}, u32[]{:S(2)}) collective-permute-start(bf16[400,128]{1,0:T(8,128)(2,1)S(1)} %line.1.s0), channel_id=1, source_target_pairs={{0,32},{16,48},{32,0},{48,16},{1,33},{17,49},{33,1},{49,17},{2,34}... | collective-permute-start | bytes 307208 | tf_op jit(solution)/shard_map/ppermute | solution.py:236
  31.9 10.9 %collective-permute-start.8 = (bf16[400,128]{1,0:T(8,128)(2,1)S(1)}, bf16[400,128]{1,0:T(8,128)(2,1)S(1)}, u32[]{:S(2)}, u32[]{:S(2)}) collective-permute-start(bf16[400,128]{1,0:T(8,128)(2,1)S(1)} %line.1.s0), channel_id=1, source_target_pairs={{0,16},{16,32},{32,48},{48,0},{1,17},{17,33},{33,49},{49,1},{2,18}... | collective-permute-start | bytes 307208 | tf_op jit(solution)/shard_map/ppermute | solution.py:236
  37.7 10.1 %collective-permute-start.12 = (bf16[768,128]{1,0:T(8,128)(2,1)S(1)}, bf16[768,128]{1,0:T(8,128)(2,1)S(1)}, u32[]{:S(2)}, u32[]{:S(2)}) collective-permute-start(bf16[768,128]{1,0:T(8,128)(2,1)S(1)} %slice.9), channel_id=1, source_target_pairs={{0,48},{16,0},{32,16},{48,32},{1,49},{17,1},{33,17},{49,33},{2,50}... | collective-permute-start | bytes 589832 | tf_op jit(solution)/shard_map/ppermute | solution.py:238
  42.8 10.8 %collective-permute-start.11 = (bf16[768,128]{1,0:T(8,128)(2,1)S(1)}, bf16[768,128]{1,0:T(8,128)(2,1)S(1)}, u32[]{:S(2)}, u32[]{:S(2)}) collective-permute-start(bf16[768,128]{1,0:T(8,128)(2,1)S(1)} %slice.8), channel_id=1, source_target_pairs={{0,16},{16,32},{32,48},{48,0},{1,17},{17,33},{33,49},{49,1},{2,18}... | collective-permute-start | bytes 589832 | tf_op jit(solution)/shard_map/ppermute | solution.py:237
  44.4 1.0 %copy-start = (bf16[2,6,128,128]{3,2,1,0:T(8,128)(2,1)S(1)}, bf16[2,6,128,128]{3,2,1,0:T(8,128)(2,1)}, u32[]{:S(2)}) copy-start(bf16[2,6,128,128]{3,2,1,0:T(8,128)(2,1)} %param.4) | copy-start | bytes 1179652
  56.4 4.2 %collective-permute-start.13 = (f32[4,2,256,256]{3,2,1,0:T(8,128)S(1)}, f32[4,2,256,256]{3,2,1,0:T(8,128)S(1)}, u32[]{:S(2)}, u32[]{:S(2)}) collective-permute-start(f32[4,2,256,256]{3,2,1,0:T(8,128)S(1)} %send.1), channel_id=1, source_target_pairs={{0,1},{1,0},{2,3},{3,2},{4,5},{5,4},{6,7},{7,6},{8,9},{9,8},{10,11... | collective-permute-start | bytes 6291464 | tf_op jit(solution)/shard_map/ppermute | solution.py:242
  61.4 7.8 %collective-permute-start.14 = (bf16[256,256]{1,0:T(8,128)(2,1)S(1)}, bf16[256,256]{1,0:T(8,128)(2,1)S(1)}, u32[]{:S(2)}, u32[]{:S(2)}) collective-permute-start(bf16[256,256]{1,0:T(8,128)(2,1)S(1)} %get-tuple-element.20), channel_id=1, source_target_pairs={{0,4},{2,6},{4,8},{6,10},{8,12},{10,14},{12,0},{14,2},{1,5},{3,7},... | collective-permute-start | bytes 393224 | tf_op jit(solution)/shard_map/ppermute | solution.py:246
  63.0 13.8 %collective-permute-start.15 = (bf16[256,256]{1,0:T(8,128)(2,1)S(1)}, bf16[256,256]{1,0:T(8,128)(2,1)S(1)}, u32[]{:S(2)}, u32[]{:S(2)}) collective-permute-start(bf16[256,256]{1,0:T(8,128)(2,1)S(1)} %get-tuple-element.21), channel_id=1, source_target_pairs={{0,8},{2,10},{4,12},{6,14},{8,0},{10,2},{12,4},{14,6},{1,9},{3,11}... | collective-permute-start | bytes 393224 | tf_op jit(solution)/shard_map/ppermute | solution.py:246
  65.7 11.1 %collective-permute-start.16 = (bf16[256,256]{1,0:T(8,128)(2,1)S(1)}, bf16[256,256]{1,0:T(8,128)(2,1)S(1)}, u32[]{:S(2)}, u32[]{:S(2)}) collective-permute-start(bf16[256,256]{1,0:T(8,128)(2,1)S(1)} %get-tuple-element.22), channel_id=1, source_target_pairs={{0,12},{2,14},{4,0},{6,2},{8,4},{10,6},{12,8},{14,10},{1,13},{3,15... | collective-permute-start | bytes 393224 | tf_op jit(solution)/shard_map/ppermute | solution.py:246
  67.1 9.6 %collective-permute-start.17 = (bf16[256,256]{1,0:T(8,128)(2,1)S(1)}, bf16[256,256]{1,0:T(8,128)(2,1)S(1)}, u32[]{:S(2)}, u32[]{:S(2)}) collective-permute-start(bf16[256,256]{1,0:T(8,128)(2,1)S(1)} %get-tuple-element.23), channel_id=1, source_target_pairs={{0,2},{2,0},{4,6},{6,4},{8,10},{10,8},{12,14},{14,12},{1,3},{3,1},... | collective-permute-start | bytes 393224 | tf_op jit(solution)/shard_map/ppermute | solution.py:246
  67.2 9.6 %collective-permute-start.18 = (bf16[256,256]{1,0:T(8,128)(2,1)S(1)}, bf16[256,256]{1,0:T(8,128)(2,1)S(1)}, u32[]{:S(2)}, u32[]{:S(2)}) collective-permute-start(bf16[256,256]{1,0:T(8,128)(2,1)S(1)} %get-tuple-element.24), channel_id=1, source_target_pairs={{0,6},{2,4},{4,10},{6,8},{8,14},{10,12},{12,2},{14,0},{1,7},{3,5},... | collective-permute-start | bytes 393224 | tf_op jit(solution)/shard_map/ppermute | solution.py:246
  69.2 9.6 %collective-permute-start.19 = (bf16[256,256]{1,0:T(8,128)(2,1)S(1)}, bf16[256,256]{1,0:T(8,128)(2,1)S(1)}, u32[]{:S(2)}, u32[]{:S(2)}) collective-permute-start(bf16[256,256]{1,0:T(8,128)(2,1)S(1)} %get-tuple-element.25), channel_id=1, source_target_pairs={{0,10},{2,8},{4,14},{6,12},{8,2},{10,0},{12,6},{14,4},{1,11},{3,9}... | collective-permute-start | bytes 393224 | tf_op jit(solution)/shard_map/ppermute | solution.py:246
  76.8 5.9 %collective-permute-start.20 = (bf16[256,256]{1,0:T(8,128)(2,1)S(1)}, bf16[256,256]{1,0:T(8,128)(2,1)S(1)}, u32[]{:S(2)}, u32[]{:S(2)}) collective-permute-start(bf16[256,256]{1,0:T(8,128)(2,1)S(1)} %get-tuple-element.26), channel_id=1, source_target_pairs={{0,14},{2,12},{4,2},{6,0},{8,6},{10,4},{12,10},{14,8},{1,15},{3,13... | collective-permute-start | bytes 393224 | tf_op jit(solution)/shard_map/ppermute | solution.py:246
  82.8 14.6 %collective-permute-start.21 = (f32[256,256]{1,0:T(8,128)S(1)}, f32[256,256]{1,0:T(8,128)S(1)}, u32[]{:S(2)}, u32[]{:S(2)}) collective-permute-start(f32[256,256]{1,0:T(8,128)S(1)} %convert_add_fusion), channel_id=1, source_target_pairs={{0,0},{1,16},{2,32},{3,48},{16,1},{17,17},{18,33},{19,49},{32,2},{... | collective-permute-start | bytes 786440 | tf_op jit(solution)/shard_map/ppermute | solution.py:248

commit v4 on v3

--- a/solution.py
+++ b/solution.py
@@ -145,79 +145,104 @@
     )(sc, *tiles, *zs, *parts, *smalls)
 
 
-def gram_kernel(flip, sc_ref, dy, dz, met, f1, f3, s2, out, far, lv, ls, sem):
-    zh, co = sc_ref[1], sc_ref[2]
-    parity = 1 - co if flip else co
-    opposite = back(zh, 2)
-    factor = 1.0 / (QS * 16 * AUXB) ** 0.5
-
-    @pl.when(lax.rem(zh, 2) == parity)
-    def _():
-        lv[...] = read_lists(s2, LIST0)
-        copy = pltpu.make_async_copy(lv, ls, sem)
-        copy.start()
-        far[...] = jnp.zeros_like(far)
-        copy.wait()
-        fill(f1, 0, met, ls, 0, far, 0)
-        fill(f3, 0, met, ls, 1, far, BS)
-
-    for h in range(2):
-        p = 2 * h + parity
-
-        def product(rhs):
-            for q in range(4):
-                lhs = dy[q * ROWS : (q + 1) * ROWS, 0:USED]
-                prod = lax.dot_general(
-                    lhs, rhs, (((1,), (1,)), ((), ())), preferred_element_type=F32
-                )
-                out[q, h] = prod * factor
-
-        @pl.when(p == opposite)
-        def _():
-            product(far[:, 0:USED])
-
-        @pl.when(p != opposite)
-        def _():
-            product(dz[pl.ds(pl.multiple_of(p * ROWS, ROWS), ROWS), 0:USED])
-
-
-def gram(flip, sc, dy, dz, met, f1, f3, small):
-    return pl.pallas_call(
-        functools.partial(gram_kernel, flip),
-        out_shape=jax.ShapeDtypeStruct((4, 2, ROWS, ROWS), F32),
-        in_specs=[SMEM] + [VMEM] * 6,
+def hold_kernel(tiles, late, out):
+    out[...] = tiles[...]
+
+
+def hold(tiles, late):
+    return pl.pallas_call(
+        hold_kernel,
+        out_shape=jax.ShapeDtypeStruct(tiles.shape, tiles.dtype),
+        in_specs=[VMEM] * 2,
+        out_specs=VMEM,
+        compiler_params=PARAMS,
+        name="hold",
+    )(tiles, late)
+
+
+def far_kernel(met, f1, f3, s2, far, lv, ls, sem):
+    lv[...] = read_lists(s2, LIST0)
+    copy = pltpu.make_async_copy(lv, ls, sem)
+    copy.start()
+    far[...] = jnp.zeros_like(far)
+    copy.wait()
+    fill(f1, 0, met, ls, 0, far, 0)
+    fill(f3, 0, met, ls, 1, far, BS)
+
+
+def far_block(met, f1, f3, small):
+    return pl.pallas_call(
+        far_kernel,
+        out_shape=jax.ShapeDtypeStruct((ROWS, WIDE), BF16),
+        in_specs=[VMEM] * 4,
         out_specs=VMEM,
         scratch_shapes=[
-            pltpu.VMEM((ROWS, WIDE), BF16),
             pltpu.VMEM((8, 128), jnp.int32),
             pltpu.SMEM((8, 128), jnp.int32),
             pltpu.SemaphoreType.DMA,
         ],
         compiler_params=PARAMS,
-        name="send" if flip else "keep",
-    )(sc, dy, dz, met, f1, f3, small)
-
-
-STEPS = tuple((k, w) for w in range(2) for k in range(4))
-
-
-def share_kernel(sc_ref, keep, got, own, *outs):
-    x, zl = sc_ref[3], sc_ref[4]
-    for (k, w), out in zip(STEPS, (own,) + outs):
-        q, h = lax.rem(x + k, 4), lax.rem(zl + w, 2)
-        out[...] = (keep[q, h] + got[q, h]).astype(out.dtype)
-
-
-def share(sc, keep, got):
-    piece = (ROWS, ROWS)
+        name="far",
+    )(met, f1, f3, small)
+
+
+def gram_kernel(flip, shifts, sc_ref, dy, dz, far, out):
+    zh, co, x = sc_ref[1], sc_ref[2], sc_ref[3]
+    core = 1 - co if flip else co
+    inner = jnp.logical_or(zh == 1, zh == 2)
+    opposite = back(zh, 2)
+    factor = 1.0 / (QS * 16 * AUXB) ** 0.5
+    for h in range(2):
+        p = jnp.where(inner, 2 * h + core, h + 2 * core)
+
+        def product(rhs):
+            for i, k in enumerate(shifts):
+                q = lax.rem(x + k, 4)
+                lhs = dy[pl.ds(pl.multiple_of(q * ROWS, ROWS), ROWS), 0:USED]
+                prod = lax.dot_general(
+                    lhs, rhs, (((1,), (1,)), ((), ())), preferred_element_type=F32
+                )
+                out[i, h] = prod * factor
+
+        @pl.when(p == opposite)
+        def _():
+            product(far[:, 0:USED])
+
+        @pl.when(p != opposite)
+        def _():
+            product(dz[pl.ds(pl.multiple_of(p * ROWS, ROWS), ROWS), 0:USED])
+
+
+def gram(flip, shifts, sc, dy, dz, far):
+    return pl.pallas_call(
+        functools.partial(gram_kernel, flip, shifts),
+        out_shape=jax.ShapeDtypeStruct((2, 2, ROWS, ROWS), F32),
+        in_specs=[SMEM] + [VMEM] * 3,
+        out_specs=VMEM,
+        compiler_params=PARAMS,
+    )(sc, dy, dz, far)
+
+
+def share_kernel(sc_ref, keep, got, *outs):
+    zl = sc_ref[4]
+    for n, out in enumerate(outs):
+        h = lax.rem(zl + n % 2, 2)
+        out[...] = (keep[n // 2, h] + got[n // 2, h]).astype(out.dtype)
+
+
+def share(sc, keep, got, types):
     return pl.pallas_call(
         share_kernel,
-        out_shape=(jax.ShapeDtypeStruct(piece, F32),) + (jax.ShapeDtypeStruct(piece, BF16),) * 7,
+        out_shape=tuple(jax.ShapeDtypeStruct((ROWS, ROWS), t) for t in types),
         in_specs=[SMEM, VMEM, VMEM],
-        out_specs=(VMEM,) * 8,
+        out_specs=(VMEM,) * 4,
         compiler_params=PARAMS,
         name="share",
     )(sc, keep, got)
+
+
+def landed(z, zl, co):
+    return 2 * zl + co if z in (1, 2) else zl + 2 * co
 
 
 def hop(k, w):
@@ -237,15 +262,21 @@
     f1 = lax.ppermute(z1[:HALF], "zh", ring(4, 1))
     f3 = lax.ppermute(z3[HALF:], "zh", ring(4, 3))
 
-    dy, dz, met = build(sc, ys, [z1, z3], parts, smalls)
-    send = gram(True, sc, dy, dz, met, f1, f3, smalls[2])
-    got = lax.ppermute(send, "co", ring(2, 1))
-    keep = gram(False, sc, dy, dz, met, f1, f3, smalls[2])
-    total, *shares = share(sc, keep, got)
-    for (k, w), piece in zip(STEPS[1:], shares):
-        total = total + lax.ppermute(piece, ("x", "zl"), hop(k, w)).astype(F32)
-    swap = [(a * 4 + b, b * 4 + a) for a in range(4) for b in range(4)]
-    return lax.ppermute(total, ("zh", "zl", "co"), swap)
+    dy, dz, met = build(sc, [hold(tiles, z3)] + ys[1:], [z1, z3], parts, smalls)
+    far = far_block(met, f1, f3, smalls[2])
+    pieces = {}
+    for shifts, last in (((2, 1), BF16), ((3, 0), F32)):
+        send = gram(True, shifts, sc, dy, dz, far)
+        got = lax.ppermute(send, "co", ring(2, 1))
+        keep = gram(False, shifts, sc, dy, dz, far)
+        names = [(k, w) for k in shifts for w in range(2)]
+        pieces.update(zip(names, share(sc, keep, got, (BF16, BF16, last, BF16))))
+    total = pieces[0, 0]
+    for k, w in ((2, 1), (2, 0), (1, 1), (1, 0), (3, 1), (3, 0), (0, 1)):
+        total = total + lax.ppermute(pieces[k, w], ("x", "zl"), hop(k, w)).astype(F32)
+    spots = [(z, zl, co) for z in range(4) for zl in range(2) for co in range(2)]
+    move = [(4 * z + 2 * zl + co, 4 * landed(z, zl, co) + z) for z, zl, co in spots]
+    return lax.ppermute(total, ("zh", "zl", "co"), move)
 
 
 def solution(mesh):

time: 98.3 us -> 96 us (0.977)
  the two profiles are of different devices: /device:TPU:40 before, /device:TPU:32 now
where the time goes in v4:
time: 96 us; the launch traced here: 95.8 us
  starting transfers between devices  41.3 us (43%)
  waiting for transfers between devices  37.6 us (39%)
  Pallas kernels  12.5 us (13%)
  local copies, waits for them, and re-layouts  3.97 us (4%)
    ppermute x1, waiting for transfers between devices, local(): return lax.ppermute(total, ('zh', 'zl', 'co'), move)  12.2 us
    ppermute x7, starting transfers between devices, local(): lax.ppermute(pieces[k, w], ('x', 'zl'), hop(k, w)).astype(F32)  9.76 us
    ppermute x3, waiting for transfers between devices, local(): lax.ppermute(small, 'zh', ring(4, k))  7.68 us
    ppermute x1, waiting for transfers between devices, local(): f1 = lax.ppermute(z1[:HALF], 'zh', ring(4, 1))  7.29 us
    pallas_call x4, Pallas kernels, gram(): pl.pallas_call(functools.partial(gram_kernel, flip, shifts), out_shape=ja...  7.22 us
    ppermute x3, starting transfers between devices, local(): ys = [tiles] + [lax.ppermute(tiles, 'y', ring(4, k)) for k in (1, 2, 3)]  7.05 us
    ppermute x7, waiting for transfers between devices, local(): lax.ppermute(pieces[k, w], ('x', 'zl'), hop(k, w)).astype(F32)  6.85 us
    ppermute x3, starting transfers between devices, local(): lax.ppermute(small, 'zh', ring(4, k))  6.82 us
  transfers between devices with their start and end apart: 23, of which 13 were waited for; matrix products, arithmetic and copies ran while one was open for 1% of the time, Pallas kernels for 10%

profile of v4, /device:TPU:32, one launch (start us, length us, event | category | flops | bytes accessed | tf_op | source)
XLA Modules:
  0.0 95.8 jit_solution(2792298333350179864)
XLA Ops:
  0.0 5.4 %collective-permute-start = (bf16[1536,128]{1,0:T(8,128)(2,1)}, bf16[1536,128]{1,0:T(8,128)(2,1)S(1)}, u32[]{:S(2)}, u32[]{:S(2)}) collective-permute-start(bf16[1536,128]{1,0:T(8,128)(2,1)} %bitcast.7), channel_id=1, source_target_pairs={{0,48},{16,0},{32,16},{48,32},{1,49},{17,1},{33,17},{49,33},{2,50}... | collective-permute-start | bytes 1179656 | tf_op jit(solution)/shard_map/ppermute | solution.py:258
  7.6 1.6 %collective-permute-start.5 = (bf16[104,128]{1,0:T(8,128)(2,1)S(1)}, bf16[104,128]{1,0:T(8,128)(2,1)S(1)}, u32[]{:S(2)}, u32[]{:S(2)}) collective-permute-start(bf16[104,128]{1,0:T(8,128)(2,1)S(1)} %pack.1.m0.p0), channel_id=1, source_target_pairs={{0,64},{64,128},{128,192},{192,0},{1,65},{65,129},{129,193},{193,1... | collective-permute-start | bytes 79880 | tf_op jit(solution)/shard_map/ppermute | solution.py:255
  9.2 2.9 %collective-permute-start.6 = (bf16[104,128]{1,0:T(8,128)(2,1)S(1)}, bf16[104,128]{1,0:T(8,128)(2,1)S(1)}, u32[]{:S(2)}, u32[]{:S(2)}) collective-permute-start(bf16[104,128]{1,0:T(8,128)(2,1)S(1)} %pack.1.m0.p0), channel_id=1, source_target_pairs={{0,128},{64,192},{128,0},{192,64},{1,129},{65,193},{129,1},{193,65... | collective-permute-start | bytes 79880 | tf_op jit(solution)/shard_map/ppermute | solution.py:255
  12.1 1.3 %collective-permute-start.7 = (bf16[104,128]{1,0:T(8,128)(2,1)S(1)}, bf16[104,128]{1,0:T(8,128)(2,1)S(1)}, u32[]{:S(2)}, u32[]{:S(2)}) collective-permute-start(bf16[104,128]{1,0:T(8,128)(2,1)S(1)} %pack.1.m0.p0), channel_id=1, source_target_pairs={{0,192},{64,0},{128,64},{192,128},{1,193},{65,1},{129,65},{193,129... | collective-permute-start | bytes 79880 | tf_op jit(solution)/shard_map/ppermute | solution.py:255
  13.6 1.0 %collective-permute-done.6.m2.p2 = bf16[104,128]{1,0:T(8,128)(2,1)S(1)} collective-permute-done((bf16[104,128]{1,0:T(8,128)(2,1)S(1)}, bf16[104,128]{1,0:T(8,128)(2,1)S(1)}, u32[]{:S(2)}, u32[]{:S(2)}) %collective-permute-start.6) | collective-permute-done | bytes 26656 | tf_op jit(solution)/shard_map/ppermute | solution.py:255
  14.6 1.4 %collective-permute-done.7.m3.p3 = bf16[104,128]{1,0:T(8,128)(2,1)S(1)} collective-permute-done((bf16[104,128]{1,0:T(8,128)(2,1)S(1)}, bf16[104,128]{1,0:T(8,128)(2,1)S(1)}, u32[]{:S(2)}, u32[]{:S(2)}) %collective-permute-start.7) | collective-permute-done | bytes 26656 | tf_op jit(solution)/shard_map/ppermute | solution.py:255
  16.5 3.9 %collective-permute-start.9 = (bf16[400,128]{1,0:T(8,128)(2,1)S(1)}, bf16[400,128]{1,0:T(8,128)(2,1)S(1)}, u32[]{:S(2)}, u32[]{:S(2)}) collective-permute-start(bf16[400,128]{1,0:T(8,128)(2,1)S(1)} %line.1.s0), channel_id=1, source_target_pairs={{0,32},{16,48},{32,0},{48,16},{1,33},{17,49},{33,1},{49,17},{2,34}... | collective-permute-start | bytes 307208 | tf_op jit(solution)/shard_map/ppermute | solution.py:261
  20.6 3.8 %collective-permute-start.2 = (bf16[1536,128]{1,0:T(8,128)(2,1)}, bf16[1536,128]{1,0:T(8,128)(2,1)S(1)}, u32[]{:S(2)}, u32[]{:S(2)}) collective-permute-start(bf16[1536,128]{1,0:T(8,128)(2,1)} %bitcast.10), channel_id=1, source_target_pairs={{0,128},{64,192},{128,0},{192,64},{1,129},{65,193},{129,1},{193,65... | collective-permute-start | bytes 1179656 | tf_op jit(solution)/shard_map/ppermute | solution.py:259
  24.5 4.1 %collective-permute-done.9.s2 = bf16[400,128]{1,0:T(8,128)(2,1)S(1)} collective-permute-done((bf16[400,128]{1,0:T(8,128)(2,1)S(1)}, bf16[400,128]{1,0:T(8,128)(2,1)S(1)}, u32[]{:S(2)}, u32[]{:S(2)}) %collective-permute-start.9) | collective-permute-done | bytes 102432 | tf_op jit(solution)/shard_map/ppermute | solution.py:261
  28.6 3.0 %collective-permute-start.3 = (bf16[1536,128]{1,0:T(8,128)(2,1)}, bf16[1536,128]{1,0:T(8,128)(2,1)S(1)}, u32[]{:S(2)}, u32[]{:S(2)}) collective-permute-start(bf16[1536,128]{1,0:T(8,128)(2,1)} %bitcast.11), channel_id=1, source_target_pairs={{0,192},{64,0},{128,64},{192,128},{1,193},{65,1},{129,65},{193,129... | collective-permute-start | bytes 1179656 | tf_op jit(solution)/shard_map/ppermute | solution.py:259
  31.6 1.5 %collective-permute-start.10 = (bf16[400,128]{1,0:T(8,128)(2,1)S(1)}, bf16[400,128]{1,0:T(8,128)(2,1)S(1)}, u32[]{:S(2)}, u32[]{:S(2)}) collective-permute-start(bf16[400,128]{1,0:T(8,128)(2,1)S(1)} %line.1.s0), channel_id=1, source_target_pairs={{0,48},{16,0},{32,16},{48,32},{1,49},{17,1},{33,17},{49,33},{2,50}... | collective-permute-start | bytes 307208 | tf_op jit(solution)/shard_map/ppermute | solution.py:261
  33.1 1.5 %collective-permute-start.8 = (bf16[400,128]{1,0:T(8,128)(2,1)S(1)}, bf16[400,128]{1,0:T(8,128)(2,1)S(1)}, u32[]{:S(2)}, u32[]{:S(2)}) collective-permute-start(bf16[400,128]{1,0:T(8,128)(2,1)S(1)} %line.1.s0), channel_id=1, source_target_pairs={{0,16},{16,32},{32,48},{48,0},{1,17},{17,33},{33,49},{49,1},{2,18}... | collective-permute-start | bytes 307208 | tf_op jit(solution)/shard_map/ppermute | solution.py:261
  34.6 2.6 %collective-permute-done.10.s3 = bf16[400,128]{1,0:T(8,128)(2,1)S(1)} collective-permute-done((bf16[400,128]{1,0:T(8,128)(2,1)S(1)}, bf16[400,128]{1,0:T(8,128)(2,1)S(1)}, u32[]{:S(2)}, u32[]{:S(2)}) %collective-permute-start.10) | collective-permute-done | bytes 102432 | tf_op jit(solution)/shard_map/ppermute | solution.py:261
  37.2 2.8 %collective-permute-start.12 = (bf16[768,128]{1,0:T(8,128)(2,1)S(1)}, bf16[768,128]{1,0:T(8,128)(2,1)S(1)}, u32[]{:S(2)}, u32[]{:S(2)}) collective-permute-start(bf16[768,128]{1,0:T(8,128)(2,1)S(1)} %slice.9), channel_id=1, source_target_pairs={{0,48},{16,0},{32,16},{48,32},{1,49},{17,1},{33,17},{49,33},{2,50}... | collective-permute-start | bytes 589832 | tf_op jit(solution)/shard_map/ppermute | solution.py:263
  40.0 1.0 %collective-permute-done.8.s1 = bf16[400,128]{1,0:T(8,128)(2,1)S(1)} collective-permute-done((bf16[400,128]{1,0:T(8,128)(2,1)S(1)}, bf16[400,128]{1,0:T(8,128)(2,1)S(1)}, u32[]{:S(2)}, u32[]{:S(2)}) %collective-permute-start.8) | collective-permute-done | bytes 102432 | tf_op jit(solution)/shard_map/ppermute | solution.py:261
  41.0 1.0 %copy-done = bf16[2,6,128,128]{3,2,1,0:T(8,128)(2,1)S(1)} copy-done((bf16[2,6,128,128]{3,2,1,0:T(8,128)(2,1)S(1)}, bf16[2,6,128,128]{3,2,1,0:T(8,128)(2,1)}, u32[]{:S(2)}) %copy-start) | copy-done | bytes 393240
  42.0 2.4 %build.1 = (bf16[1024,1664]{1,0:T(8,128)(2,1)S(1)}, bf16[1024,1664]{1,0:T(8,128)(2,1)S(1)}, bf16[13,128,128]{2,1,0:T(8,128)(2,1)S(1)}) custom-call(s32[5]{0:T(128)S(1)} %stack.23.sc_ref, bf16[1536,128]{1,0:T(8,128)(2,1)S(1)} %hold.1.t0, bf16[1536,128]{1,0:T(8,128)(2,1)S(1)} %collective-permute-done.1.t1, bf16[1536,128]{1,0:T(8,128)(2,1)S(1)} %collective-permute-done.2.t2, ...), custom_call_target="tpu_custom_call" | custom-call | tf_op jit(solution)/shard_map/build/pallas_call | solution.py:133
  44.5 1.2 %collective-permute-done.12.f3 = bf16[768,128]{1,0:T(8,128)(2,1)S(1)} collective-permute-done((bf16[768,128]{1,0:T(8,128)(2,1)S(1)}, bf16[768,128]{1,0:T(8,128)(2,1)S(1)}, u32[]{:S(2)}, u32[]{:S(2)}) %collective-permute-start.12) | collective-permute-done | bytes 196640 | tf_op jit(solution)/shard_map/ppermute | solution.py:263
  45.7 7.3 %collective-permute-done.11.f1 = bf16[768,128]{1,0:T(8,128)(2,1)S(1)} collective-permute-done((bf16[768,128]{1,0:T(8,128)(2,1)S(1)}, bf16[768,128]{1,0:T(8,128)(2,1)S(1)}, u32[]{:S(2)}, u32[]{:S(2)}) %collective-permute-start.11) | collective-permute-done | bytes 196640 | tf_op jit(solution)/shard_map/ppermute | solution.py:262
  53.9 1.9 %shard_map.49 = f32[2,2,256,256]{3,2,1,0:T(8,128)S(1)} custom-call(s32[5]{0:T(128)S(1)} %stack.23.sc_ref, bf16[1024,1664]{1,0:T(8,128)(2,1)S(1)} %get-tuple-element.16.dy, bf16[1024,1664]{1,0:T(8,128)(2,1)S(1)} %get-tuple-element.17.dz, bf16[256,1664]{1,0:T(8,128)(2,1)S(1)} %far.1), custom_call_target="tpu_custom_call" | custom-call | tf_op jit(solution)/shard_map/pallas_call | solution.py:217
  55.9 1.8 %shard_map.47 = f32[2,2,256,256]{3,2,1,0:T(8,128)S(1)} custom-call(s32[5]{0:T(128)S(1)} %stack.23.sc_ref, bf16[1024,1664]{1,0:T(8,128)(2,1)S(1)} %get-tuple-element.16.dy, bf16[1024,1664]{1,0:T(8,128)(2,1)S(1)} %get-tuple-element.17.dz, bf16[256,1664]{1,0:T(8,128)(2,1)S(1)} %far.1), custom_call_target="tpu_custom_call" | custom-call | tf_op jit(solution)/shard_map/pallas_call | solution.py:217
  58.3 1.8 %shard_map.48.keep = f32[2,2,256,256]{3,2,1,0:T(8,128)S(1)} custom-call(s32[5]{0:T(128)S(1)} %stack.23.sc_ref, bf16[1024,1664]{1,0:T(8,128)(2,1)S(1)} %get-tuple-element.16.dy, bf16[1024,1664]{1,0:T(8,128)(2,1)S(1)} %get-tuple-element.17.dz, bf16[256,1664]{1,0:T(8,128)(2,1)S(1)} %far.1), custom_call_target="tpu_custom_call" | custom-call | tf_op jit(solution)/shard_map/pallas_call | solution.py:217
  60.7 2.4 %collective-permute-start.15 = (bf16[256,256]{1,0:T(8,128)(2,1)S(1)}, bf16[256,256]{1,0:T(8,128)(2,1)S(1)}, u32[]{:S(2)}, u32[]{:S(2)}) collective-permute-start(bf16[256,256]{1,0:T(8,128)(2,1)S(1)} %get-tuple-element.20), channel_id=1, source_target_pairs={{0,10},{2,8},{4,14},{6,12},{8,2},{10,0},{12,6},{14,4},{1,11},{3,9}... | collective-permute-start | bytes 393224 | tf_op jit(solution)/shard_map/ppermute | solution.py:276
  63.9 1.8 %shard_map.46.keep = f32[2,2,256,256]{3,2,1,0:T(8,128)S(1)} custom-call(s32[5]{0:T(128)S(1)} %stack.23.sc_ref, bf16[1024,1664]{1,0:T(8,128)(2,1)S(1)} %get-tuple-element.16.dy, bf16[1024,1664]{1,0:T(8,128)(2,1)S(1)} %get-tuple-element.17.dz, bf16[256,1664]{1,0:T(8,128)(2,1)S(1)} %far.1), custom_call_target="tpu_custom_call" | custom-call | tf_op jit(solution)/shard_map/pallas_call | solution.py:217
  65.7 2.9 %collective-permute-start.17 = (bf16[256,256]{1,0:T(8,128)(2,1)S(1)}, bf16[256,256]{1,0:T(8,128)(2,1)S(1)}, u32[]{:S(2)}, u32[]{:S(2)}) collective-permute-start(bf16[256,256]{1,0:T(8,128)(2,1)S(1)} %get-tuple-element.22), channel_id=1, source_target_pairs={{0,6},{2,4},{4,10},{6,8},{8,14},{10,12},{12,2},{14,0},{1,7},{3,5},... | collective-permute-start | bytes 393224 | tf_op jit(solution)/shard_map/ppermute | solution.py:276
  68.6 1.5 %collective-permute-start.18 = (bf16[256,256]{1,0:T(8,128)(2,1)S(1)}, bf16[256,256]{1,0:T(8,128)(2,1)S(1)}, u32[]{:S(2)}, u32[]{:S(2)}) collective-permute-start(bf16[256,256]{1,0:T(8,128)(2,1)S(1)} %get-tuple-element.23), channel_id=1, source_target_pairs={{0,4},{2,6},{4,8},{6,10},{8,12},{10,14},{12,0},{14,2},{1,5},{3,7},... | collective-permute-start | bytes 393224 | tf_op jit(solution)/shard_map/ppermute | solution.py:276
  70.7 1.1 %collective-permute-start.19 = (bf16[256,256]{1,0:T(8,128)(2,1)S(1)}, bf16[256,256]{1,0:T(8,128)(2,1)S(1)}, u32[]{:S(2)}, u32[]{:S(2)}) collective-permute-start(bf16[256,256]{1,0:T(8,128)(2,1)S(1)} %get-tuple-element.24), channel_id=1, source_target_pairs={{0,14},{2,12},{4,2},{6,0},{8,6},{10,4},{12,10},{14,8},{1,15},{3,13... | collective-permute-start | bytes 393224 | tf_op jit(solution)/shard_map/ppermute | solution.py:276
  72.7 1.7 %collective-permute-done.16 = bf16[256,256]{1,0:T(8,128)(2,1)S(1)} collective-permute-done((bf16[256,256]{1,0:T(8,128)(2,1)S(1)}, bf16[256,256]{1,0:T(8,128)(2,1)S(1)}, u32[]{:S(2)}, u32[]{:S(2)}) %collective-permute-start.16) | collective-permute-done | bytes 131104 | tf_op jit(solution)/shard_map/ppermute | solution.py:276
  74.6 2.5 %collective-permute-done.18 = bf16[256,256]{1,0:T(8,128)(2,1)S(1)} collective-permute-done((bf16[256,256]{1,0:T(8,128)(2,1)S(1)}, bf16[256,256]{1,0:T(8,128)(2,1)S(1)}, u32[]{:S(2)}, u32[]{:S(2)}) %collective-permute-start.18) | collective-permute-done | bytes 131104 | tf_op jit(solution)/shard_map/ppermute | solution.py:276
  78.6 1.1 %collective-permute-done.21 = bf16[256,256]{1,0:T(8,128)(2,1)S(1)} collective-permute-done((bf16[256,256]{1,0:T(8,128)(2,1)S(1)}, bf16[256,256]{1,0:T(8,128)(2,1)S(1)}, u32[]{:S(2)}, u32[]{:S(2)}) %collective-permute-start.21) | collective-permute-done | bytes 131104 | tf_op jit(solution)/shard_map/ppermute | solution.py:276
  79.9 3.0 %collective-permute-start.22 = (f32[256,256]{1,0:T(8,128)S(1)}, f32[256,256]{1,0:T(8,128)S(1)}, u32[]{:S(2)}, u32[]{:S(2)}) collective-permute-start(f32[256,256]{1,0:T(8,128)S(1)} %convert_add_fusion), channel_id=1, source_target_pairs={{0,0},{1,32},{2,16},{3,48},{16,1},{17,17},{18,33},{19,49},{32,2},{... | collective-permute-start | bytes 786440 | tf_op jit(solution)/shard_map/ppermute | solution.py:279
  82.9 12.2 %collective-permute-done.22 = f32[256,256]{1,0:T(8,128)S(1)} collective-permute-done((f32[256,256]{1,0:T(8,128)S(1)}, f32[256,256]{1,0:T(8,128)S(1)}, u32[]{:S(2)}, u32[]{:S(2)}) %collective-permute-start.22) | collective-permute-done | bytes 262176 | tf_op jit(solution)/shard_map/ppermute | solution.py:279
  (37 shorter events, 10.4 us)
Async XLA Ops:
  0.0 31.6 %collective-permute-start = (bf16[1536,128]{1,0:T(8,128)(2,1)}, bf16[1536,128]{1,0:T(8,128)(2,1)S(1)}, u32[]{:S(2)}, u32[]{:S(2)}) collective-permute-start(bf16[1536,128]{1,0:T(8,128)(2,1)} %bitcast.7), channel_id=1, source_target_pairs={{0,48},{16,0},{32,16},{48,32},{1,49},{17,1},{33,17},{49,33},{2,50}... | collective-permute-start | bytes 1179656 | tf_op jit(solution)/shard_map/ppermute | solution.py:258
  5.4 27.7 %collective-permute-start.4 = (bf16[1536,128]{1,0:T(8,128)(2,1)}, bf16[1536,128]{1,0:T(8,128)(2,1)S(1)}, u32[]{:S(2)}, u32[]{:S(2)}) collective-permute-start(bf16[1536,128]{1,0:T(8,128)(2,1)} %bitcast.8), channel_id=1, source_target_pairs={{0,16},{16,32},{32,48},{48,0},{1,17},{17,33},{33,49},{49,1},{2,18}... | collective-permute-start | bytes 1179656 | tf_op jit(solution)/shard_map/ppermute | solution.py:257
  6.1 0.7 copy-start.1
  6.9 0.7 copy-start.2
  7.6 5.9 %collective-permute-start.5 = (bf16[104,128]{1,0:T(8,128)(2,1)S(1)}, bf16[104,128]{1,0:T(8,128)(2,1)S(1)}, u32[]{:S(2)}, u32[]{:S(2)}) collective-permute-start(bf16[104,128]{1,0:T(8,128)(2,1)S(1)} %pack.1.m0.p0), channel_id=1, source_target_pairs={{0,64},{64,128},{128,192},{192,0},{1,65},{65,129},{129,193},{193,1... | collective-permute-start | bytes 79880 | tf_op jit(solution)/shard_map/ppermute | solution.py:255
  9.2 5.4 %collective-permute-start.6 = (bf16[104,128]{1,0:T(8,128)(2,1)S(1)}, bf16[104,128]{1,0:T(8,128)(2,1)S(1)}, u32[]{:S(2)}, u32[]{:S(2)}) collective-permute-start(bf16[104,128]{1,0:T(8,128)(2,1)S(1)} %pack.1.m0.p0), channel_id=1, source_target_pairs={{0,128},{64,192},{128,0},{192,64},{1,129},{65,193},{129,1},{193,65... | collective-permute-start | bytes 79880 | tf_op jit(solution)/shard_map/ppermute | solution.py:255
  12.1 3.8 %collective-permute-start.7 = (bf16[104,128]{1,0:T(8,128)(2,1)S(1)}, bf16[104,128]{1,0:T(8,128)(2,1)S(1)}, u32[]{:S(2)}, u32[]{:S(2)}) collective-permute-start(bf16[104,128]{1,0:T(8,128)(2,1)S(1)} %pack.1.m0.p0), channel_id=1, source_target_pairs={{0,192},{64,0},{128,64},{192,128},{1,193},{65,1},{129,65},{193,129... | collective-permute-start | bytes 79880 | tf_op jit(solution)/shard_map/ppermute | solution.py:255
  16.5 12.0 %collective-permute-start.9 = (bf16[400,128]{1,0:T(8,128)(2,1)S(1)}, bf16[400,128]{1,0:T(8,128)(2,1)S(1)}, u32[]{:S(2)}, u32[]{:S(2)}) collective-permute-start(bf16[400,128]{1,0:T(8,128)(2,1)S(1)} %line.1.s0), channel_id=1, source_target_pairs={{0,32},{16,48},{32,0},{48,16},{1,33},{17,49},{33,1},{49,17},{2,34}... | collective-permute-start | bytes 307208 | tf_op jit(solution)/shard_map/ppermute | solution.py:261
  20.4 21.6 %collective-permute-start.1 = (bf16[1536,128]{1,0:T(8,128)(2,1)}, bf16[1536,128]{1,0:T(8,128)(2,1)S(1)}, u32[]{:S(2)}, u32[]{:S(2)}) collective-permute-start(bf16[1536,128]{1,0:T(8,128)(2,1)} %bitcast.9), channel_id=1, source_target_pairs={{0,64},{64,128},{128,192},{192,0},{1,65},{65,129},{129,193},{193,1... | collective-permute-start | bytes 1179656 | tf_op jit(solution)/shard_map/ppermute | solution.py:259
  20.6 21.4 %collective-permute-start.2 = (bf16[1536,128]{1,0:T(8,128)(2,1)}, bf16[1536,128]{1,0:T(8,128)(2,1)S(1)}, u32[]{:S(2)}, u32[]{:S(2)}) collective-permute-start(bf16[1536,128]{1,0:T(8,128)(2,1)} %bitcast.10), channel_id=1, source_target_pairs={{0,128},{64,192},{128,0},{192,64},{1,129},{65,193},{129,1},{193,65... | collective-permute-start | bytes 1179656 | tf_op jit(solution)/shard_map/ppermute | solution.py:259
  28.6 13.4 %collective-permute-start.3 = (bf16[1536,128]{1,0:T(8,128)(2,1)}, bf16[1536,128]{1,0:T(8,128)(2,1)S(1)}, u32[]{:S(2)}, u32[]{:S(2)}) collective-permute-start(bf16[1536,128]{1,0:T(8,128)(2,1)} %bitcast.11), channel_id=1, source_target_pairs={{0,192},{64,0},{128,64},{192,128},{1,193},{65,1},{129,65},{193,129... | collective-permute-start | bytes 1179656 | tf_op jit(solution)/shard_map/ppermute | solution.py:259
  31.6 5.6 %collective-permute-start.10 = (bf16[400,128]{1,0:T(8,128)(2,1)S(1)}, bf16[400,128]{1,0:T(8,128)(2,1)S(1)}, u32[]{:S(2)}, u32[]{:S(2)}) collective-permute-start(bf16[400,128]{1,0:T(8,128)(2,1)S(1)} %line.1.s0), channel_id=1, source_target_pairs={{0,48},{16,0},{32,16},{48,32},{1,49},{17,1},{33,17},{49,33},{2,50}... | collective-permute-start | bytes 307208 | tf_op jit(solution)/shard_map/ppermute | solution.py:261
  33.1 7.9 %collective-permute-start.8 = (bf16[400,128]{1,0:T(8,128)(2,1)S(1)}, bf16[400,128]{1,0:T(8,128)(2,1)S(1)}, u32[]{:S(2)}, u32[]{:S(2)}) collective-permute-start(bf16[400,128]{1,0:T(8,128)(2,1)S(1)} %line.1.s0), channel_id=1, source_target_pairs={{0,16},{16,32},{32,48},{48,0},{1,17},{17,33},{33,49},{49,1},{2,18}... | collective-permute-start | bytes 307208 | tf_op jit(solution)/shard_map/ppermute | solution.py:261
  37.2 8.5 %collective-permute-start.12 = (bf16[768,128]{1,0:T(8,128)(2,1)S(1)}, bf16[768,128]{1,0:T(8,128)(2,1)S(1)}, u32[]{:S(2)}, u32[]{:S(2)}) collective-permute-start(bf16[768,128]{1,0:T(8,128)(2,1)S(1)} %slice.9), channel_id=1, source_target_pairs={{0,48},{16,0},{32,16},{48,32},{1,49},{17,1},{33,17},{49,33},{2,50}... | collective-permute-start | bytes 589832 | tf_op jit(solution)/shard_map/ppermute | solution.py:263
  41.0 12.0 %collective-permute-start.11 = (bf16[768,128]{1,0:T(8,128)(2,1)S(1)}, bf16[768,128]{1,0:T(8,128)(2,1)S(1)}, u32[]{:S(2)}, u32[]{:S(2)}) collective-permute-start(bf16[768,128]{1,0:T(8,128)(2,1)S(1)} %slice.8), channel_id=1, source_target_pairs={{0,16},{16,32},{32,48},{48,0},{1,17},{17,33},{33,49},{49,1},{2,18}... | collective-permute-start | bytes 589832 | tf_op jit(solution)/shard_map/ppermute | solution.py:262
  41.0 1.0 %copy-start = (bf16[2,6,128,128]{3,2,1,0:T(8,128)(2,1)S(1)}, bf16[2,6,128,128]{3,2,1,0:T(8,128)(2,1)}, u32[]{:S(2)}) copy-start(bf16[2,6,128,128]{3,2,1,0:T(8,128)(2,1)} %param.4) | copy-start | bytes 1179652
  55.8 4.2 %collective-permute-start.14 = (f32[2,2,256,256]{3,2,1,0:T(8,128)S(1)}, f32[2,2,256,256]{3,2,1,0:T(8,128)S(1)}, u32[]{:S(2)}, u32[]{:S(2)}) collective-permute-start(f32[2,2,256,256]{3,2,1,0:T(8,128)S(1)} %shard_map.49), channel_id=1, source_target_pairs={{0,1},{1,0},{2,3},{3,2},{4,5},{5,4},{6,7},{7,6},{8,9},{9,8},{10,11... | collective-permute-start | bytes 3145736 | tf_op jit(solution)/shard_map/ppermute | solution.py:270
  57.7 12.4 %collective-permute-start.13 = (f32[2,2,256,256]{3,2,1,0:T(8,128)S(1)}, f32[2,2,256,256]{3,2,1,0:T(8,128)S(1)}, u32[]{:S(2)}, u32[]{:S(2)}) collective-permute-start(f32[2,2,256,256]{3,2,1,0:T(8,128)S(1)} %shard_map.47), channel_id=1, source_target_pairs={{0,1},{1,0},{2,3},{3,2},{4,5},{5,4},{6,7},{7,6},{8,9},{9,8},{10,11... | collective-permute-start | bytes 3145736 | tf_op jit(solution)/shard_map/ppermute | solution.py:270
  60.7 11.1 %collective-permute-start.15 = (bf16[256,256]{1,0:T(8,128)(2,1)S(1)}, bf16[256,256]{1,0:T(8,128)(2,1)S(1)}, u32[]{:S(2)}, u32[]{:S(2)}) collective-permute-start(bf16[256,256]{1,0:T(8,128)(2,1)S(1)} %get-tuple-element.20), channel_id=1, source_target_pairs={{0,10},{2,8},{4,14},{6,12},{8,2},{10,0},{12,6},{14,4},{1,11},{3,9}... | collective-permute-start | bytes 393224 | tf_op jit(solution)/shard_map/ppermute | solution.py:276
  63.1 11.2 %collective-permute-start.16 = (bf16[256,256]{1,0:T(8,128)(2,1)S(1)}, bf16[256,256]{1,0:T(8,128)(2,1)S(1)}, u32[]{:S(2)}, u32[]{:S(2)}) collective-permute-start(bf16[256,256]{1,0:T(8,128)(2,1)S(1)} %get-tuple-element.21), channel_id=1, source_target_pairs={{0,8},{2,10},{4,12},{6,14},{8,0},{10,2},{12,4},{14,6},{1,9},{3,11}... | collective-permute-start | bytes 393224 | tf_op jit(solution)/shard_map/ppermute | solution.py:276
  65.7 8.9 %collective-permute-start.17 = (bf16[256,256]{1,0:T(8,128)(2,1)S(1)}, bf16[256,256]{1,0:T(8,128)(2,1)S(1)}, u32[]{:S(2)}, u32[]{:S(2)}) collective-permute-start(bf16[256,256]{1,0:T(8,128)(2,1)S(1)} %get-tuple-element.22), channel_id=1, source_target_pairs={{0,6},{2,4},{4,10},{6,8},{8,14},{10,12},{12,2},{14,0},{1,7},{3,5},... | collective-permute-start | bytes 393224 | tf_op jit(solution)/shard_map/ppermute | solution.py:276
  68.6 8.5 %collective-permute-start.18 = (bf16[256,256]{1,0:T(8,128)(2,1)S(1)}, bf16[256,256]{1,0:T(8,128)(2,1)S(1)}, u32[]{:S(2)}, u32[]{:S(2)}) collective-permute-start(bf16[256,256]{1,0:T(8,128)(2,1)S(1)} %get-tuple-element.23), channel_id=1, source_target_pairs={{0,4},{2,6},{4,8},{6,10},{8,12},{10,14},{12,0},{14,2},{1,5},{3,7},... | collective-permute-start | bytes 393224 | tf_op jit(solution)/shard_map/ppermute | solution.py:276
  70.7 7.2 %collective-permute-start.19 = (bf16[256,256]{1,0:T(8,128)(2,1)S(1)}, bf16[256,256]{1,0:T(8,128)(2,1)S(1)}, u32[]{:S(2)}, u32[]{:S(2)}) collective-permute-start(bf16[256,256]{1,0:T(8,128)(2,1)S(1)} %get-tuple-element.24), channel_id=1, source_target_pairs={{0,14},{2,12},{4,2},{6,0},{8,6},{10,4},{12,10},{14,8},{1,15},{3,13... | collective-permute-start | bytes 393224 | tf_op jit(solution)/shard_map/ppermute | solution.py:276
  71.8 6.8 %collective-permute-start.20 = (bf16[256,256]{1,0:T(8,128)(2,1)S(1)}, bf16[256,256]{1,0:T(8,128)(2,1)S(1)}, u32[]{:S(2)}, u32[]{:S(2)}) collective-permute-start(bf16[256,256]{1,0:T(8,128)(2,1)S(1)} %get-tuple-element.25), channel_id=1, source_target_pairs={{0,12},{2,14},{4,0},{6,2},{8,4},{10,6},{12,8},{14,10},{1,13},{3,15... | collective-permute-start | bytes 393224 | tf_op jit(solution)/shard_map/ppermute | solution.py:276
  74.3 5.4 %collective-permute-start.21 = (bf16[256,256]{1,0:T(8,128)(2,1)S(1)}, bf16[256,256]{1,0:T(8,128)(2,1)S(1)}, u32[]{:S(2)}, u32[]{:S(2)}) collective-permute-start(bf16[256,256]{1,0:T(8,128)(2,1)S(1)} %get-tuple-element.26), channel_id=1, source_target_pairs={{0,2},{2,0},{4,6},{6,4},{8,10},{10,8},{12,14},{14,12},{1,3},{3,1},... | collective-permute-start | bytes 393224 | tf_op jit(solution)/shard_map/ppermute | solution.py:276
  79.9 15.2 %collective-permute-start.22 = (f32[256,256]{1,0:T(8,128)S(1)}, f32[256,256]{1,0:T(8,128)S(1)}, u32[]{:S(2)}, u32[]{:S(2)}) collective-permute-start(f32[256,256]{1,0:T(8,128)S(1)} %convert_add_fusion), channel_id=1, source_target_pairs={{0,0},{1,32},{2,16},{3,48},{16,1},{17,17},{18,33},{19,49},{32,2},{... | collective-permute-start | bytes 786440 | tf_op jit(solution)/shard_map/ppermute | solution.py:279

commit v5 on v3

--- a/solution.py
+++ b/solution.py
@@ -161,24 +161,24 @@
         fill(f1, 0, met, ls, 0, far, 0)
         fill(f3, 0, met, ls, 1, far, BS)
 
+    def product(h, swapped, block):
+        for q in range(4):
+            row = dy[q * ROWS : (q + 1) * ROWS, 0:USED]
+            pair = (block, row) if swapped else (row, block)
+            prod = lax.dot_general(*pair, (((1,), (1,)), ((), ())), preferred_element_type=F32)
+            out[q, h] = prod * factor
+
     for h in range(2):
         p = 2 * h + parity
 
-        def product(rhs):
-            for q in range(4):
-                lhs = dy[q * ROWS : (q + 1) * ROWS, 0:USED]
-                prod = lax.dot_general(
-                    lhs, rhs, (((1,), (1,)), ((), ())), preferred_element_type=F32
-                )
-                out[q, h] = prod * factor
-
         @pl.when(p == opposite)
         def _():
-            product(far[:, 0:USED])
+            product(h, True, far[:, 0:USED])
 
         @pl.when(p != opposite)
         def _():
-            product(dz[pl.ds(pl.multiple_of(p * ROWS, ROWS), ROWS), 0:USED])
+            at = pl.multiple_of(p * ROWS, ROWS)
+            product(h, False, dz[pl.ds(at, ROWS), 0:USED])
 
 
 def gram(flip, sc, dy, dz, met, f1, f3, small):
@@ -198,6 +198,21 @@
     )(sc, dy, dz, met, f1, f3, small)
 
 
+def hold_kernel(tiles, late, out):
+    out[...] = tiles[...]
+
+
+def hold(tiles, late):
+    return pl.pallas_call(
+        hold_kernel,
+        out_shape=jax.ShapeDtypeStruct(tiles.shape, tiles.dtype),
+        in_specs=[VMEM] * 2,
+        out_specs=VMEM,
+        compiler_params=PARAMS,
+        name="hold",
+    )(tiles, late)
+
+
 STEPS = tuple((k, w) for w in range(2) for k in range(4))
 
 
@@ -222,6 +237,15 @@
 
 def hop(k, w):
     return [(2 * a + b, 2 * ((a + k) % 4) + (b + w) % 2) for a in range(4) for b in range(2)]
+
+
+def homes():
+    moves = []
+    for n in range(256):
+        y, z, x, p = n // 64, n // 16 % 4, n // 4 % 4, n % 4
+        home = (x, z, y, p) if p == (z + 2) % 4 else (y, p, x, z)
+        moves.append((n, home[0] * 64 + home[1] * 16 + home[2] * 4 + home[3]))
+    return moves
 
 
 def local(fit_tiles, aux_list, aux_count, metric):
@@ -237,15 +261,14 @@
     f1 = lax.ppermute(z1[:HALF], "zh", ring(4, 1))
     f3 = lax.ppermute(z3[HALF:], "zh", ring(4, 3))
 
-    dy, dz, met = build(sc, ys, [z1, z3], parts, smalls)
+    dy, dz, met = build(sc, [hold(tiles, z3)] + ys[1:], [z1, z3], parts, smalls)
     send = gram(True, sc, dy, dz, met, f1, f3, smalls[2])
     got = lax.ppermute(send, "co", ring(2, 1))
     keep = gram(False, sc, dy, dz, met, f1, f3, smalls[2])
     total, *shares = share(sc, keep, got)
     for (k, w), piece in zip(STEPS[1:], shares):
         total = total + lax.ppermute(piece, ("x", "zl"), hop(k, w)).astype(F32)
-    swap = [(a * 4 + b, b * 4 + a) for a in range(4) for b in range(4)]
-    return lax.ppermute(total, ("zh", "zl", "co"), swap)
+    return lax.ppermute(total, ("y", "zh", "x", "zl", "co"), homes())
 
 
 def solution(mesh):

time: 98.3 us -> 97.1 us (0.988)
  the two profiles are of different devices: /device:TPU:40 before, /device:TPU:56 now
where the time goes in v5:
time: 97.1 us; the launch traced here: 96.9 us
  starting transfers between devices  48 us (49%)
  waiting for transfers between devices  34.5 us (36%)
  Pallas kernels  10.1 us (10%)
  local copies, waits for them, and re-layouts  3.97 us (4%)
    ppermute x7, waiting for transfers between devices, local(): total = total + lax.ppermute(piece, ('x', 'zl'), hop(k, w)).astype(F32)  12.3 us
    ppermute x1, waiting for transfers between devices, local(): return lax.ppermute(total, ('y', 'zh', 'x', 'zl', 'co'), homes())  10.6 us
    ppermute x3, starting transfers between devices, local(): ys = [tiles] + [lax.ppermute(tiles, 'y', ring(4, k)) for k in (1, 2, 3)]  10.4 us
    ppermute x3, starting transfers between devices, local(): lax.ppermute(small, 'zh', ring(4, k))  9.92 us
    ppermute x7, starting transfers between devices, local(): total = total + lax.ppermute(piece, ('x', 'zl'), hop(k, w)).astype(F32)  9.15 us
    pallas_call x2, Pallas kernels, gram(): pl.pallas_call(functools.partial(gram_kernel, flip), out_shape=jax.ShapeD...  6.27 us
    ppermute x3, waiting for transfers between devices, local(): lax.ppermute(small, 'zh', ring(4, k))  6.19 us
    ppermute x1, starting transfers between devices, local(): f1 = lax.ppermute(z1[:HALF], 'zh', ring(4, 1))  4.83 us
  transfers between devices with their start and end apart: 22, of which 13 were waited for; matrix products, arithmetic and copies ran while one was open for 1% of the time, Pallas kernels for 7%

profile of v5, /device:TPU:56, one launch (start us, length us, event | category | flops | bytes accessed | tf_op | source)
XLA Modules:
  0.0 96.9 jit_solution(4943381861798138134)
XLA Ops:
  0.0 3.3 %collective-permute-start.4 = (bf16[1536,128]{1,0:T(8,128)(2,1)}, bf16[1536,128]{1,0:T(8,128)(2,1)S(1)}, u32[]{:S(2)}, u32[]{:S(2)}) collective-permute-start(bf16[1536,128]{1,0:T(8,128)(2,1)} %bitcast.7), channel_id=1, source_target_pairs={{0,16},{16,32},{32,48},{48,0},{1,17},{17,33},{33,49},{49,1},{2,18}... | collective-permute-start | bytes 1179656 | tf_op jit(solution)/shard_map/ppermute | solution.py:256
  3.3 2.1 %collective-permute-start = (bf16[1536,128]{1,0:T(8,128)(2,1)}, bf16[1536,128]{1,0:T(8,128)(2,1)S(1)}, u32[]{:S(2)}, u32[]{:S(2)}) collective-permute-start(bf16[1536,128]{1,0:T(8,128)(2,1)} %bitcast.8), channel_id=1, source_target_pairs={{0,48},{16,0},{32,16},{48,32},{1,49},{17,1},{33,17},{49,33},{2,50}... | collective-permute-start | bytes 1179656 | tf_op jit(solution)/shard_map/ppermute | solution.py:257
  5.4 0.7 copy.5.counts
  7.6 0.8 collective-permute-start.7
  8.4 0.9 collective-permute-start.6
  9.3 2.2 %collective-permute-start.5 = (bf16[104,128]{1,0:T(8,128)(2,1)S(1)}, bf16[104,128]{1,0:T(8,128)(2,1)S(1)}, u32[]{:S(2)}, u32[]{:S(2)}) collective-permute-start(bf16[104,128]{1,0:T(8,128)(2,1)S(1)} %pack.1.m0.p0), channel_id=1, source_target_pairs={{0,64},{64,128},{128,192},{192,0},{1,65},{65,129},{129,193},{193,1... | collective-permute-start | bytes 79880 | tf_op jit(solution)/shard_map/ppermute | solution.py:254
  11.6 1.1 %collective-permute-done.7.m3.p3 = bf16[104,128]{1,0:T(8,128)(2,1)S(1)} collective-permute-done((bf16[104,128]{1,0:T(8,128)(2,1)S(1)}, bf16[104,128]{1,0:T(8,128)(2,1)S(1)}, u32[]{:S(2)}, u32[]{:S(2)}) %collective-permute-start.7) | collective-permute-done | bytes 26656 | tf_op jit(solution)/shard_map/ppermute | solution.py:254
  12.7 1.0 %collective-permute-done.6.m2.p2 = bf16[104,128]{1,0:T(8,128)(2,1)S(1)} collective-permute-done((bf16[104,128]{1,0:T(8,128)(2,1)S(1)}, bf16[104,128]{1,0:T(8,128)(2,1)S(1)}, u32[]{:S(2)}, u32[]{:S(2)}) %collective-permute-start.6) | collective-permute-done | bytes 26656 | tf_op jit(solution)/shard_map/ppermute | solution.py:254
  14.4 3.0 %collective-permute-start.10 = (bf16[400,128]{1,0:T(8,128)(2,1)S(1)}, bf16[400,128]{1,0:T(8,128)(2,1)S(1)}, u32[]{:S(2)}, u32[]{:S(2)}) collective-permute-start(bf16[400,128]{1,0:T(8,128)(2,1)S(1)} %line.1.s0), channel_id=1, source_target_pairs={{0,48},{16,0},{32,16},{48,32},{1,49},{17,1},{33,17},{49,33},{2,50}... | collective-permute-start | bytes 307208 | tf_op jit(solution)/shard_map/ppermute | solution.py:260
  17.4 1.7 %collective-permute-start.3 = (bf16[1536,128]{1,0:T(8,128)(2,1)}, bf16[1536,128]{1,0:T(8,128)(2,1)S(1)}, u32[]{:S(2)}, u32[]{:S(2)}) collective-permute-start(bf16[1536,128]{1,0:T(8,128)(2,1)} %bitcast.9), channel_id=1, source_target_pairs={{0,192},{64,0},{128,64},{192,128},{1,193},{65,1},{129,65},{193,129... | collective-permute-start | bytes 1179656 | tf_op jit(solution)/shard_map/ppermute | solution.py:258
  19.2 2.4 %collective-permute-start.2 = (bf16[1536,128]{1,0:T(8,128)(2,1)}, bf16[1536,128]{1,0:T(8,128)(2,1)S(1)}, u32[]{:S(2)}, u32[]{:S(2)}) collective-permute-start(bf16[1536,128]{1,0:T(8,128)(2,1)} %bitcast.10), channel_id=1, source_target_pairs={{0,128},{64,192},{128,0},{192,64},{1,129},{65,193},{129,1},{193,65... | collective-permute-start | bytes 1179656 | tf_op jit(solution)/shard_map/ppermute | solution.py:258
  21.8 6.2 %collective-permute-start.1 = (bf16[1536,128]{1,0:T(8,128)(2,1)}, bf16[1536,128]{1,0:T(8,128)(2,1)S(1)}, u32[]{:S(2)}, u32[]{:S(2)}) collective-permute-start(bf16[1536,128]{1,0:T(8,128)(2,1)} %bitcast.11), channel_id=1, source_target_pairs={{0,64},{64,128},{128,192},{192,0},{1,65},{65,129},{129,193},{193,1... | collective-permute-start | bytes 1179656 | tf_op jit(solution)/shard_map/ppermute | solution.py:258
  28.0 4.9 %collective-permute-start.9 = (bf16[400,128]{1,0:T(8,128)(2,1)S(1)}, bf16[400,128]{1,0:T(8,128)(2,1)S(1)}, u32[]{:S(2)}, u32[]{:S(2)}) collective-permute-start(bf16[400,128]{1,0:T(8,128)(2,1)S(1)} %line.1.s0), channel_id=1, source_target_pairs={{0,32},{16,48},{32,0},{48,16},{1,33},{17,49},{33,1},{49,17},{2,34}... | collective-permute-start | bytes 307208 | tf_op jit(solution)/shard_map/ppermute | solution.py:260
  33.0 2.0 %collective-permute-start.8 = (bf16[400,128]{1,0:T(8,128)(2,1)S(1)}, bf16[400,128]{1,0:T(8,128)(2,1)S(1)}, u32[]{:S(2)}, u32[]{:S(2)}) collective-permute-start(bf16[400,128]{1,0:T(8,128)(2,1)S(1)} %line.1.s0), channel_id=1, source_target_pairs={{0,16},{16,32},{32,48},{48,0},{1,17},{17,33},{33,49},{49,1},{2,18}... | collective-permute-start | bytes 307208 | tf_op jit(solution)/shard_map/ppermute | solution.py:260
  35.0 2.8 %collective-permute-done.9.s2 = bf16[400,128]{1,0:T(8,128)(2,1)S(1)} collective-permute-done((bf16[400,128]{1,0:T(8,128)(2,1)S(1)}, bf16[400,128]{1,0:T(8,128)(2,1)S(1)}, u32[]{:S(2)}, u32[]{:S(2)}) %collective-permute-start.9) | collective-permute-done | bytes 102432 | tf_op jit(solution)/shard_map/ppermute | solution.py:260
  37.8 4.8 %collective-permute-start.11 = (bf16[768,128]{1,0:T(8,128)(2,1)S(1)}, bf16[768,128]{1,0:T(8,128)(2,1)S(1)}, u32[]{:S(2)}, u32[]{:S(2)}) collective-permute-start(bf16[768,128]{1,0:T(8,128)(2,1)S(1)} %slice.8), channel_id=1, source_target_pairs={{0,16},{16,32},{32,48},{48,0},{1,17},{17,33},{33,49},{49,1},{2,18}... | collective-permute-start | bytes 589832 | tf_op jit(solution)/shard_map/ppermute | solution.py:261
  42.6 3.2 %collective-permute-done.8.s1 = bf16[400,128]{1,0:T(8,128)(2,1)S(1)} collective-permute-done((bf16[400,128]{1,0:T(8,128)(2,1)S(1)}, bf16[400,128]{1,0:T(8,128)(2,1)S(1)}, u32[]{:S(2)}, u32[]{:S(2)}) %collective-permute-start.8) | collective-permute-done | bytes 102432 | tf_op jit(solution)/shard_map/ppermute | solution.py:260
  46.4 1.0 %copy-done = bf16[2,6,128,128]{3,2,1,0:T(8,128)(2,1)S(1)} copy-done((bf16[2,6,128,128]{3,2,1,0:T(8,128)(2,1)S(1)}, bf16[2,6,128,128]{3,2,1,0:T(8,128)(2,1)}, u32[]{:S(2)}) %copy-start) | copy-done | bytes 393240
  47.4 2.4 %build.1 = (bf16[1024,1664]{1,0:T(8,128)(2,1)S(1)}, bf16[1024,1664]{1,0:T(8,128)(2,1)S(1)}, bf16[13,128,128]{2,1,0:T(8,128)(2,1)S(1)}) custom-call(s32[5]{0:T(128)S(1)} %stack.23.sc_ref, bf16[1536,128]{1,0:T(8,128)(2,1)S(1)} %hold.1.t0, bf16[1536,128]{1,0:T(8,128)(2,1)S(1)} %collective-permute-done.1.t1, bf16[1536,128]{1,0:T(8,128)(2,1)S(1)} %collective-permute-done.2.t2, ...), custom_call_target="tpu_custom_call" | custom-call | tf_op jit(solution)/shard_map/build/pallas_call | solution.py:133
  50.0 2.4 %collective-permute-done.12.f3 = bf16[768,128]{1,0:T(8,128)(2,1)S(1)} collective-permute-done((bf16[768,128]{1,0:T(8,128)(2,1)S(1)}, bf16[768,128]{1,0:T(8,128)(2,1)S(1)}, u32[]{:S(2)}, u32[]{:S(2)}) %collective-permute-start.12) | collective-permute-done | bytes 196640 | tf_op jit(solution)/shard_map/ppermute | solution.py:262
  52.4 2.8 %send.1 = f32[4,2,256,256]{3,2,1,0:T(8,128)S(1)} custom-call(s32[5]{0:T(128)S(1)} %stack.23.sc_ref, bf16[1024,1664]{1,0:T(8,128)(2,1)S(1)} %get-tuple-element.16.dy, bf16[1024,1664]{1,0:T(8,128)(2,1)S(1)} %get-tuple-element.17.dz, bf16[13,128,128]{2,1,0:T(8,128)(2,1)S(1)} %get-tuple-element.18.met, bf16[768,128]{1,0:T(8,128)(2,1)S(1)} %collective-permute-done.11.f1, ...), custom_call_target="tpu_custom_call" | custom-call | tf_op jit(solution)/shard_map/send/pallas_call | solution.py:185
  55.3 3.5 %keep.1 = f32[4,2,256,256]{3,2,1,0:T(8,128)S(1)} custom-call(s32[5]{0:T(128)S(1)} %stack.23.sc_ref, bf16[1024,1664]{1,0:T(8,128)(2,1)S(1)} %get-tuple-element.16.dy, bf16[1024,1664]{1,0:T(8,128)(2,1)S(1)} %get-tuple-element.17.dz, bf16[13,128,128]{2,1,0:T(8,128)(2,1)S(1)} %get-tuple-element.18.met, bf16[768,128]{1,0:T(8,128)(2,1)S(1)} %collective-permute-done.11.f1, ...), custom_call_target="tpu_custom_call" | custom-call | tf_op jit(solution)/shard_map/keep/pallas_call | solution.py:185
  60.2 1.6 %collective-permute-start.14 = (bf16[256,256]{1,0:T(8,128)(2,1)S(1)}, bf16[256,256]{1,0:T(8,128)(2,1)S(1)}, u32[]{:S(2)}, u32[]{:S(2)}) collective-permute-start(bf16[256,256]{1,0:T(8,128)(2,1)S(1)} %get-tuple-element.20), channel_id=1, source_target_pairs={{0,4},{2,6},{4,8},{6,10},{8,12},{10,14},{12,0},{14,2},{1,5},{3,7},... | collective-permute-start | bytes 393224 | tf_op jit(solution)/shard_map/ppermute | solution.py:270
  61.7 2.7 %collective-permute-start.15 = (bf16[256,256]{1,0:T(8,128)(2,1)S(1)}, bf16[256,256]{1,0:T(8,128)(2,1)S(1)}, u32[]{:S(2)}, u32[]{:S(2)}) collective-permute-start(bf16[256,256]{1,0:T(8,128)(2,1)S(1)} %get-tuple-element.21), channel_id=1, source_target_pairs={{0,8},{2,10},{4,12},{6,14},{8,0},{10,2},{12,4},{14,6},{1,9},{3,11}... | collective-permute-start | bytes 393224 | tf_op jit(solution)/shard_map/ppermute | solution.py:270
  64.5 1.4 %collective-permute-start.16 = (bf16[256,256]{1,0:T(8,128)(2,1)S(1)}, bf16[256,256]{1,0:T(8,128)(2,1)S(1)}, u32[]{:S(2)}, u32[]{:S(2)}) collective-permute-start(bf16[256,256]{1,0:T(8,128)(2,1)S(1)} %get-tuple-element.22), channel_id=1, source_target_pairs={{0,12},{2,14},{4,0},{6,2},{8,4},{10,6},{12,8},{14,10},{1,13},{3,15... | collective-permute-start | bytes 393224 | tf_op jit(solution)/shard_map/ppermute | solution.py:270
  66.6 1.4 %collective-permute-start.18 = (bf16[256,256]{1,0:T(8,128)(2,1)S(1)}, bf16[256,256]{1,0:T(8,128)(2,1)S(1)}, u32[]{:S(2)}, u32[]{:S(2)}) collective-permute-start(bf16[256,256]{1,0:T(8,128)(2,1)S(1)} %get-tuple-element.24), channel_id=1, source_target_pairs={{0,6},{2,4},{4,10},{6,8},{8,14},{10,12},{12,2},{14,0},{1,7},{3,5},... | collective-permute-start | bytes 393224 | tf_op jit(solution)/shard_map/ppermute | solution.py:270
  68.0 1.4 %collective-permute-start.19 = (bf16[256,256]{1,0:T(8,128)(2,1)S(1)}, bf16[256,256]{1,0:T(8,128)(2,1)S(1)}, u32[]{:S(2)}, u32[]{:S(2)}) collective-permute-start(bf16[256,256]{1,0:T(8,128)(2,1)S(1)} %get-tuple-element.25), channel_id=1, source_target_pairs={{0,10},{2,8},{4,14},{6,12},{8,2},{10,0},{12,6},{14,4},{1,11},{3,9}... | collective-permute-start | bytes 393224 | tf_op jit(solution)/shard_map/ppermute | solution.py:270
  69.3 6.5 %collective-permute-done.15 = bf16[256,256]{1,0:T(8,128)(2,1)S(1)} collective-permute-done((bf16[256,256]{1,0:T(8,128)(2,1)S(1)}, bf16[256,256]{1,0:T(8,128)(2,1)S(1)}, u32[]{:S(2)}, u32[]{:S(2)}) %collective-permute-start.15) | collective-permute-done | bytes 131104 | tf_op jit(solution)/shard_map/ppermute | solution.py:270
  75.8 1.8 %collective-permute-done.19 = bf16[256,256]{1,0:T(8,128)(2,1)S(1)} collective-permute-done((bf16[256,256]{1,0:T(8,128)(2,1)S(1)}, bf16[256,256]{1,0:T(8,128)(2,1)S(1)}, u32[]{:S(2)}, u32[]{:S(2)}) %collective-permute-start.19) | collective-permute-done | bytes 131104 | tf_op jit(solution)/shard_map/ppermute | solution.py:270
  77.6 4.0 %collective-permute-done.20 = bf16[256,256]{1,0:T(8,128)(2,1)S(1)} collective-permute-done((bf16[256,256]{1,0:T(8,128)(2,1)S(1)}, bf16[256,256]{1,0:T(8,128)(2,1)S(1)}, u32[]{:S(2)}, u32[]{:S(2)}) %collective-permute-start.20) | collective-permute-done | bytes 131104 | tf_op jit(solution)/shard_map/ppermute | solution.py:270
  81.8 3.8 %collective-permute-start.21 = (f32[256,256]{1,0:T(8,128)S(1)}, f32[256,256]{1,0:T(8,128)S(1)}, u32[]{:S(2)}, u32[]{:S(2)}) collective-permute-start(f32[256,256]{1,0:T(8,128)S(1)} %convert_add_fusion), channel_id=1, source_target_pairs={{0,0},{1,16},{2,2},{3,48},{4,4},{5,20},{6,66},{7,52},{8,8},{9,24},... | collective-permute-start | bytes 786440 | tf_op jit(solution)/shard_map/ppermute | solution.py:271
  85.6 10.6 %collective-permute-done.21 = f32[256,256]{1,0:T(8,128)S(1)} collective-permute-done((f32[256,256]{1,0:T(8,128)S(1)}, f32[256,256]{1,0:T(8,128)S(1)}, u32[]{:S(2)}, u32[]{:S(2)}) %collective-permute-start.21) | collective-permute-done | bytes 262176 | tf_op jit(solution)/shard_map/ppermute | solution.py:271
  (31 shorter events, 6.2 us)
Async XLA Ops:
  0.0 28.0 %collective-permute-start.4 = (bf16[1536,128]{1,0:T(8,128)(2,1)}, bf16[1536,128]{1,0:T(8,128)(2,1)S(1)}, u32[]{:S(2)}, u32[]{:S(2)}) collective-permute-start(bf16[1536,128]{1,0:T(8,128)(2,1)} %bitcast.7), channel_id=1, source_target_pairs={{0,16},{16,32},{32,48},{48,0},{1,17},{17,33},{33,49},{49,1},{2,18}... | collective-permute-start | bytes 1179656 | tf_op jit(solution)/shard_map/ppermute | solution.py:256
  3.3 29.7 %collective-permute-start = (bf16[1536,128]{1,0:T(8,128)(2,1)}, bf16[1536,128]{1,0:T(8,128)(2,1)S(1)}, u32[]{:S(2)}, u32[]{:S(2)}) collective-permute-start(bf16[1536,128]{1,0:T(8,128)(2,1)} %bitcast.8), channel_id=1, source_target_pairs={{0,48},{16,0},{32,16},{48,32},{1,49},{17,1},{33,17},{49,33},{2,50}... | collective-permute-start | bytes 1179656 | tf_op jit(solution)/shard_map/ppermute | solution.py:257
  6.1 0.7 copy-start.1
  6.9 0.7 copy-start.2
  7.6 5.1 %collective-permute-start.7 = (bf16[104,128]{1,0:T(8,128)(2,1)S(1)}, bf16[104,128]{1,0:T(8,128)(2,1)S(1)}, u32[]{:S(2)}, u32[]{:S(2)}) collective-permute-start(bf16[104,128]{1,0:T(8,128)(2,1)S(1)} %pack.1.m0.p0), channel_id=1, source_target_pairs={{0,192},{64,0},{128,64},{192,128},{1,193},{65,1},{129,65},{193,129... | collective-permute-start | bytes 79880 | tf_op jit(solution)/shard_map/ppermute | solution.py:254
  8.4 5.4 %collective-permute-start.6 = (bf16[104,128]{1,0:T(8,128)(2,1)S(1)}, bf16[104,128]{1,0:T(8,128)(2,1)S(1)}, u32[]{:S(2)}, u32[]{:S(2)}) collective-permute-start(bf16[104,128]{1,0:T(8,128)(2,1)S(1)} %pack.1.m0.p0), channel_id=1, source_target_pairs={{0,128},{64,192},{128,0},{192,64},{1,129},{65,193},{129,1},{193,65... | collective-permute-start | bytes 79880 | tf_op jit(solution)/shard_map/ppermute | solution.py:254
  9.3 4.5 %collective-permute-start.5 = (bf16[104,128]{1,0:T(8,128)(2,1)S(1)}, bf16[104,128]{1,0:T(8,128)(2,1)S(1)}, u32[]{:S(2)}, u32[]{:S(2)}) collective-permute-start(bf16[104,128]{1,0:T(8,128)(2,1)S(1)} %pack.1.m0.p0), channel_id=1, source_target_pairs={{0,64},{64,128},{128,192},{192,0},{1,65},{65,129},{129,193},{193,1... | collective-permute-start | bytes 79880 | tf_op jit(solution)/shard_map/ppermute | solution.py:254
  14.4 7.4 %collective-permute-start.10 = (bf16[400,128]{1,0:T(8,128)(2,1)S(1)}, bf16[400,128]{1,0:T(8,128)(2,1)S(1)}, u32[]{:S(2)}, u32[]{:S(2)}) collective-permute-start(bf16[400,128]{1,0:T(8,128)(2,1)S(1)} %line.1.s0), channel_id=1, source_target_pairs={{0,48},{16,0},{32,16},{48,32},{1,49},{17,1},{33,17},{49,33},{2,50}... | collective-permute-start | bytes 307208 | tf_op jit(solution)/shard_map/ppermute | solution.py:260
  17.4 30.0 %collective-permute-start.3 = (bf16[1536,128]{1,0:T(8,128)(2,1)}, bf16[1536,128]{1,0:T(8,128)(2,1)S(1)}, u32[]{:S(2)}, u32[]{:S(2)}) collective-permute-start(bf16[1536,128]{1,0:T(8,128)(2,1)} %bitcast.9), channel_id=1, source_target_pairs={{0,192},{64,0},{128,64},{192,128},{1,193},{65,1},{129,65},{193,129... | collective-permute-start | bytes 1179656 | tf_op jit(solution)/shard_map/ppermute | solution.py:258
  19.2 28.2 %collective-permute-start.2 = (bf16[1536,128]{1,0:T(8,128)(2,1)}, bf16[1536,128]{1,0:T(8,128)(2,1)S(1)}, u32[]{:S(2)}, u32[]{:S(2)}) collective-permute-start(bf16[1536,128]{1,0:T(8,128)(2,1)} %bitcast.10), channel_id=1, source_target_pairs={{0,128},{64,192},{128,0},{192,64},{1,129},{65,193},{129,1},{193,65... | collective-permute-start | bytes 1179656 | tf_op jit(solution)/shard_map/ppermute | solution.py:258
  21.8 25.6 %collective-permute-start.1 = (bf16[1536,128]{1,0:T(8,128)(2,1)}, bf16[1536,128]{1,0:T(8,128)(2,1)S(1)}, u32[]{:S(2)}, u32[]{:S(2)}) collective-permute-start(bf16[1536,128]{1,0:T(8,128)(2,1)} %bitcast.11), channel_id=1, source_target_pairs={{0,64},{64,128},{128,192},{192,0},{1,65},{65,129},{129,193},{193,1... | collective-permute-start | bytes 1179656 | tf_op jit(solution)/shard_map/ppermute | solution.py:258
  28.0 9.8 %collective-permute-start.9 = (bf16[400,128]{1,0:T(8,128)(2,1)S(1)}, bf16[400,128]{1,0:T(8,128)(2,1)S(1)}, u32[]{:S(2)}, u32[]{:S(2)}) collective-permute-start(bf16[400,128]{1,0:T(8,128)(2,1)S(1)} %line.1.s0), channel_id=1, source_target_pairs={{0,32},{16,48},{32,0},{48,16},{1,33},{17,49},{33,1},{49,17},{2,34}... | collective-permute-start | bytes 307208 | tf_op jit(solution)/shard_map/ppermute | solution.py:260
  33.0 12.9 %collective-permute-start.8 = (bf16[400,128]{1,0:T(8,128)(2,1)S(1)}, bf16[400,128]{1,0:T(8,128)(2,1)S(1)}, u32[]{:S(2)}, u32[]{:S(2)}) collective-permute-start(bf16[400,128]{1,0:T(8,128)(2,1)S(1)} %line.1.s0), channel_id=1, source_target_pairs={{0,16},{16,32},{32,48},{48,0},{1,17},{17,33},{33,49},{49,1},{2,18}... | collective-permute-start | bytes 307208 | tf_op jit(solution)/shard_map/ppermute | solution.py:260
  37.8 12.2 %collective-permute-start.11 = (bf16[768,128]{1,0:T(8,128)(2,1)S(1)}, bf16[768,128]{1,0:T(8,128)(2,1)S(1)}, u32[]{:S(2)}, u32[]{:S(2)}) collective-permute-start(bf16[768,128]{1,0:T(8,128)(2,1)S(1)} %slice.8), channel_id=1, source_target_pairs={{0,16},{16,32},{32,48},{48,0},{1,17},{17,33},{33,49},{49,1},{2,18}... | collective-permute-start | bytes 589832 | tf_op jit(solution)/shard_map/ppermute | solution.py:261
  45.8 6.6 %collective-permute-start.12 = (bf16[768,128]{1,0:T(8,128)(2,1)S(1)}, bf16[768,128]{1,0:T(8,128)(2,1)S(1)}, u32[]{:S(2)}, u32[]{:S(2)}) collective-permute-start(bf16[768,128]{1,0:T(8,128)(2,1)S(1)} %slice.9), channel_id=1, source_target_pairs={{0,48},{16,0},{32,16},{48,32},{1,49},{17,1},{33,17},{49,33},{2,50}... | collective-permute-start | bytes 589832 | tf_op jit(solution)/shard_map/ppermute | solution.py:262
  46.4 1.0 %copy-start = (bf16[2,6,128,128]{3,2,1,0:T(8,128)(2,1)S(1)}, bf16[2,6,128,128]{3,2,1,0:T(8,128)(2,1)}, u32[]{:S(2)}) copy-start(bf16[2,6,128,128]{3,2,1,0:T(8,128)(2,1)} %param.4) | copy-start | bytes 1179652
  55.2 4.2 %collective-permute-start.13 = (f32[4,2,256,256]{3,2,1,0:T(8,128)S(1)}, f32[4,2,256,256]{3,2,1,0:T(8,128)S(1)}, u32[]{:S(2)}, u32[]{:S(2)}) collective-permute-start(f32[4,2,256,256]{3,2,1,0:T(8,128)S(1)} %send.1), channel_id=1, source_target_pairs={{0,1},{1,0},{2,3},{3,2},{4,5},{5,4},{6,7},{7,6},{8,9},{9,8},{10,11... | collective-permute-start | bytes 6291464 | tf_op jit(solution)/shard_map/ppermute | solution.py:266
  60.2 7.8 %collective-permute-start.14 = (bf16[256,256]{1,0:T(8,128)(2,1)S(1)}, bf16[256,256]{1,0:T(8,128)(2,1)S(1)}, u32[]{:S(2)}, u32[]{:S(2)}) collective-permute-start(bf16[256,256]{1,0:T(8,128)(2,1)S(1)} %get-tuple-element.20), channel_id=1, source_target_pairs={{0,4},{2,6},{4,8},{6,10},{8,12},{10,14},{12,0},{14,2},{1,5},{3,7},... | collective-permute-start | bytes 393224 | tf_op jit(solution)/shard_map/ppermute | solution.py:270
  61.7 14.0 %collective-permute-start.15 = (bf16[256,256]{1,0:T(8,128)(2,1)S(1)}, bf16[256,256]{1,0:T(8,128)(2,1)S(1)}, u32[]{:S(2)}, u32[]{:S(2)}) collective-permute-start(bf16[256,256]{1,0:T(8,128)(2,1)S(1)} %get-tuple-element.21), channel_id=1, source_target_pairs={{0,8},{2,10},{4,12},{6,14},{8,0},{10,2},{12,4},{14,6},{1,9},{3,11}... | collective-permute-start | bytes 393224 | tf_op jit(solution)/shard_map/ppermute | solution.py:270
  64.5 11.3 %collective-permute-start.16 = (bf16[256,256]{1,0:T(8,128)(2,1)S(1)}, bf16[256,256]{1,0:T(8,128)(2,1)S(1)}, u32[]{:S(2)}, u32[]{:S(2)}) collective-permute-start(bf16[256,256]{1,0:T(8,128)(2,1)S(1)} %get-tuple-element.22), channel_id=1, source_target_pairs={{0,12},{2,14},{4,0},{6,2},{8,4},{10,6},{12,8},{14,10},{1,13},{3,15... | collective-permute-start | bytes 393224 | tf_op jit(solution)/shard_map/ppermute | solution.py:270
  65.9 9.9 %collective-permute-start.17 = (bf16[256,256]{1,0:T(8,128)(2,1)S(1)}, bf16[256,256]{1,0:T(8,128)(2,1)S(1)}, u32[]{:S(2)}, u32[]{:S(2)}) collective-permute-start(bf16[256,256]{1,0:T(8,128)(2,1)S(1)} %get-tuple-element.23), channel_id=1, source_target_pairs={{0,2},{2,0},{4,6},{6,4},{8,10},{10,8},{12,14},{14,12},{1,3},{3,1},... | collective-permute-start | bytes 393224 | tf_op jit(solution)/shard_map/ppermute | solution.py:270
  66.6 9.2 %collective-permute-start.18 = (bf16[256,256]{1,0:T(8,128)(2,1)S(1)}, bf16[256,256]{1,0:T(8,128)(2,1)S(1)}, u32[]{:S(2)}, u32[]{:S(2)}) collective-permute-start(bf16[256,256]{1,0:T(8,128)(2,1)S(1)} %get-tuple-element.24), channel_id=1, source_target_pairs={{0,6},{2,4},{4,10},{6,8},{8,14},{10,12},{12,2},{14,0},{1,7},{3,5},... | collective-permute-start | bytes 393224 | tf_op jit(solution)/shard_map/ppermute | solution.py:270
  68.0 9.6 %collective-permute-start.19 = (bf16[256,256]{1,0:T(8,128)(2,1)S(1)}, bf16[256,256]{1,0:T(8,128)(2,1)S(1)}, u32[]{:S(2)}, u32[]{:S(2)}) collective-permute-start(bf16[256,256]{1,0:T(8,128)(2,1)S(1)} %get-tuple-element.25), channel_id=1, source_target_pairs={{0,10},{2,8},{4,14},{6,12},{8,2},{10,0},{12,6},{14,4},{1,11},{3,9}... | collective-permute-start | bytes 393224 | tf_op jit(solution)/shard_map/ppermute | solution.py:270
  75.8 5.9 %collective-permute-start.20 = (bf16[256,256]{1,0:T(8,128)(2,1)S(1)}, bf16[256,256]{1,0:T(8,128)(2,1)S(1)}, u32[]{:S(2)}, u32[]{:S(2)}) collective-permute-start(bf16[256,256]{1,0:T(8,128)(2,1)S(1)} %get-tuple-element.26), channel_id=1, source_target_pairs={{0,14},{2,12},{4,2},{6,0},{8,6},{10,4},{12,10},{14,8},{1,15},{3,13... | collective-permute-start | bytes 393224 | tf_op jit(solution)/shard_map/ppermute | solution.py:270
  81.8 14.4 %collective-permute-start.21 = (f32[256,256]{1,0:T(8,128)S(1)}, f32[256,256]{1,0:T(8,128)S(1)}, u32[]{:S(2)}, u32[]{:S(2)}) collective-permute-start(f32[256,256]{1,0:T(8,128)S(1)} %convert_add_fusion), channel_id=1, source_target_pairs={{0,0},{1,16},{2,2},{3,48},{4,4},{5,20},{6,66},{7,52},{8,8},{9,24},... | collective-permute-start | bytes 786440 | tf_op jit(solution)/shard_map/ppermute | solution.py:271

commit v6 on v5

--- a/solution.py
+++ b/solution.py
@@ -1,5 +1,3 @@
-import functools
-
 import jax
 import jax.numpy as jnp
 from jax import lax
@@ -145,57 +143,100 @@
     )(sc, *tiles, *zs, *parts, *smalls)
 
 
-def gram_kernel(flip, sc_ref, dy, dz, met, f1, f3, s2, out, far, lv, ls, sem):
+FACTOR = 1.0 / (QS * 16 * AUXB) ** 0.5
+
+
+def early(zh, core):
+    opposite = back(zh, 2)
+    return jnp.where(lax.rem(zh, 2) == core, 1 - opposite // 2, 0)
+
+
+def product(out, dy, block, swapped):
+    for q in range(4):
+        row = dy[q * ROWS : (q + 1) * ROWS, 0:USED]
+        pair = (block, row) if swapped else (row, block)
+        prod = lax.dot_general(*pair, (((1,), (1,)), ((), ())), preferred_element_type=F32)
+        out[q] = prod * FACTOR
+
+
+def near_product(out, dy, dz, h, core):
+    at = pl.multiple_of((2 * h + core) * ROWS, ROWS)
+    product(out, dy, dz[pl.ds(at, ROWS), 0:USED], False)
+
+
+def first_kernel(sc_ref, dy, dz, send_e):
+    zh, other = sc_ref[1], 1 - sc_ref[2]
+    near_product(send_e, dy, dz, early(zh, other), other)
+
+
+def near_kernel(sc_ref, dy, dz, keep_e, send_l, keep_l):
     zh, co = sc_ref[1], sc_ref[2]
-    parity = 1 - co if flip else co
-    opposite = back(zh, 2)
-    factor = 1.0 / (QS * 16 * AUXB) ** 0.5
-
-    @pl.when(lax.rem(zh, 2) == parity)
+    near_product(keep_e, dy, dz, early(zh, co), co)
+    mine = lax.rem(zh, 2) == co
+
+    @pl.when(mine)
     def _():
-        lv[...] = read_lists(s2, LIST0)
-        copy = pltpu.make_async_copy(lv, ls, sem)
-        copy.start()
-        far[...] = jnp.zeros_like(far)
-        copy.wait()
-        fill(f1, 0, met, ls, 0, far, 0)
-        fill(f3, 0, met, ls, 1, far, BS)
-
-    def product(h, swapped, block):
-        for q in range(4):
-            row = dy[q * ROWS : (q + 1) * ROWS, 0:USED]
-            pair = (block, row) if swapped else (row, block)
-            prod = lax.dot_general(*pair, (((1,), (1,)), ((), ())), preferred_element_type=F32)
-            out[q, h] = prod * factor
-
-    for h in range(2):
-        p = 2 * h + parity
-
-        @pl.when(p == opposite)
-        def _():
-            product(h, True, far[:, 0:USED])
-
-        @pl.when(p != opposite)
-        def _():
-            at = pl.multiple_of(p * ROWS, ROWS)
-            product(h, False, dz[pl.ds(at, ROWS), 0:USED])
-
-
-def gram(flip, sc, dy, dz, met, f1, f3, small):
-    return pl.pallas_call(
-        functools.partial(gram_kernel, flip),
-        out_shape=jax.ShapeDtypeStruct((4, 2, ROWS, ROWS), F32),
-        in_specs=[SMEM] + [VMEM] * 6,
+        near_product(send_l, dy, dz, 1 - early(zh, 1 - co), 1 - co)
+
+    @pl.when(jnp.logical_not(mine))
+    def _():
+        near_product(keep_l, dy, dz, 1 - early(zh, co), co)
+
+
+def far_kernel(sc_ref, dy, met, f1, f3, s2, send_in, keep_in, send_l, keep_l, far, lv, ls, sem):
+    lv[...] = read_lists(s2, LIST0)
+    copy = pltpu.make_async_copy(lv, ls, sem)
+    copy.start()
+    far[...] = jnp.zeros_like(far)
+    copy.wait()
+    fill(f1, 0, met, ls, 0, far, 0)
+    fill(f3, 0, met, ls, 1, far, BS)
+    mine = lax.rem(sc_ref[1], 2) == sc_ref[2]
+    pl.when(mine)(lambda: product(keep_l, dy, far[:, 0:USED], True))
+    pl.when(jnp.logical_not(mine))(lambda: product(send_l, dy, far[:, 0:USED], True))
+
+
+ROW = jax.ShapeDtypeStruct((4, ROWS, ROWS), F32)
+
+
+def first_row(sc, dy, dz):
+    return pl.pallas_call(
+        first_kernel,
+        out_shape=ROW,
+        in_specs=[SMEM, VMEM, VMEM],
         out_specs=VMEM,
+        compiler_params=PARAMS,
+        name="first",
+    )(sc, dy, dz)
+
+
+def near_rows(sc, dy, dz):
+    return pl.pallas_call(
+        near_kernel,
+        out_shape=(ROW,) * 3,
+        in_specs=[SMEM, VMEM, VMEM],
+        out_specs=(VMEM,) * 3,
+        compiler_params=PARAMS,
+        name="near",
+    )(sc, dy, dz)
+
+
+def far_row(sc, dy, met, f1, f3, small, send_l, keep_l):
+    return pl.pallas_call(
+        far_kernel,
+        out_shape=(ROW,) * 2,
+        in_specs=[SMEM] + [VMEM] * 7,
+        out_specs=(VMEM,) * 2,
         scratch_shapes=[
             pltpu.VMEM((ROWS, WIDE), BF16),
             pltpu.VMEM((8, 128), jnp.int32),
             pltpu.SMEM((8, 128), jnp.int32),
             pltpu.SemaphoreType.DMA,
         ],
-        compiler_params=PARAMS,
-        name="send" if flip else "keep",
-    )(sc, dy, dz, met, f1, f3, small)
+        input_output_aliases={6: 0, 7: 1},
+        compiler_params=PARAMS,
+        name="far",
+    )(sc, dy, met, f1, f3, small, send_l, keep_l)
 
 
 def hold_kernel(tiles, late, out):
@@ -216,23 +257,31 @@
 STEPS = tuple((k, w) for w in range(2) for k in range(4))
 
 
-def share_kernel(sc_ref, keep, got, own, *outs):
-    x, zl = sc_ref[3], sc_ref[4]
-    for (k, w), out in zip(STEPS, (own,) + outs):
-        q, h = lax.rem(x + k, 4), lax.rem(zl + w, 2)
-        out[...] = (keep[q, h] + got[q, h]).astype(out.dtype)
-
-
-def share(sc, keep, got):
+def share_kernel(sc_ref, keep_e, got_e, keep_l, got_l, *outs):
+    zh, co, x, zl = sc_ref[1], sc_ref[2], sc_ref[3], sc_ref[4]
+
+    def write(order):
+        for (k, w), out in zip(STEPS, outs):
+            q = lax.rem(x + k, 4)
+            keep, got = order[w]
+            out[...] = (keep[q] + got[q]).astype(out.dtype)
+
+    rows = ((keep_e, got_e), (keep_l, got_l))
+    same = early(zh, co) == zl
+    pl.when(same)(lambda: write(rows))
+    pl.when(jnp.logical_not(same))(lambda: write(rows[::-1]))
+
+
+def share(sc, *rows):
     piece = (ROWS, ROWS)
     return pl.pallas_call(
         share_kernel,
         out_shape=(jax.ShapeDtypeStruct(piece, F32),) + (jax.ShapeDtypeStruct(piece, BF16),) * 7,
-        in_specs=[SMEM, VMEM, VMEM],
+        in_specs=[SMEM] + [VMEM] * 4,
         out_specs=(VMEM,) * 8,
         compiler_params=PARAMS,
         name="share",
-    )(sc, keep, got)
+    )(sc, *rows)
 
 
 def hop(k, w):
@@ -262,10 +311,11 @@
     f3 = lax.ppermute(z3[HALF:], "zh", ring(4, 3))
 
     dy, dz, met = build(sc, [hold(tiles, z3)] + ys[1:], [z1, z3], parts, smalls)
-    send = gram(True, sc, dy, dz, met, f1, f3, smalls[2])
-    got = lax.ppermute(send, "co", ring(2, 1))
-    keep = gram(False, sc, dy, dz, met, f1, f3, smalls[2])
-    total, *shares = share(sc, keep, got)
+    got_e = lax.ppermute(first_row(sc, dy, dz), "co", ring(2, 1))
+    keep_e, send_l, keep_l = near_rows(sc, dy, dz)
+    send_l, keep_l = far_row(sc, dy, met, f1, f3, smalls[2], send_l, keep_l)
+    got_l = lax.ppermute(send_l, "co", ring(2, 1))
+    total, *shares = share(sc, keep_e, got_e, keep_l, got_l)
     for (k, w), piece in zip(STEPS[1:], shares):
         total = total + lax.ppermute(piece, ("x", "zl"), hop(k, w)).astype(F32)
     return lax.ppermute(total, ("y", "zh", "x", "zl", "co"), homes())

time: 97.1 us -> 97.6 us (level)
    ppermute x1, waiting for transfers between devices: 2.36 us -> 0.01 us  [local(): f3 = lax.ppermute(z3[HALF:], 'zh', ring(4, 3))]
    ppermute x1 -> x2, waiting for transfers between devices: 0.63 us -> 2.29 us  [the longest x1 2.28 us: local(): got_l = lax.ppermute(send_l, 'co', ring(2, 1))]
    ppermute x7, waiting for transfers between devices: 12.3 us -> 13.8 us  [local(): total = total + lax.ppermute(piece, ('x', 'zl'), hop(k, w)).astype(F32)]
    ppermute x7, starting transfers between devices: 9.15 us -> 8.1 us  [local(): total = total + lax.ppermute(piece, ('x', 'zl'), hop(k, w)).astype(F32)]
    pallas_call x2 -> x3, Pallas kernels: 6.27 us -> 6.62 us  [the longest x1 2.59 us: near_rows(): pl.pallas_call(near_kernel, out_shape=(ROW,) * 3, in_specs=[SMEM, VMEM, V...]
  transfers between devices with their start and end apart: 22 -> 23, of which waited for: 13 -> 11; matrix products, arithmetic and copies ran while one was open for 1% -> 1% of each run, Pallas kernels for 7% -> 10%
where the time goes in v6:
time: 97.6 us; the launch traced here: 97.3 us
  starting transfers between devices  47.5 us (49%)
  waiting for transfers between devices  35.2 us (36%)
  Pallas kernels  10.4 us (11%)
  local copies, waits for them, and re-layouts  3.97 us (4%)
    ppermute x7, waiting for transfers between devices, local(): total = total + lax.ppermute(piece, ('x', 'zl'), hop(k, w)).astype(F32)  13.8 us
    ppermute x1, waiting for transfers between devices, local(): return lax.ppermute(total, ('y', 'zh', 'x', 'zl', 'co'), homes())  10.7 us
    ppermute x3, starting transfers between devices, local(): ys = [tiles] + [lax.ppermute(tiles, 'y', ring(4, k)) for k in (1, 2, 3)]  10.4 us
    ppermute x3, starting transfers between devices, local(): lax.ppermute(small, 'zh', ring(4, k))  9.92 us
    ppermute x7, starting transfers between devices, local(): total = total + lax.ppermute(piece, ('x', 'zl'), hop(k, w)).astype(F32)  8.1 us
    ppermute x3, waiting for transfers between devices, local(): lax.ppermute(small, 'zh', ring(4, k))  6.19 us
    ppermute x1, starting transfers between devices, local(): f1 = lax.ppermute(z1[:HALF], 'zh', ring(4, 1))  4.83 us
    ppermute x3, starting transfers between devices, local(): parts = [part] + [lax.ppermute(part, 'y', ring(4, k)) for k in (1, 2, 3)]  3.88 us
  transfers between devices with their start and end apart: 23, of which 11 were waited for; matrix products, arithmetic and copies ran while one was open for 1% of the time, Pallas kernels for 10%

profile of v6, /device:TPU:56, one launch (start us, length us, event | category | flops | bytes accessed | tf_op | source)
XLA Modules:
  0.0 97.3 jit_solution(2455893129387007704)
XLA Ops:
  0.0 3.3 %collective-permute-start.4 = (bf16[1536,128]{1,0:T(8,128)(2,1)}, bf16[1536,128]{1,0:T(8,128)(2,1)S(1)}, u32[]{:S(2)}, u32[]{:S(2)}) collective-permute-start(bf16[1536,128]{1,0:T(8,128)(2,1)} %bitcast.7), channel_id=1, source_target_pairs={{0,16},{16,32},{32,48},{48,0},{1,17},{17,33},{33,49},{49,1},{2,18}... | collective-permute-start | bytes 1179656 | tf_op jit(solution)/shard_map/ppermute | solution.py:305
  3.3 2.1 %collective-permute-start = (bf16[1536,128]{1,0:T(8,128)(2,1)}, bf16[1536,128]{1,0:T(8,128)(2,1)S(1)}, u32[]{:S(2)}, u32[]{:S(2)}) collective-permute-start(bf16[1536,128]{1,0:T(8,128)(2,1)} %bitcast.8), channel_id=1, source_target_pairs={{0,48},{16,0},{32,16},{48,32},{1,49},{17,1},{33,17},{49,33},{2,50}... | collective-permute-start | bytes 1179656 | tf_op jit(solution)/shard_map/ppermute | solution.py:306
  7.6 0.8 collective-permute-start.7
  8.4 0.9 collective-permute-start.6
  9.3 2.2 %collective-permute-start.5 = (bf16[104,128]{1,0:T(8,128)(2,1)S(1)}, bf16[104,128]{1,0:T(8,128)(2,1)S(1)}, u32[]{:S(2)}, u32[]{:S(2)}) collective-permute-start(bf16[104,128]{1,0:T(8,128)(2,1)S(1)} %pack.1.m0.p0), channel_id=1, source_target_pairs={{0,64},{64,128},{128,192},{192,0},{1,65},{65,129},{129,193},{193,1... | collective-permute-start | bytes 79880 | tf_op jit(solution)/shard_map/ppermute | solution.py:303
  11.6 1.1 %collective-permute-done.7.m3.p3 = bf16[104,128]{1,0:T(8,128)(2,1)S(1)} collective-permute-done((bf16[104,128]{1,0:T(8,128)(2,1)S(1)}, bf16[104,128]{1,0:T(8,128)(2,1)S(1)}, u32[]{:S(2)}, u32[]{:S(2)}) %collective-permute-start.7) | collective-permute-done | bytes 26656 | tf_op jit(solution)/shard_map/ppermute | solution.py:303
  12.7 1.0 %collective-permute-done.6.m2.p2 = bf16[104,128]{1,0:T(8,128)(2,1)S(1)} collective-permute-done((bf16[104,128]{1,0:T(8,128)(2,1)S(1)}, bf16[104,128]{1,0:T(8,128)(2,1)S(1)}, u32[]{:S(2)}, u32[]{:S(2)}) %collective-permute-start.6) | collective-permute-done | bytes 26656 | tf_op jit(solution)/shard_map/ppermute | solution.py:303
  14.4 3.0 %collective-permute-start.10 = (bf16[400,128]{1,0:T(8,128)(2,1)S(1)}, bf16[400,128]{1,0:T(8,128)(2,1)S(1)}, u32[]{:S(2)}, u32[]{:S(2)}) collective-permute-start(bf16[400,128]{1,0:T(8,128)(2,1)S(1)} %line.1.s0), channel_id=1, source_target_pairs={{0,48},{16,0},{32,16},{48,32},{1,49},{17,1},{33,17},{49,33},{2,50}... | collective-permute-start | bytes 307208 | tf_op jit(solution)/shard_map/ppermute | solution.py:309
  17.4 1.7 %collective-permute-start.3 = (bf16[1536,128]{1,0:T(8,128)(2,1)}, bf16[1536,128]{1,0:T(8,128)(2,1)S(1)}, u32[]{:S(2)}, u32[]{:S(2)}) collective-permute-start(bf16[1536,128]{1,0:T(8,128)(2,1)} %bitcast.9), channel_id=1, source_target_pairs={{0,192},{64,0},{128,64},{192,128},{1,193},{65,1},{129,65},{193,129... | collective-permute-start | bytes 1179656 | tf_op jit(solution)/shard_map/ppermute | solution.py:307
  19.2 2.4 %collective-permute-start.2 = (bf16[1536,128]{1,0:T(8,128)(2,1)}, bf16[1536,128]{1,0:T(8,128)(2,1)S(1)}, u32[]{:S(2)}, u32[]{:S(2)}) collective-permute-start(bf16[1536,128]{1,0:T(8,128)(2,1)} %bitcast.10), channel_id=1, source_target_pairs={{0,128},{64,192},{128,0},{192,64},{1,129},{65,193},{129,1},{193,65... | collective-permute-start | bytes 1179656 | tf_op jit(solution)/shard_map/ppermute | solution.py:307
  21.8 6.2 %collective-permute-start.1 = (bf16[1536,128]{1,0:T(8,128)(2,1)}, bf16[1536,128]{1,0:T(8,128)(2,1)S(1)}, u32[]{:S(2)}, u32[]{:S(2)}) collective-permute-start(bf16[1536,128]{1,0:T(8,128)(2,1)} %bitcast.11), channel_id=1, source_target_pairs={{0,64},{64,128},{128,192},{192,0},{1,65},{65,129},{129,193},{193,1... | collective-permute-start | bytes 1179656 | tf_op jit(solution)/shard_map/ppermute | solution.py:307
  28.0 4.9 %collective-permute-start.9 = (bf16[400,128]{1,0:T(8,128)(2,1)S(1)}, bf16[400,128]{1,0:T(8,128)(2,1)S(1)}, u32[]{:S(2)}, u32[]{:S(2)}) collective-permute-start(bf16[400,128]{1,0:T(8,128)(2,1)S(1)} %line.1.s0), channel_id=1, source_target_pairs={{0,32},{16,48},{32,0},{48,16},{1,33},{17,49},{33,1},{49,17},{2,34}... | collective-permute-start | bytes 307208 | tf_op jit(solution)/shard_map/ppermute | solution.py:309
  33.0 2.0 %collective-permute-start.8 = (bf16[400,128]{1,0:T(8,128)(2,1)S(1)}, bf16[400,128]{1,0:T(8,128)(2,1)S(1)}, u32[]{:S(2)}, u32[]{:S(2)}) collective-permute-start(bf16[400,128]{1,0:T(8,128)(2,1)S(1)} %line.1.s0), channel_id=1, source_target_pairs={{0,16},{16,32},{32,48},{48,0},{1,17},{17,33},{33,49},{49,1},{2,18}... | collective-permute-start | bytes 307208 | tf_op jit(solution)/shard_map/ppermute | solution.py:309
  35.0 2.8 %collective-permute-done.9.s2 = bf16[400,128]{1,0:T(8,128)(2,1)S(1)} collective-permute-done((bf16[400,128]{1,0:T(8,128)(2,1)S(1)}, bf16[400,128]{1,0:T(8,128)(2,1)S(1)}, u32[]{:S(2)}, u32[]{:S(2)}) %collective-permute-start.9) | collective-permute-done | bytes 102432 | tf_op jit(solution)/shard_map/ppermute | solution.py:309
  37.8 4.8 %collective-permute-start.12 = (bf16[768,128]{1,0:T(8,128)(2,1)S(1)}, bf16[768,128]{1,0:T(8,128)(2,1)S(1)}, u32[]{:S(2)}, u32[]{:S(2)}) collective-permute-start(bf16[768,128]{1,0:T(8,128)(2,1)S(1)} %slice.8), channel_id=1, source_target_pairs={{0,16},{16,32},{32,48},{48,0},{1,17},{17,33},{33,49},{49,1},{2,18}... | collective-permute-start | bytes 589832 | tf_op jit(solution)/shard_map/ppermute | solution.py:310
  42.6 3.2 %collective-permute-done.8.s1 = bf16[400,128]{1,0:T(8,128)(2,1)S(1)} collective-permute-done((bf16[400,128]{1,0:T(8,128)(2,1)S(1)}, bf16[400,128]{1,0:T(8,128)(2,1)S(1)}, u32[]{:S(2)}, u32[]{:S(2)}) %collective-permute-start.8) | collective-permute-done | bytes 102432 | tf_op jit(solution)/shard_map/ppermute | solution.py:309
  46.4 1.0 %copy-done = bf16[2,6,128,128]{3,2,1,0:T(8,128)(2,1)S(1)} copy-done((bf16[2,6,128,128]{3,2,1,0:T(8,128)(2,1)S(1)}, bf16[2,6,128,128]{3,2,1,0:T(8,128)(2,1)}, u32[]{:S(2)}) %copy-start) | copy-done | bytes 393240
  47.4 2.4 %build.1 = (bf16[1024,1664]{1,0:T(8,128)(2,1)S(1)}, bf16[1024,1664]{1,0:T(8,128)(2,1)S(1)}, bf16[13,128,128]{2,1,0:T(8,128)(2,1)S(1)}) custom-call(s32[5]{0:T(128)S(1)} %stack.23.sc_ref, bf16[1536,128]{1,0:T(8,128)(2,1)S(1)} %hold.1.t0, bf16[1536,128]{1,0:T(8,128)(2,1)S(1)} %collective-permute-done.1.t1, bf16[1536,128]{1,0:T(8,128)(2,1)S(1)} %collective-permute-done.2.t2, ...), custom_call_target="tpu_custom_call" | custom-call | tf_op jit(solution)/shard_map/build/pallas_call | solution.py:131
  49.8 1.6 %first.1 = f32[4,256,256]{2,1,0:T(8,128)S(1)} custom-call(s32[5]{0:T(128)S(1)} %stack.23.sc_ref, bf16[1024,1664]{1,0:T(8,128)(2,1)S(1)} %get-tuple-element.21.dy, bf16[1024,1664]{1,0:T(8,128)(2,1)S(1)} %get-tuple-element.22.dz), custom_call_target="tpu_custom_call" | custom-call | tf_op jit(solution)/shard_map/first/pallas_call | solution.py:203
  51.4 2.6 %near.1 = (f32[4,256,256]{2,1,0:T(8,128)S(1)}, f32[4,256,256]{2,1,0:T(8,128)S(1)}, f32[4,256,256]{2,1,0:T(8,128)S(1)}) custom-call(s32[5]{0:T(128)S(1)} %stack.23.sc_ref, bf16[1024,1664]{1,0:T(8,128)(2,1)S(1)} %get-tuple-element.21.dy, bf16[1024,1664]{1,0:T(8,128)(2,1)S(1)} %get-tuple-element.22.dz), custom_call_target="tpu_custom_call" | custom-call | tf_op jit(solution)/shard_map/near/pallas_call | solution.py:214
  54.1 2.5 %far.1 = (f32[4,256,256]{2,1,0:T(8,128)S(1)}, f32[4,256,256]{2,1,0:T(8,128)S(1)}) custom-call(s32[5]{0:T(128)S(1)} %stack.23.sc_ref, bf16[1024,1664]{1,0:T(8,128)(2,1)S(1)} %get-tuple-element.21.dy, bf16[13,128,128]{2,1,0:T(8,128)(2,1)S(1)} %get-tuple-element.24.met, ...), custom_call_target="tpu_custom_call", output_to_operand_aliasing={{0}: (6, {}), {1}: (7, {})} | custom-call | tf_op jit(solution)/shard_map/far/pallas_call | solution.py:225
  57.2 2.3 %collective-permute-done.14.got_l = f32[4,256,256]{2,1,0:T(8,128)S(1)} collective-permute-done((f32[4,256,256]{2,1,0:T(8,128)S(1)}, f32[4,256,256]{2,1,0:T(8,128)S(1)}, u32[]{:S(2)}, u32[]{:S(2)}) %collective-permute-start.14) | collective-permute-done | bytes 1048608 | tf_op jit(solution)/shard_map/ppermute | solution.py:317
  59.5 0.7 share.1
  60.2 1.6 %collective-permute-start.15 = (bf16[256,256]{1,0:T(8,128)(2,1)S(1)}, bf16[256,256]{1,0:T(8,128)(2,1)S(1)}, u32[]{:S(2)}, u32[]{:S(2)}) collective-permute-start(bf16[256,256]{1,0:T(8,128)(2,1)S(1)} %get-tuple-element.30), channel_id=1, source_target_pairs={{0,4},{2,6},{4,8},{6,10},{8,12},{10,14},{12,0},{14,2},{1,5},{3,7},... | collective-permute-start | bytes 393224 | tf_op jit(solution)/shard_map/ppermute | solution.py:320
  61.8 2.7 %collective-permute-start.16 = (bf16[256,256]{1,0:T(8,128)(2,1)S(1)}, bf16[256,256]{1,0:T(8,128)(2,1)S(1)}, u32[]{:S(2)}, u32[]{:S(2)}) collective-permute-start(bf16[256,256]{1,0:T(8,128)(2,1)S(1)} %get-tuple-element.31), channel_id=1, source_target_pairs={{0,8},{2,10},{4,12},{6,14},{8,0},{10,2},{12,4},{14,6},{1,9},{3,11}... | collective-permute-start | bytes 393224 | tf_op jit(solution)/shard_map/ppermute | solution.py:320
  64.5 1.4 %collective-permute-start.17 = (bf16[256,256]{1,0:T(8,128)(2,1)S(1)}, bf16[256,256]{1,0:T(8,128)(2,1)S(1)}, u32[]{:S(2)}, u32[]{:S(2)}) collective-permute-start(bf16[256,256]{1,0:T(8,128)(2,1)S(1)} %get-tuple-element.32), channel_id=1, source_target_pairs={{0,12},{2,14},{4,0},{6,2},{8,4},{10,6},{12,8},{14,10},{1,13},{3,15... | collective-permute-start | bytes 393224 | tf_op jit(solution)/shard_map/ppermute | solution.py:320
  66.0 2.0 %collective-permute-start.19 = (bf16[256,256]{1,0:T(8,128)(2,1)S(1)}, bf16[256,256]{1,0:T(8,128)(2,1)S(1)}, u32[]{:S(2)}, u32[]{:S(2)}) collective-permute-start(bf16[256,256]{1,0:T(8,128)(2,1)S(1)} %get-tuple-element.34), channel_id=1, source_target_pairs={{0,6},{2,4},{4,10},{6,8},{8,14},{10,12},{12,2},{14,0},{1,7},{3,5},... | collective-permute-start | bytes 393224 | tf_op jit(solution)/shard_map/ppermute | solution.py:320
  68.3 7.9 %collective-permute-done.16 = bf16[256,256]{1,0:T(8,128)(2,1)S(1)} collective-permute-done((bf16[256,256]{1,0:T(8,128)(2,1)S(1)}, bf16[256,256]{1,0:T(8,128)(2,1)S(1)}, u32[]{:S(2)}, u32[]{:S(2)}) %collective-permute-start.16) | collective-permute-done | bytes 131104 | tf_op jit(solution)/shard_map/ppermute | solution.py:320
  76.3 1.6 %collective-permute-done.20 = bf16[256,256]{1,0:T(8,128)(2,1)S(1)} collective-permute-done((bf16[256,256]{1,0:T(8,128)(2,1)S(1)}, bf16[256,256]{1,0:T(8,128)(2,1)S(1)}, u32[]{:S(2)}, u32[]{:S(2)}) %collective-permute-start.20) | collective-permute-done | bytes 131104 | tf_op jit(solution)/shard_map/ppermute | solution.py:320
  77.9 4.2 %collective-permute-done.21 = bf16[256,256]{1,0:T(8,128)(2,1)S(1)} collective-permute-done((bf16[256,256]{1,0:T(8,128)(2,1)S(1)}, bf16[256,256]{1,0:T(8,128)(2,1)S(1)}, u32[]{:S(2)}, u32[]{:S(2)}) %collective-permute-start.21) | collective-permute-done | bytes 131104 | tf_op jit(solution)/shard_map/ppermute | solution.py:320
  82.2 3.7 %collective-permute-start.22 = (f32[256,256]{1,0:T(8,128)S(1)}, f32[256,256]{1,0:T(8,128)S(1)}, u32[]{:S(2)}, u32[]{:S(2)}) collective-permute-start(f32[256,256]{1,0:T(8,128)S(1)} %convert_add_fusion), channel_id=1, source_target_pairs={{0,0},{1,16},{2,2},{3,48},{4,4},{5,20},{6,66},{7,52},{8,8},{9,24},... | collective-permute-start | bytes 786440 | tf_op jit(solution)/shard_map/ppermute | solution.py:321
  86.0 10.7 %collective-permute-done.22 = f32[256,256]{1,0:T(8,128)S(1)} collective-permute-done((f32[256,256]{1,0:T(8,128)S(1)}, f32[256,256]{1,0:T(8,128)S(1)}, u32[]{:S(2)}, u32[]{:S(2)}) %collective-permute-start.22) | collective-permute-done | bytes 262176 | tf_op jit(solution)/shard_map/ppermute | solution.py:321
  (34 shorter events, 5.6 us)
Async XLA Ops:
  0.0 28.0 %collective-permute-start.4 = (bf16[1536,128]{1,0:T(8,128)(2,1)}, bf16[1536,128]{1,0:T(8,128)(2,1)S(1)}, u32[]{:S(2)}, u32[]{:S(2)}) collective-permute-start(bf16[1536,128]{1,0:T(8,128)(2,1)} %bitcast.7), channel_id=1, source_target_pairs={{0,16},{16,32},{32,48},{48,0},{1,17},{17,33},{33,49},{49,1},{2,18}... | collective-permute-start | bytes 1179656 | tf_op jit(solution)/shard_map/ppermute | solution.py:305
  3.3 29.7 %collective-permute-start = (bf16[1536,128]{1,0:T(8,128)(2,1)}, bf16[1536,128]{1,0:T(8,128)(2,1)S(1)}, u32[]{:S(2)}, u32[]{:S(2)}) collective-permute-start(bf16[1536,128]{1,0:T(8,128)(2,1)} %bitcast.8), channel_id=1, source_target_pairs={{0,48},{16,0},{32,16},{48,32},{1,49},{17,1},{33,17},{49,33},{2,50}... | collective-permute-start | bytes 1179656 | tf_op jit(solution)/shard_map/ppermute | solution.py:306
  6.1 0.7 copy-start.1
  6.9 0.7 copy-start.2
  7.6 5.1 %collective-permute-start.7 = (bf16[104,128]{1,0:T(8,128)(2,1)S(1)}, bf16[104,128]{1,0:T(8,128)(2,1)S(1)}, u32[]{:S(2)}, u32[]{:S(2)}) collective-permute-start(bf16[104,128]{1,0:T(8,128)(2,1)S(1)} %pack.1.m0.p0), channel_id=1, source_target_pairs={{0,192},{64,0},{128,64},{192,128},{1,193},{65,1},{129,65},{193,129... | collective-permute-start | bytes 79880 | tf_op jit(solution)/shard_map/ppermute | solution.py:303
  8.4 5.4 %collective-permute-start.6 = (bf16[104,128]{1,0:T(8,128)(2,1)S(1)}, bf16[104,128]{1,0:T(8,128)(2,1)S(1)}, u32[]{:S(2)}, u32[]{:S(2)}) collective-permute-start(bf16[104,128]{1,0:T(8,128)(2,1)S(1)} %pack.1.m0.p0), channel_id=1, source_target_pairs={{0,128},{64,192},{128,0},{192,64},{1,129},{65,193},{129,1},{193,65... | collective-permute-start | bytes 79880 | tf_op jit(solution)/shard_map/ppermute | solution.py:303
  9.3 4.5 %collective-permute-start.5 = (bf16[104,128]{1,0:T(8,128)(2,1)S(1)}, bf16[104,128]{1,0:T(8,128)(2,1)S(1)}, u32[]{:S(2)}, u32[]{:S(2)}) collective-permute-start(bf16[104,128]{1,0:T(8,128)(2,1)S(1)} %pack.1.m0.p0), channel_id=1, source_target_pairs={{0,64},{64,128},{128,192},{192,0},{1,65},{65,129},{129,193},{193,1... | collective-permute-start | bytes 79880 | tf_op jit(solution)/shard_map/ppermute | solution.py:303
  14.4 7.4 %collective-permute-start.10 = (bf16[400,128]{1,0:T(8,128)(2,1)S(1)}, bf16[400,128]{1,0:T(8,128)(2,1)S(1)}, u32[]{:S(2)}, u32[]{:S(2)}) collective-permute-start(bf16[400,128]{1,0:T(8,128)(2,1)S(1)} %line.1.s0), channel_id=1, source_target_pairs={{0,48},{16,0},{32,16},{48,32},{1,49},{17,1},{33,17},{49,33},{2,50}... | collective-permute-start | bytes 307208 | tf_op jit(solution)/shard_map/ppermute | solution.py:309
  17.4 30.0 %collective-permute-start.3 = (bf16[1536,128]{1,0:T(8,128)(2,1)}, bf16[1536,128]{1,0:T(8,128)(2,1)S(1)}, u32[]{:S(2)}, u32[]{:S(2)}) collective-permute-start(bf16[1536,128]{1,0:T(8,128)(2,1)} %bitcast.9), channel_id=1, source_target_pairs={{0,192},{64,0},{128,64},{192,128},{1,193},{65,1},{129,65},{193,129... | collective-permute-start | bytes 1179656 | tf_op jit(solution)/shard_map/ppermute | solution.py:307
  19.2 28.2 %collective-permute-start.2 = (bf16[1536,128]{1,0:T(8,128)(2,1)}, bf16[1536,128]{1,0:T(8,128)(2,1)S(1)}, u32[]{:S(2)}, u32[]{:S(2)}) collective-permute-start(bf16[1536,128]{1,0:T(8,128)(2,1)} %bitcast.10), channel_id=1, source_target_pairs={{0,128},{64,192},{128,0},{192,64},{1,129},{65,193},{129,1},{193,65... | collective-permute-start | bytes 1179656 | tf_op jit(solution)/shard_map/ppermute | solution.py:307
  21.8 25.6 %collective-permute-start.1 = (bf16[1536,128]{1,0:T(8,128)(2,1)}, bf16[1536,128]{1,0:T(8,128)(2,1)S(1)}, u32[]{:S(2)}, u32[]{:S(2)}) collective-permute-start(bf16[1536,128]{1,0:T(8,128)(2,1)} %bitcast.11), channel_id=1, source_target_pairs={{0,64},{64,128},{128,192},{192,0},{1,65},{65,129},{129,193},{193,1... | collective-permute-start | bytes 1179656 | tf_op jit(solution)/shard_map/ppermute | solution.py:307
  28.0 9.8 %collective-permute-start.9 = (bf16[400,128]{1,0:T(8,128)(2,1)S(1)}, bf16[400,128]{1,0:T(8,128)(2,1)S(1)}, u32[]{:S(2)}, u32[]{:S(2)}) collective-permute-start(bf16[400,128]{1,0:T(8,128)(2,1)S(1)} %line.1.s0), channel_id=1, source_target_pairs={{0,32},{16,48},{32,0},{48,16},{1,33},{17,49},{33,1},{49,17},{2,34}... | collective-permute-start | bytes 307208 | tf_op jit(solution)/shard_map/ppermute | solution.py:309
  33.0 12.9 %collective-permute-start.8 = (bf16[400,128]{1,0:T(8,128)(2,1)S(1)}, bf16[400,128]{1,0:T(8,128)(2,1)S(1)}, u32[]{:S(2)}, u32[]{:S(2)}) collective-permute-start(bf16[400,128]{1,0:T(8,128)(2,1)S(1)} %line.1.s0), channel_id=1, source_target_pairs={{0,16},{16,32},{32,48},{48,0},{1,17},{17,33},{33,49},{49,1},{2,18}... | collective-permute-start | bytes 307208 | tf_op jit(solution)/shard_map/ppermute | solution.py:309
  37.8 16.3 %collective-permute-start.12 = (bf16[768,128]{1,0:T(8,128)(2,1)S(1)}, bf16[768,128]{1,0:T(8,128)(2,1)S(1)}, u32[]{:S(2)}, u32[]{:S(2)}) collective-permute-start(bf16[768,128]{1,0:T(8,128)(2,1)S(1)} %slice.8), channel_id=1, source_target_pairs={{0,16},{16,32},{32,48},{48,0},{1,17},{17,33},{33,49},{49,1},{2,18}... | collective-permute-start | bytes 589832 | tf_op jit(solution)/shard_map/ppermute | solution.py:310
  45.8 8.3 %collective-permute-start.13 = (bf16[768,128]{1,0:T(8,128)(2,1)S(1)}, bf16[768,128]{1,0:T(8,128)(2,1)S(1)}, u32[]{:S(2)}, u32[]{:S(2)}) collective-permute-start(bf16[768,128]{1,0:T(8,128)(2,1)S(1)} %slice.9), channel_id=1, source_target_pairs={{0,48},{16,0},{32,16},{48,32},{1,49},{17,1},{33,17},{49,33},{2,50}... | collective-permute-start | bytes 589832 | tf_op jit(solution)/shard_map/ppermute | solution.py:311
  46.4 1.0 %copy-start = (bf16[2,6,128,128]{3,2,1,0:T(8,128)(2,1)S(1)}, bf16[2,6,128,128]{3,2,1,0:T(8,128)(2,1)}, u32[]{:S(2)}) copy-start(bf16[2,6,128,128]{3,2,1,0:T(8,128)(2,1)} %param.4) | copy-start | bytes 1179652
  54.0 3.2 %collective-permute-start.11 = (f32[4,256,256]{2,1,0:T(8,128)S(1)}, f32[4,256,256]{2,1,0:T(8,128)S(1)}, u32[]{:S(2)}, u32[]{:S(2)}) collective-permute-start(f32[4,256,256]{2,1,0:T(8,128)S(1)} %first.1), channel_id=1, source_target_pairs={{0,1},{1,0},{2,3},{3,2},{4,5},{5,4},{6,7},{7,6},{8,9},{9,8},{10,11... | collective-permute-start | bytes 3145736 | tf_op jit(solution)/shard_map/ppermute | solution.py:314
  56.6 2.9 %collective-permute-start.14 = (f32[4,256,256]{2,1,0:T(8,128)S(1)}, f32[4,256,256]{2,1,0:T(8,128)S(1)}, u32[]{:S(2)}, u32[]{:S(2)}) collective-permute-start(f32[4,256,256]{2,1,0:T(8,128)S(1)} %get-tuple-element.28), channel_id=1, source_target_pairs={{0,1},{1,0},{2,3},{3,2},{4,5},{5,4},{6,7},{7,6},{8,9},{9,8},{10,11... | collective-permute-start | bytes 3145736 | tf_op jit(solution)/shard_map/ppermute | solution.py:317
  60.2 7.8 %collective-permute-start.15 = (bf16[256,256]{1,0:T(8,128)(2,1)S(1)}, bf16[256,256]{1,0:T(8,128)(2,1)S(1)}, u32[]{:S(2)}, u32[]{:S(2)}) collective-permute-start(bf16[256,256]{1,0:T(8,128)(2,1)S(1)} %get-tuple-element.30), channel_id=1, source_target_pairs={{0,4},{2,6},{4,8},{6,10},{8,12},{10,14},{12,0},{14,2},{1,5},{3,7},... | collective-permute-start | bytes 393224 | tf_op jit(solution)/shard_map/ppermute | solution.py:320
  61.8 14.4 %collective-permute-start.16 = (bf16[256,256]{1,0:T(8,128)(2,1)S(1)}, bf16[256,256]{1,0:T(8,128)(2,1)S(1)}, u32[]{:S(2)}, u32[]{:S(2)}) collective-permute-start(bf16[256,256]{1,0:T(8,128)(2,1)S(1)} %get-tuple-element.31), channel_id=1, source_target_pairs={{0,8},{2,10},{4,12},{6,14},{8,0},{10,2},{12,4},{14,6},{1,9},{3,11}... | collective-permute-start | bytes 393224 | tf_op jit(solution)/shard_map/ppermute | solution.py:320
  64.5 11.7 %collective-permute-start.17 = (bf16[256,256]{1,0:T(8,128)(2,1)S(1)}, bf16[256,256]{1,0:T(8,128)(2,1)S(1)}, u32[]{:S(2)}, u32[]{:S(2)}) collective-permute-start(bf16[256,256]{1,0:T(8,128)(2,1)S(1)} %get-tuple-element.32), channel_id=1, source_target_pairs={{0,12},{2,14},{4,0},{6,2},{8,4},{10,6},{12,8},{14,10},{1,13},{3,15... | collective-permute-start | bytes 393224 | tf_op jit(solution)/shard_map/ppermute | solution.py:320
  66.0 10.3 %collective-permute-start.18 = (bf16[256,256]{1,0:T(8,128)(2,1)S(1)}, bf16[256,256]{1,0:T(8,128)(2,1)S(1)}, u32[]{:S(2)}, u32[]{:S(2)}) collective-permute-start(bf16[256,256]{1,0:T(8,128)(2,1)S(1)} %get-tuple-element.33), channel_id=1, source_target_pairs={{0,2},{2,0},{4,6},{6,4},{8,10},{10,8},{12,14},{14,12},{1,3},{3,1},... | collective-permute-start | bytes 393224 | tf_op jit(solution)/shard_map/ppermute | solution.py:320
  66.0 10.3 %collective-permute-start.19 = (bf16[256,256]{1,0:T(8,128)(2,1)S(1)}, bf16[256,256]{1,0:T(8,128)(2,1)S(1)}, u32[]{:S(2)}, u32[]{:S(2)}) collective-permute-start(bf16[256,256]{1,0:T(8,128)(2,1)S(1)} %get-tuple-element.34), channel_id=1, source_target_pairs={{0,6},{2,4},{4,10},{6,8},{8,14},{10,12},{12,2},{14,0},{1,7},{3,5},... | collective-permute-start | bytes 393224 | tf_op jit(solution)/shard_map/ppermute | solution.py:320
  68.0 9.8 %collective-permute-start.20 = (bf16[256,256]{1,0:T(8,128)(2,1)S(1)}, bf16[256,256]{1,0:T(8,128)(2,1)S(1)}, u32[]{:S(2)}, u32[]{:S(2)}) collective-permute-start(bf16[256,256]{1,0:T(8,128)(2,1)S(1)} %get-tuple-element.35), channel_id=1, source_target_pairs={{0,10},{2,8},{4,14},{6,12},{8,2},{10,0},{12,6},{14,4},{1,11},{3,9}... | collective-permute-start | bytes 393224 | tf_op jit(solution)/shard_map/ppermute | solution.py:320
  76.2 5.9 %collective-permute-start.21 = (bf16[256,256]{1,0:T(8,128)(2,1)S(1)}, bf16[256,256]{1,0:T(8,128)(2,1)S(1)}, u32[]{:S(2)}, u32[]{:S(2)}) collective-permute-start(bf16[256,256]{1,0:T(8,128)(2,1)S(1)} %get-tuple-element.36), channel_id=1, source_target_pairs={{0,14},{2,12},{4,2},{6,0},{8,6},{10,4},{12,10},{14,8},{1,15},{3,13... | collective-permute-start | bytes 393224 | tf_op jit(solution)/shard_map/ppermute | solution.py:320
  82.2 14.4 %collective-permute-start.22 = (f32[256,256]{1,0:T(8,128)S(1)}, f32[256,256]{1,0:T(8,128)S(1)}, u32[]{:S(2)}, u32[]{:S(2)}) collective-permute-start(f32[256,256]{1,0:T(8,128)S(1)} %convert_add_fusion), channel_id=1, source_target_pairs={{0,0},{1,16},{2,2},{3,48},{4,4},{5,20},{6,66},{7,52},{8,8},{9,24},... | collective-permute-start | bytes 786440 | tf_op jit(solution)/shard_map/ppermute | solution.py:321

commit v7 on v5

--- a/solution.py
+++ b/solution.py
@@ -21,6 +21,7 @@
 PART = QB * MROWS
 LIST0 = 4 * PART
 SMALL = LIST0 + 16
+MHALF = LIST0 // 2
 F32 = jnp.float32
 BF16 = jnp.bfloat16
 
@@ -95,17 +96,37 @@
     return ref[at : at + 8, :].astype(F32).astype(jnp.int32)
 
 
+def relay_kernel(first, tiles, rows, out):
+    start, at = (0, 0) if first else (HALF, MHALF)
+    out[0:HALF, :] = tiles[start : start + HALF, :]
+    out[HALF : out.shape[0], :] = rows[at : at + out.shape[0] - HALF, :]
+
+
+def relay(first, tiles, rows):
+    size = HALF + (MHALF if first else SMALL - MHALF)
+    return pl.pallas_call(
+        functools.partial(relay_kernel, first),
+        out_shape=jax.ShapeDtypeStruct((size, AUXB), BF16),
+        in_specs=[VMEM] * 2,
+        out_specs=VMEM,
+        compiler_params=PARAMS,
+        name="relay",
+    )(tiles, rows)
+
+
 def build_kernel(
-    sc_ref, t0, t1, t2, t3, z1, z3, p0, p1, p2, p3, s0, s1, s2, s3, dy, dz, met, lv, ls, sem
+    sc_ref, t0, t1, t2, t3, z1, z3, f1, f3, p0, p1, p2, p3, s0, s1, s3, dy, dz, met, lv, ls, sem
 ):
     y, zh = sc_ref[0], sc_ref[1]
     for k, p in enumerate((p0, p1, p2, p3)):
         lv[8 * k : 8 * k + 8, :] = read_lists(p, PART)
-    for n, s in ((4, s1), (5, s3)):
-        lv[8 * n : 8 * n + 8, :] = read_lists(s, LIST0)
+    for n, s, at in ((4, s1, LIST0), (5, s3, LIST0), (6, f3, HALF + MHALF)):
+        lv[8 * n : 8 * n + 8, :] = read_lists(s, at)
     copy = pltpu.make_async_copy(lv, ls, sem)
     copy.start()
-    lines = [s[0:LIST0, :].astype(F32) for s in (s0, s1, s2, s3)]
+    two = [f[HALF : HALF + MHALF, :].astype(F32) for f in (f1, f3)]
+    lines = [s[0:LIST0, :].astype(F32) for s in (s0, s1, s3)]
+    lines.insert(2, jnp.concatenate(two, axis=0))
     for src in range(4):
         k = back(zh, src)
         near = jnp.where(k == 0, lines[0], lines[1])
@@ -126,18 +147,21 @@
         fill_block(t, met, ls, 8 * k, dy, back(y, k) * ROWS)
     for n, k, t in ((4, 1, z1), (5, 3, z3)):
         fill_block(t, met, ls, 8 * n, dz, back(zh, k) * ROWS)
+    for a, f in enumerate((f1, f3)):
+        fill(f, 0, met, ls, 48 + a, dz, back(zh, 2) * ROWS + a * BS)
 
 
 def build(sc, tiles, zs, parts, smalls):
     dense = jax.ShapeDtypeStruct((4 * ROWS, WIDE), BF16)
     return pl.pallas_call(
         build_kernel,
-        out_shape=(dense, dense, jax.ShapeDtypeStruct((QB + 1, AUXB, AUXB), BF16)),
-        in_specs=[SMEM] + [VMEM] * 14,
-        out_specs=(VMEM,) * 3,
+        out_shape=(dense, dense),
+        in_specs=[SMEM] + [VMEM] * 15,
+        out_specs=(VMEM,) * 2,
         scratch_shapes=[
-            pltpu.VMEM((48, 128), jnp.int32),
-            pltpu.SMEM((48, 128), jnp.int32),
+            pltpu.VMEM((QB + 1, AUXB, AUXB), BF16),
+            pltpu.VMEM((56, 128), jnp.int32),
+            pltpu.SMEM((56, 128), jnp.int32),
             pltpu.SemaphoreType.DMA,
         ],
         compiler_params=PARAMS,
@@ -145,57 +169,35 @@
     )(sc, *tiles, *zs, *parts, *smalls)
 
 
-def gram_kernel(flip, sc_ref, dy, dz, met, f1, f3, s2, out, far, lv, ls, sem):
+def gram_kernel(flip, sc_ref, dy, dz, out):
     zh, co = sc_ref[1], sc_ref[2]
     parity = 1 - co if flip else co
     opposite = back(zh, 2)
     factor = 1.0 / (QS * 16 * AUXB) ** 0.5
-
-    @pl.when(lax.rem(zh, 2) == parity)
-    def _():
-        lv[...] = read_lists(s2, LIST0)
-        copy = pltpu.make_async_copy(lv, ls, sem)
-        copy.start()
-        far[...] = jnp.zeros_like(far)
-        copy.wait()
-        fill(f1, 0, met, ls, 0, far, 0)
-        fill(f3, 0, met, ls, 1, far, BS)
-
-    def product(h, swapped, block):
-        for q in range(4):
-            row = dy[q * ROWS : (q + 1) * ROWS, 0:USED]
-            pair = (block, row) if swapped else (row, block)
-            prod = lax.dot_general(*pair, (((1,), (1,)), ((), ())), preferred_element_type=F32)
-            out[q, h] = prod * factor
-
     for h in range(2):
         p = 2 * h + parity
-
-        @pl.when(p == opposite)
-        def _():
-            product(h, True, far[:, 0:USED])
-
-        @pl.when(p != opposite)
-        def _():
-            at = pl.multiple_of(p * ROWS, ROWS)
-            product(h, False, dz[pl.ds(at, ROWS), 0:USED])
-
-
-def gram(flip, sc, dy, dz, met, f1, f3, small):
+        block = dz[pl.ds(pl.multiple_of(p * ROWS, ROWS), ROWS), 0:USED]
+
+        def product(swapped):
+            for q in range(4):
+                row = dy[q * ROWS : (q + 1) * ROWS, 0:USED]
+                pair = (block, row) if swapped else (row, block)
+                prod = lax.dot_general(*pair, (((1,), (1,)), ((), ())), preferred_element_type=F32)
+                out[q, h] = prod * factor
+
+        pl.when(p == opposite)(lambda: product(True))
+        pl.when(p != opposite)(lambda: product(False))
+
+
+def gram(flip, sc, dy, dz):
     return pl.pallas_call(
         functools.partial(gram_kernel, flip),
         out_shape=jax.ShapeDtypeStruct((4, 2, ROWS, ROWS), F32),
-        in_specs=[SMEM] + [VMEM] * 6,
-        out_specs=VMEM,
-        scratch_shapes=[
-            pltpu.VMEM((ROWS, WIDE), BF16),
-            pltpu.VMEM((8, 128), jnp.int32),
-            pltpu.SMEM((8, 128), jnp.int32),
-            pltpu.SemaphoreType.DMA,
-        ],
+        in_specs=[SMEM] + [VMEM] * 2,
+        out_specs=VMEM,
         compiler_params=PARAMS,
         name="send" if flip else "keep",
-    )(sc, dy, dz, met, f1, f3, small)
+    )(sc, dy, dz)
 
 
 def hold_kernel(tiles, late, out):
@@ -257,14 +259,16 @@
     z3 = lax.ppermute(tiles, "zh", ring(4, 3))
     ys = [tiles] + [lax.ppermute(tiles, "y", ring(4, k)) for k in (1, 2, 3)]
     small = line(sc, parts)
-    smalls = [small] + [lax.ppermute(small, "zh", ring(4, k)) for k in (1, 2, 3)]
-    f1 = lax.ppermute(z1[:HALF], "zh", ring(4, 1))
-    f3 = lax.ppermute(z3[HALF:], "zh", ring(4, 3))
-
-    dy, dz, met = build(sc, [hold(tiles, z3)] + ys[1:], [z1, z3], parts, smalls)
-    send = gram(True, sc, dy, dz, met, f1, f3, smalls[2])
+    s1 = lax.ppermute(small, "zh", ring(4, 1))
+    s3 = lax.ppermute(small, "zh", ring(4, 3))
+    f1 = lax.ppermute(relay(True, z1, s1), "zh", ring(4, 1))
+    f3 = lax.ppermute(relay(False, z3, s3), "zh", ring(4, 3))
+
+    mine = hold(tiles, z3)
+    dy, dz = build(sc, [mine] + ys[1:], [z1, z3, f1, f3], parts, [small, s1, s3])
+    send = gram(True, sc, dy, dz)
     got = lax.ppermute(send, "co", ring(2, 1))
-    keep = gram(False, sc, dy, dz, met, f1, f3, smalls[2])
+    keep = gram(False, sc, dy, dz)
     total, *shares = share(sc, keep, got)
     for (k, w), piece in zip(STEPS[1:], shares):
         total = total + lax.ppermute(piece, ("x", "zl"), hop(k, w)).astype(F32)

time: 97.1 us -> 95.5 us (0.984)
  the two profiles are of different devices: /device:TPU:56 before, /device:TPU:38 now
where the time goes in v7:
time: 95.5 us; the launch traced here: 95.3 us
  waiting for transfers between devices  45.9 us (48%)
  starting transfers between devices  35.7 us (37%)
  Pallas kernels  9.54 us (10%)
  local copies, waits for them, and re-layouts  3.93 us (4%)
    ppermute x1, waiting for transfers between devices, local(): f1 = lax.ppermute(relay(True, z1, s1), 'zh', ring(4, 1))  10.4 us
    ppermute x1, waiting for transfers between devices, local(): return lax.ppermute(total, ('y', 'zh', 'x', 'zl', 'co'), homes())  10 us
    ppermute x7, starting transfers between devices, local(): total = total + lax.ppermute(piece, ('x', 'zl'), hop(k, w)).astype(F32)  9.49 us
    ppermute x7, waiting for transfers between devices, local(): total = total + lax.ppermute(piece, ('x', 'zl'), hop(k, w)).astype(F32)  9.31 us
    pallas_call x2, Pallas kernels, gram(): pl.pallas_call(functools.partial(gram_kernel, flip), out_shape=jax.ShapeD...  5.57 us
    ppermute x1, waiting for transfers between devices, local(): s1 = lax.ppermute(small, 'zh', ring(4, 1))  5.48 us
    ppermute x1, starting transfers between devices, local(): z3 = lax.ppermute(tiles, 'zh', ring(4, 3))  5.4 us
    ppermute x3, starting transfers between devices, local(): parts = [part] + [lax.ppermute(part, 'y', ring(4, k)) for k in (1, 2, 3)]  4.63 us
  transfers between devices with their start and end apart: 21, of which 13 were waited for; matrix products, arithmetic and copies ran while one was open for 1% of the time, Pallas kernels for 4%

profile of v7, /device:TPU:38, one launch (start us, length us, event | category | flops | bytes accessed | tf_op | source)
XLA Modules:
  0.0 95.3 jit_solution(4043453611370637556)
XLA Ops:
  0.0 5.4 %collective-permute-start = (bf16[1536,128]{1,0:T(8,128)(2,1)}, bf16[1536,128]{1,0:T(8,128)(2,1)S(1)}, u32[]{:S(2)}, u32[]{:S(2)}) collective-permute-start(bf16[1536,128]{1,0:T(8,128)(2,1)} %bitcast.7), channel_id=1, source_target_pairs={{0,48},{16,0},{32,16},{48,32},{1,49},{17,1},{33,17},{49,33},{2,50}... | collective-permute-start | bytes 1179656 | tf_op jit(solution)/shard_map/ppermute | solution.py:259
  5.4 0.7 copy.5.counts
  6.1 0.7 copy-done.1
  6.9 0.7 copy-done.2
  7.6 3.0 %collective-permute-start.7 = (bf16[104,128]{1,0:T(8,128)(2,1)S(1)}, bf16[104,128]{1,0:T(8,128)(2,1)S(1)}, u32[]{:S(2)}, u32[]{:S(2)}) collective-permute-start(bf16[104,128]{1,0:T(8,128)(2,1)S(1)} %pack.1.m0.p0), channel_id=1, source_target_pairs={{0,192},{64,0},{128,64},{192,128},{1,193},{65,1},{129,65},{193,129... | collective-permute-start | bytes 79880 | tf_op jit(solution)/shard_map/ppermute | solution.py:256
  10.7 0.6 collective-permute-start.6
  11.3 1.0 %collective-permute-start.5 = (bf16[104,128]{1,0:T(8,128)(2,1)S(1)}, bf16[104,128]{1,0:T(8,128)(2,1)S(1)}, u32[]{:S(2)}, u32[]{:S(2)}) collective-permute-start(bf16[104,128]{1,0:T(8,128)(2,1)S(1)} %pack.1.m0.p0), channel_id=1, source_target_pairs={{0,64},{64,128},{128,192},{192,0},{1,65},{65,129},{129,193},{193,1... | collective-permute-start | bytes 79880 | tf_op jit(solution)/shard_map/ppermute | solution.py:256
  12.4 3.7 %collective-permute-done.6.m2.p2 = bf16[104,128]{1,0:T(8,128)(2,1)S(1)} collective-permute-done((bf16[104,128]{1,0:T(8,128)(2,1)S(1)}, bf16[104,128]{1,0:T(8,128)(2,1)S(1)}, u32[]{:S(2)}, u32[]{:S(2)}) %collective-permute-start.6) | collective-permute-done | bytes 26656 | tf_op jit(solution)/shard_map/ppermute | solution.py:256
  16.4 0.6 line.1.s0
  16.9 4.2 %collective-permute-start.10 = (bf16[400,128]{1,0:T(8,128)(2,1)S(1)}, bf16[400,128]{1,0:T(8,128)(2,1)S(1)}, u32[]{:S(2)}, u32[]{:S(2)}) collective-permute-start(bf16[400,128]{1,0:T(8,128)(2,1)S(1)} %line.1.s0), channel_id=1, source_target_pairs={{0,48},{16,0},{32,16},{48,32},{1,49},{17,1},{33,17},{49,33},{2,50}... | collective-permute-start | bytes 307208 | tf_op jit(solution)/shard_map/ppermute | solution.py:263
  21.6 1.3 %collective-permute-start.2 = (bf16[1536,128]{1,0:T(8,128)(2,1)}, bf16[1536,128]{1,0:T(8,128)(2,1)S(1)}, u32[]{:S(2)}, u32[]{:S(2)}) collective-permute-start(bf16[1536,128]{1,0:T(8,128)(2,1)} %bitcast.10), channel_id=1, source_target_pairs={{0,128},{64,192},{128,0},{192,64},{1,129},{65,193},{129,1},{193,65... | collective-permute-start | bytes 1179656 | tf_op jit(solution)/shard_map/ppermute | solution.py:260
  23.0 4.3 %collective-permute-done.10.rows.s3 = bf16[400,128]{1,0:T(8,128)(2,1)S(1)} collective-permute-done((bf16[400,128]{1,0:T(8,128)(2,1)S(1)}, bf16[400,128]{1,0:T(8,128)(2,1)S(1)}, u32[]{:S(2)}, u32[]{:S(2)}) %collective-permute-start.10) | collective-permute-done | bytes 102432 | tf_op jit(solution)/shard_map/ppermute | solution.py:263
  27.2 2.3 %collective-permute-start.8 = (bf16[400,128]{1,0:T(8,128)(2,1)S(1)}, bf16[400,128]{1,0:T(8,128)(2,1)S(1)}, u32[]{:S(2)}, u32[]{:S(2)}) collective-permute-start(bf16[400,128]{1,0:T(8,128)(2,1)S(1)} %line.1.s0), channel_id=1, source_target_pairs={{0,16},{16,32},{32,48},{48,0},{1,17},{17,33},{33,49},{49,1},{2,18}... | collective-permute-start | bytes 307208 | tf_op jit(solution)/shard_map/ppermute | solution.py:262
  29.5 5.5 %collective-permute-done.8.rows.s1 = bf16[400,128]{1,0:T(8,128)(2,1)S(1)} collective-permute-done((bf16[400,128]{1,0:T(8,128)(2,1)S(1)}, bf16[400,128]{1,0:T(8,128)(2,1)S(1)}, u32[]{:S(2)}, u32[]{:S(2)}) %collective-permute-start.8) | collective-permute-done | bytes 102432 | tf_op jit(solution)/shard_map/ppermute | solution.py:262
  35.0 3.3 %collective-permute-start.11 = (bf16[976,128]{1,0:T(8,128)(2,1)S(1)}, bf16[976,128]{1,0:T(8,128)(2,1)S(1)}, u32[]{:S(2)}, u32[]{:S(2)}) collective-permute-start(bf16[976,128]{1,0:T(8,128)(2,1)S(1)} %relay.3), channel_id=1, source_target_pairs={{0,48},{16,0},{32,16},{48,32},{1,49},{17,1},{33,17},{49,33},{2,50}... | collective-permute-start | bytes 749576 | tf_op jit(solution)/shard_map/ppermute | solution.py:265
  38.4 1.0 %copy-done = bf16[2,6,128,128]{3,2,1,0:T(8,128)(2,1)S(1)} copy-done((bf16[2,6,128,128]{3,2,1,0:T(8,128)(2,1)S(1)}, bf16[2,6,128,128]{3,2,1,0:T(8,128)(2,1)}, u32[]{:S(2)}) %copy-start) | copy-done | bytes 393240
  39.5 0.9 collective-permute-done.1.t1
  40.4 10.4 %collective-permute-done.9.f1 = bf16[960,128]{1,0:T(8,128)(2,1)S(1)} collective-permute-done((bf16[960,128]{1,0:T(8,128)(2,1)S(1)}, bf16[960,128]{1,0:T(8,128)(2,1)S(1)}, u32[]{:S(2)}, u32[]{:S(2)}) %collective-permute-start.9) | collective-permute-done | bytes 245792 | tf_op jit(solution)/shard_map/ppermute | solution.py:264
  50.8 2.5 %build.1 = (bf16[1024,1664]{1,0:T(8,128)(2,1)S(1)}, bf16[1024,1664]{1,0:T(8,128)(2,1)S(1)}) custom-call(s32[5]{0:T(128)S(1)} %stack.23.sc_ref, bf16[1536,128]{1,0:T(8,128)(2,1)S(1)} %hold.1.t0, bf16[1536,128]{1,0:T(8,128)(2,1)S(1)} %collective-permute-done.1.t1, bf16[1536,128]{1,0:T(8,128)(2,1)S(1)} %collective-permute-done.2.t2, ...), custom_call_target="tpu_custom_call" | custom-call | tf_op jit(solution)/shard_map/build/pallas_call | solution.py:156
  53.4 2.9 %send.1 = f32[4,2,256,256]{3,2,1,0:T(8,128)S(1)} custom-call(s32[5]{0:T(128)S(1)} %stack.23.sc_ref, bf16[1024,1664]{1,0:T(8,128)(2,1)S(1)} %get-tuple-element.15.dy, bf16[1024,1664]{1,0:T(8,128)(2,1)S(1)} %get-tuple-element.16.dz), custom_call_target="tpu_custom_call" | custom-call | tf_op jit(solution)/shard_map/send/pallas_call | solution.py:193
  56.4 2.7 %keep.1 = f32[4,2,256,256]{3,2,1,0:T(8,128)S(1)} custom-call(s32[5]{0:T(128)S(1)} %stack.23.sc_ref, bf16[1024,1664]{1,0:T(8,128)(2,1)S(1)} %get-tuple-element.15.dy, bf16[1024,1664]{1,0:T(8,128)(2,1)S(1)} %get-tuple-element.16.dz), custom_call_target="tpu_custom_call" | custom-call | tf_op jit(solution)/shard_map/keep/pallas_call | solution.py:193
  59.1 1.4 %collective-permute-done.12.got = f32[4,2,256,256]{3,2,1,0:T(8,128)S(1)} collective-permute-done((f32[4,2,256,256]{3,2,1,0:T(8,128)S(1)}, f32[4,2,256,256]{3,2,1,0:T(8,128)S(1)}, u32[]{:S(2)}, u32[]{:S(2)}) %collective-permute-start.12) | collective-permute-done | bytes 2097184 | tf_op jit(solution)/shard_map/ppermute | solution.py:270
  60.5 0.7 share.1
  61.8 2.4 %collective-permute-start.14 = (bf16[256,256]{1,0:T(8,128)(2,1)S(1)}, bf16[256,256]{1,0:T(8,128)(2,1)S(1)}, u32[]{:S(2)}, u32[]{:S(2)}) collective-permute-start(bf16[256,256]{1,0:T(8,128)(2,1)S(1)} %get-tuple-element.19), channel_id=1, source_target_pairs={{0,8},{2,10},{4,12},{6,14},{8,0},{10,2},{12,4},{14,6},{1,9},{3,11}... | collective-permute-start | bytes 393224 | tf_op jit(solution)/shard_map/ppermute | solution.py:274
  64.3 4.6 %collective-permute-start.17 = (bf16[256,256]{1,0:T(8,128)(2,1)S(1)}, bf16[256,256]{1,0:T(8,128)(2,1)S(1)}, u32[]{:S(2)}, u32[]{:S(2)}) collective-permute-start(bf16[256,256]{1,0:T(8,128)(2,1)S(1)} %get-tuple-element.22), channel_id=1, source_target_pairs={{0,6},{2,4},{4,10},{6,8},{8,14},{10,12},{12,2},{14,0},{1,7},{3,5},... | collective-permute-start | bytes 393224 | tf_op jit(solution)/shard_map/ppermute | solution.py:274
  69.5 1.8 %collective-permute-start.19 = (bf16[256,256]{1,0:T(8,128)(2,1)S(1)}, bf16[256,256]{1,0:T(8,128)(2,1)S(1)}, u32[]{:S(2)}, u32[]{:S(2)}) collective-permute-start(bf16[256,256]{1,0:T(8,128)(2,1)S(1)} %get-tuple-element.24), channel_id=1, source_target_pairs={{0,14},{2,12},{4,2},{6,0},{8,6},{10,4},{12,10},{14,8},{1,15},{3,13... | collective-permute-start | bytes 393224 | tf_op jit(solution)/shard_map/ppermute | solution.py:274
  71.4 2.5 %collective-permute-done.17 = bf16[256,256]{1,0:T(8,128)(2,1)S(1)} collective-permute-done((bf16[256,256]{1,0:T(8,128)(2,1)S(1)}, bf16[256,256]{1,0:T(8,128)(2,1)S(1)}, u32[]{:S(2)}, u32[]{:S(2)}) %collective-permute-start.17) | collective-permute-done | bytes 131104 | tf_op jit(solution)/shard_map/ppermute | solution.py:274
  73.9 4.8 %collective-permute-done.18 = bf16[256,256]{1,0:T(8,128)(2,1)S(1)} collective-permute-done((bf16[256,256]{1,0:T(8,128)(2,1)S(1)}, bf16[256,256]{1,0:T(8,128)(2,1)S(1)}, u32[]{:S(2)}, u32[]{:S(2)}) %collective-permute-start.18) | collective-permute-done | bytes 131104 | tf_op jit(solution)/shard_map/ppermute | solution.py:274
  78.7 1.4 %collective-permute-done.19 = bf16[256,256]{1,0:T(8,128)(2,1)S(1)} collective-permute-done((bf16[256,256]{1,0:T(8,128)(2,1)S(1)}, bf16[256,256]{1,0:T(8,128)(2,1)S(1)}, u32[]{:S(2)}, u32[]{:S(2)}) %collective-permute-start.19) | collective-permute-done | bytes 131104 | tf_op jit(solution)/shard_map/ppermute | solution.py:274
  80.2 4.3 %collective-permute-start.20 = (f32[256,256]{1,0:T(8,128)S(1)}, f32[256,256]{1,0:T(8,128)S(1)}, u32[]{:S(2)}, u32[]{:S(2)}) collective-permute-start(f32[256,256]{1,0:T(8,128)S(1)} %convert_add_fusion), channel_id=1, source_target_pairs={{0,0},{1,16},{2,2},{3,48},{4,4},{5,20},{6,66},{7,52},{8,8},{9,24},... | collective-permute-start | bytes 786440 | tf_op jit(solution)/shard_map/ppermute | solution.py:275
  84.5 10.0 %collective-permute-done.20 = f32[256,256]{1,0:T(8,128)S(1)} collective-permute-done((f32[256,256]{1,0:T(8,128)S(1)}, f32[256,256]{1,0:T(8,128)S(1)}, u32[]{:S(2)}, u32[]{:S(2)}) %collective-permute-start.20) | collective-permute-done | bytes 262176 | tf_op jit(solution)/shard_map/ppermute | solution.py:275
  94.6 0.7 copy.7
  (29 shorter events, 2.6 us)
Async XLA Ops:
  0.0 27.2 %collective-permute-start = (bf16[1536,128]{1,0:T(8,128)(2,1)}, bf16[1536,128]{1,0:T(8,128)(2,1)S(1)}, u32[]{:S(2)}, u32[]{:S(2)}) collective-permute-start(bf16[1536,128]{1,0:T(8,128)(2,1)} %bitcast.7), channel_id=1, source_target_pairs={{0,48},{16,0},{32,16},{48,32},{1,49},{17,1},{33,17},{49,33},{2,50}... | collective-permute-start | bytes 1179656 | tf_op jit(solution)/shard_map/ppermute | solution.py:259
  5.4 32.9 %collective-permute-start.4 = (bf16[1536,128]{1,0:T(8,128)(2,1)}, bf16[1536,128]{1,0:T(8,128)(2,1)S(1)}, u32[]{:S(2)}, u32[]{:S(2)}) collective-permute-start(bf16[1536,128]{1,0:T(8,128)(2,1)} %bitcast.8), channel_id=1, source_target_pairs={{0,16},{16,32},{32,48},{48,0},{1,17},{17,33},{33,49},{49,1},{2,18}... | collective-permute-start | bytes 1179656 | tf_op jit(solution)/shard_map/ppermute | solution.py:258
  6.1 0.7 copy-start.1
  6.9 0.7 copy-start.2
  7.6 4.7 %collective-permute-start.7 = (bf16[104,128]{1,0:T(8,128)(2,1)S(1)}, bf16[104,128]{1,0:T(8,128)(2,1)S(1)}, u32[]{:S(2)}, u32[]{:S(2)}) collective-permute-start(bf16[104,128]{1,0:T(8,128)(2,1)S(1)} %pack.1.m0.p0), channel_id=1, source_target_pairs={{0,192},{64,0},{128,64},{192,128},{1,193},{65,1},{129,65},{193,129... | collective-permute-start | bytes 79880 | tf_op jit(solution)/shard_map/ppermute | solution.py:256
  10.7 5.4 %collective-permute-start.6 = (bf16[104,128]{1,0:T(8,128)(2,1)S(1)}, bf16[104,128]{1,0:T(8,128)(2,1)S(1)}, u32[]{:S(2)}, u32[]{:S(2)}) collective-permute-start(bf16[104,128]{1,0:T(8,128)(2,1)S(1)} %pack.1.m0.p0), channel_id=1, source_target_pairs={{0,128},{64,192},{128,0},{192,64},{1,129},{65,193},{129,1},{193,65... | collective-permute-start | bytes 79880 | tf_op jit(solution)/shard_map/ppermute | solution.py:256
  11.3 5.1 %collective-permute-start.5 = (bf16[104,128]{1,0:T(8,128)(2,1)S(1)}, bf16[104,128]{1,0:T(8,128)(2,1)S(1)}, u32[]{:S(2)}, u32[]{:S(2)}) collective-permute-start(bf16[104,128]{1,0:T(8,128)(2,1)S(1)} %pack.1.m0.p0), channel_id=1, source_target_pairs={{0,64},{64,128},{128,192},{192,0},{1,65},{65,129},{129,193},{193,1... | collective-permute-start | bytes 79880 | tf_op jit(solution)/shard_map/ppermute | solution.py:256
  16.9 10.3 %collective-permute-start.10 = (bf16[400,128]{1,0:T(8,128)(2,1)S(1)}, bf16[400,128]{1,0:T(8,128)(2,1)S(1)}, u32[]{:S(2)}, u32[]{:S(2)}) collective-permute-start(bf16[400,128]{1,0:T(8,128)(2,1)S(1)} %line.1.s0), channel_id=1, source_target_pairs={{0,48},{16,0},{32,16},{48,32},{1,49},{17,1},{33,17},{49,33},{2,50}... | collective-permute-start | bytes 307208 | tf_op jit(solution)/shard_map/ppermute | solution.py:263
  21.1 18.3 %collective-permute-start.3 = (bf16[1536,128]{1,0:T(8,128)(2,1)}, bf16[1536,128]{1,0:T(8,128)(2,1)S(1)}, u32[]{:S(2)}, u32[]{:S(2)}) collective-permute-start(bf16[1536,128]{1,0:T(8,128)(2,1)} %bitcast.9), channel_id=1, source_target_pairs={{0,192},{64,0},{128,64},{192,128},{1,193},{65,1},{129,65},{193,129... | collective-permute-start | bytes 1179656 | tf_op jit(solution)/shard_map/ppermute | solution.py:260
  21.6 17.8 %collective-permute-start.2 = (bf16[1536,128]{1,0:T(8,128)(2,1)}, bf16[1536,128]{1,0:T(8,128)(2,1)S(1)}, u32[]{:S(2)}, u32[]{:S(2)}) collective-permute-start(bf16[1536,128]{1,0:T(8,128)(2,1)} %bitcast.10), channel_id=1, source_target_pairs={{0,128},{64,192},{128,0},{192,64},{1,129},{65,193},{129,1},{193,65... | collective-permute-start | bytes 1179656 | tf_op jit(solution)/shard_map/ppermute | solution.py:260
  27.2 13.2 %collective-permute-start.1 = (bf16[1536,128]{1,0:T(8,128)(2,1)}, bf16[1536,128]{1,0:T(8,128)(2,1)S(1)}, u32[]{:S(2)}, u32[]{:S(2)}) collective-permute-start(bf16[1536,128]{1,0:T(8,128)(2,1)} %bitcast.11), channel_id=1, source_target_pairs={{0,64},{64,128},{128,192},{192,0},{1,65},{65,129},{129,193},{193,1... | collective-permute-start | bytes 1179656 | tf_op jit(solution)/shard_map/ppermute | solution.py:260
  27.2 7.8 %collective-permute-start.8 = (bf16[400,128]{1,0:T(8,128)(2,1)S(1)}, bf16[400,128]{1,0:T(8,128)(2,1)S(1)}, u32[]{:S(2)}, u32[]{:S(2)}) collective-permute-start(bf16[400,128]{1,0:T(8,128)(2,1)S(1)} %line.1.s0), channel_id=1, source_target_pairs={{0,16},{16,32},{32,48},{48,0},{1,17},{17,33},{33,49},{49,1},{2,18}... | collective-permute-start | bytes 307208 | tf_op jit(solution)/shard_map/ppermute | solution.py:262
  35.0 15.8 %collective-permute-start.11 = (bf16[976,128]{1,0:T(8,128)(2,1)S(1)}, bf16[976,128]{1,0:T(8,128)(2,1)S(1)}, u32[]{:S(2)}, u32[]{:S(2)}) collective-permute-start(bf16[976,128]{1,0:T(8,128)(2,1)S(1)} %relay.3), channel_id=1, source_target_pairs={{0,48},{16,0},{32,16},{48,32},{1,49},{17,1},{33,17},{49,33},{2,50}... | collective-permute-start | bytes 749576 | tf_op jit(solution)/shard_map/ppermute | solution.py:265
  38.3 12.5 %collective-permute-start.9 = (bf16[960,128]{1,0:T(8,128)(2,1)S(1)}, bf16[960,128]{1,0:T(8,128)(2,1)S(1)}, u32[]{:S(2)}, u32[]{:S(2)}) collective-permute-start(bf16[960,128]{1,0:T(8,128)(2,1)S(1)} %relay.2), channel_id=1, source_target_pairs={{0,16},{16,32},{32,48},{48,0},{1,17},{17,33},{33,49},{49,1},{2,18}... | collective-permute-start | bytes 737288 | tf_op jit(solution)/shard_map/ppermute | solution.py:264
  38.4 1.0 %copy-start = (bf16[2,6,128,128]{3,2,1,0:T(8,128)(2,1)S(1)}, bf16[2,6,128,128]{3,2,1,0:T(8,128)(2,1)}, u32[]{:S(2)}) copy-start(bf16[2,6,128,128]{3,2,1,0:T(8,128)(2,1)} %param.4) | copy-start | bytes 1179652
  56.3 4.2 %collective-permute-start.12 = (f32[4,2,256,256]{3,2,1,0:T(8,128)S(1)}, f32[4,2,256,256]{3,2,1,0:T(8,128)S(1)}, u32[]{:S(2)}, u32[]{:S(2)}) collective-permute-start(f32[4,2,256,256]{3,2,1,0:T(8,128)S(1)} %send.1), channel_id=1, source_target_pairs={{0,1},{1,0},{2,3},{3,2},{4,5},{5,4},{6,7},{7,6},{8,9},{9,8},{10,11... | collective-permute-start | bytes 6291464 | tf_op jit(solution)/shard_map/ppermute | solution.py:270
  61.3 7.7 %collective-permute-start.13 = (bf16[256,256]{1,0:T(8,128)(2,1)S(1)}, bf16[256,256]{1,0:T(8,128)(2,1)S(1)}, u32[]{:S(2)}, u32[]{:S(2)}) collective-permute-start(bf16[256,256]{1,0:T(8,128)(2,1)S(1)} %get-tuple-element.18), channel_id=1, source_target_pairs={{0,4},{2,6},{4,8},{6,10},{8,12},{10,14},{12,0},{14,2},{1,5},{3,7},... | collective-permute-start | bytes 393224 | tf_op jit(solution)/shard_map/ppermute | solution.py:274
  61.8 7.7 %collective-permute-start.14 = (bf16[256,256]{1,0:T(8,128)(2,1)S(1)}, bf16[256,256]{1,0:T(8,128)(2,1)S(1)}, u32[]{:S(2)}, u32[]{:S(2)}) collective-permute-start(bf16[256,256]{1,0:T(8,128)(2,1)S(1)} %get-tuple-element.19), channel_id=1, source_target_pairs={{0,8},{2,10},{4,12},{6,14},{8,0},{10,2},{12,4},{14,6},{1,9},{3,11}... | collective-permute-start | bytes 393224 | tf_op jit(solution)/shard_map/ppermute | solution.py:274
  64.3 7.1 %collective-permute-start.15 = (bf16[256,256]{1,0:T(8,128)(2,1)S(1)}, bf16[256,256]{1,0:T(8,128)(2,1)S(1)}, u32[]{:S(2)}, u32[]{:S(2)}) collective-permute-start(bf16[256,256]{1,0:T(8,128)(2,1)S(1)} %get-tuple-element.20), channel_id=1, source_target_pairs={{0,12},{2,14},{4,0},{6,2},{8,4},{10,6},{12,8},{14,10},{1,13},{3,15... | collective-permute-start | bytes 393224 | tf_op jit(solution)/shard_map/ppermute | solution.py:274
  64.3 7.1 %collective-permute-start.16 = (bf16[256,256]{1,0:T(8,128)(2,1)S(1)}, bf16[256,256]{1,0:T(8,128)(2,1)S(1)}, u32[]{:S(2)}, u32[]{:S(2)}) collective-permute-start(bf16[256,256]{1,0:T(8,128)(2,1)S(1)} %get-tuple-element.21), channel_id=1, source_target_pairs={{0,2},{2,0},{4,6},{6,4},{8,10},{10,8},{12,14},{14,12},{1,3},{3,1},... | collective-permute-start | bytes 393224 | tf_op jit(solution)/shard_map/ppermute | solution.py:274
  64.3 9.6 %collective-permute-start.17 = (bf16[256,256]{1,0:T(8,128)(2,1)S(1)}, bf16[256,256]{1,0:T(8,128)(2,1)S(1)}, u32[]{:S(2)}, u32[]{:S(2)}) collective-permute-start(bf16[256,256]{1,0:T(8,128)(2,1)S(1)} %get-tuple-element.22), channel_id=1, source_target_pairs={{0,6},{2,4},{4,10},{6,8},{8,14},{10,12},{12,2},{14,0},{1,7},{3,5},... | collective-permute-start | bytes 393224 | tf_op jit(solution)/shard_map/ppermute | solution.py:274
  69.0 9.7 %collective-permute-start.18 = (bf16[256,256]{1,0:T(8,128)(2,1)S(1)}, bf16[256,256]{1,0:T(8,128)(2,1)S(1)}, u32[]{:S(2)}, u32[]{:S(2)}) collective-permute-start(bf16[256,256]{1,0:T(8,128)(2,1)S(1)} %get-tuple-element.23), channel_id=1, source_target_pairs={{0,10},{2,8},{4,14},{6,12},{8,2},{10,0},{12,6},{14,4},{1,11},{3,9}... | collective-permute-start | bytes 393224 | tf_op jit(solution)/shard_map/ppermute | solution.py:274
  69.5 10.6 %collective-permute-start.19 = (bf16[256,256]{1,0:T(8,128)(2,1)S(1)}, bf16[256,256]{1,0:T(8,128)(2,1)S(1)}, u32[]{:S(2)}, u32[]{:S(2)}) collective-permute-start(bf16[256,256]{1,0:T(8,128)(2,1)S(1)} %get-tuple-element.24), channel_id=1, source_target_pairs={{0,14},{2,12},{4,2},{6,0},{8,6},{10,4},{12,10},{14,8},{1,15},{3,13... | collective-permute-start | bytes 393224 | tf_op jit(solution)/shard_map/ppermute | solution.py:274
  80.2 14.4 %collective-permute-start.20 = (f32[256,256]{1,0:T(8,128)S(1)}, f32[256,256]{1,0:T(8,128)S(1)}, u32[]{:S(2)}, u32[]{:S(2)}) collective-permute-start(f32[256,256]{1,0:T(8,128)S(1)} %convert_add_fusion), channel_id=1, source_target_pairs={{0,0},{1,16},{2,2},{3,48},{4,4},{5,20},{6,66},{7,52},{8,8},{9,24},... | collective-permute-start | bytes 786440 | tf_op jit(solution)/shard_map/ppermute | solution.py:275

commit v8 on v2

--- a/solution.py
+++ b/solution.py
@@ -160,24 +160,24 @@
         fill(f1, 0, met, ls, NA * opposite, far, 0)
         fill(f3, 0, met, ls, NA * opposite + 1, far, BS)
 
+    def product(h, swapped, block):
+        for q in range(4):
+            row = dy[q * ROWS : (q + 1) * ROWS, 0:USED]
+            pair = (block, row) if swapped else (row, block)
+            prod = lax.dot_general(*pair, (((1,), (1,)), ((), ())), preferred_element_type=F32)
+            out[q, h] = prod * factor
+
     for h in range(2):
         p = 2 * h + parity
 
-        def product(rhs):
-            for q in range(4):
-                lhs = dy[q * ROWS : (q + 1) * ROWS, 0:USED]
-                prod = lax.dot_general(
-                    lhs, rhs, (((1,), (1,)), ((), ())), preferred_element_type=F32
-                )
-                out[q, h] = prod * factor
-
         @pl.when(p == opposite)
         def _():
-            product(far[:, 0:USED])
+            product(h, True, far[:, 0:USED])
 
         @pl.when(p != opposite)
         def _():
-            product(dz[pl.ds(pl.multiple_of(p * ROWS, ROWS), ROWS), 0:USED])
+            at = pl.multiple_of(p * ROWS, ROWS)
+            product(h, False, dz[pl.ds(at, ROWS), 0:USED])
 
 
 def gram(flip, sc, dy, dz, met, f1, f3, small):
@@ -197,6 +197,21 @@
     )(sc, dy, dz, met, f1, f3, small)
 
 
+def hold_kernel(tiles, late, out):
+    out[...] = tiles[...]
+
+
+def hold(tiles, late):
+    return pl.pallas_call(
+        hold_kernel,
+        out_shape=jax.ShapeDtypeStruct(tiles.shape, tiles.dtype),
+        in_specs=[VMEM] * 2,
+        out_specs=VMEM,
+        compiler_params=PARAMS,
+        name="hold",
+    )(tiles, late)
+
+
 STEPS = tuple((k, w) for w in range(2) for k in range(4))
 
 
@@ -221,6 +236,15 @@
 
 def hop(k, w):
     return [(2 * a + b, 2 * ((a + k) % 4) + (b + w) % 2) for a in range(4) for b in range(2)]
+
+
+def homes():
+    moves = []
+    for n in range(256):
+        y, z, x, p = n // 64, n // 16 % 4, n // 4 % 4, n % 4
+        home = (x, z, y, p) if p == (z + 2) % 4 else (y, p, x, z)
+        moves.append((n, home[0] * 64 + home[1] * 16 + home[2] * 4 + home[3]))
+    return moves
 
 
 def local(fit_tiles, aux_list, aux_count, metric):
@@ -236,15 +260,14 @@
     f1 = lax.ppermute(z1[:HALF], "zh", ring(4, 1))
     f3 = lax.ppermute(z3[HALF:], "zh", ring(4, 3))
 
-    dy, dz, met = build(sc, ys, [z1, z3], smalls)
+    dy, dz, met = build(sc, [hold(tiles, z3)] + ys[1:], [z1, z3], smalls)
     send = gram(True, sc, dy, dz, met, f1, f3, small)
     got = lax.ppermute(send, "co", ring(2, 1))
     keep = gram(False, sc, dy, dz, met, f1, f3, small)
     total, *shares = share(sc, keep, got)
     for (k, w), piece in zip(STEPS[1:], shares):
         total = total + lax.ppermute(piece, ("x", "zl"), hop(k, w)).astype(F32)
-    swap = [(a * 4 + b, b * 4 + a) for a in range(4) for b in range(4)]
-    return lax.ppermute(total, ("zh", "zl", "co"), swap)
+    return lax.ppermute(total, ("y", "zh", "x", "zl", "co"), homes())
 
 
 def solution(mesh):

time: 110 us -> 108 us (0.982)
  the two profiles are of different devices: /device:TPU:32 before, /device:TPU:39 now
where the time goes in v8:
time: 108 us
  starting transfers between devices  53 us (49%)
  waiting for transfers between devices  40.2 us (37%)
  Pallas kernels  10.8 us (10%)
  local copies, waits for them, and re-layouts  3.97 us (4%)
    ppermute x3, waiting for transfers between devices, local(): smalls = [small] + [lax.ppermute(small, 'y', ring(4, k)) for k in (1, 2, 3)]  13.3 us
    ppermute x3, waiting for transfers between devices, local(): parts = [part] + [lax.ppermute(part, 'zh', ring(4, k)) for k in (1, 2, 3)]  10.9 us
    ppermute x1, starting transfers between devices, local(): return lax.ppermute(total, ('y', 'zh', 'x', 'zl', 'co'), homes())  10.2 us
    ppermute x7, starting transfers between devices, local(): total = total + lax.ppermute(piece, ('x', 'zl'), hop(k, w)).astype(F32)  9.3 us
    ppermute x7, waiting for transfers between devices, local(): total = total + lax.ppermute(piece, ('x', 'zl'), hop(k, w)).astype(F32)  7.92 us
    ppermute x1, waiting for transfers between devices, local(): return lax.ppermute(total, ('y', 'zh', 'x', 'zl', 'co'), homes())  6.85 us
    ppermute x3, starting transfers between devices, local(): parts = [part] + [lax.ppermute(part, 'zh', ring(4, k)) for k in (1, 2, 3)]  6.84 us
    ppermute x3, starting transfers between devices, local(): smalls = [small] + [lax.ppermute(small, 'y', ring(4, k)) for k in (1, 2, 3)]  6.38 us
  transfers between devices with their start and end apart: 22, of which 11 were waited for; matrix products, arithmetic and copies ran while one was open for 1% of the time, Pallas kernels for 6%

profile of v8, /device:TPU:39, one launch (start us, length us, event | category | flops | bytes accessed | tf_op | source)
XLA Modules:
  0.0 108.2 jit_solution(1236444809065688280)
XLA Ops:
  0.0 3.0 %collective-permute-start.4 = (bf16[1536,128]{1,0:T(8,128)(2,1)}, bf16[1536,128]{1,0:T(8,128)(2,1)S(1)}, u32[]{:S(2)}, u32[]{:S(2)}) collective-permute-start(bf16[1536,128]{1,0:T(8,128)(2,1)} %bitcast.7), channel_id=1, source_target_pairs={{0,16},{16,32},{32,48},{48,0},{1,17},{17,33},{33,49},{49,1},{2,18}... | collective-permute-start | bytes 1179656 | tf_op jit(solution)/shard_map/ppermute | solution.py:255
  3.0 2.1 %collective-permute-start = (bf16[1536,128]{1,0:T(8,128)(2,1)}, bf16[1536,128]{1,0:T(8,128)(2,1)S(1)}, u32[]{:S(2)}, u32[]{:S(2)}) collective-permute-start(bf16[1536,128]{1,0:T(8,128)(2,1)} %bitcast.8), channel_id=1, source_target_pairs={{0,48},{16,0},{32,16},{48,32},{1,49},{17,1},{33,17},{49,33},{2,50}... | collective-permute-start | bytes 1179656 | tf_op jit(solution)/shard_map/ppermute | solution.py:256
  5.1 0.7 copy.5.counts
  5.9 0.7 copy-done.1
  7.4 2.4 %collective-permute-start.7 = (bf16[104,128]{1,0:T(8,128)(2,1)S(1)}, bf16[104,128]{1,0:T(8,128)(2,1)S(1)}, u32[]{:S(2)}, u32[]{:S(2)}) collective-permute-start(bf16[104,128]{1,0:T(8,128)(2,1)S(1)} %pack.1.m0), channel_id=1, source_target_pairs={{0,48},{16,0},{32,16},{48,32},{1,49},{17,1},{33,17},{49,33},{2,50}... | collective-permute-start | bytes 79880 | tf_op jit(solution)/shard_map/ppermute | solution.py:253
  9.7 2.2 %collective-permute-start.6 = (bf16[104,128]{1,0:T(8,128)(2,1)S(1)}, bf16[104,128]{1,0:T(8,128)(2,1)S(1)}, u32[]{:S(2)}, u32[]{:S(2)}) collective-permute-start(bf16[104,128]{1,0:T(8,128)(2,1)S(1)} %pack.1.m0), channel_id=1, source_target_pairs={{0,32},{16,48},{32,0},{48,16},{1,33},{17,49},{33,1},{49,17},{2,34}... | collective-permute-start | bytes 79880 | tf_op jit(solution)/shard_map/ppermute | solution.py:253
  11.9 2.3 %collective-permute-start.5 = (bf16[104,128]{1,0:T(8,128)(2,1)S(1)}, bf16[104,128]{1,0:T(8,128)(2,1)S(1)}, u32[]{:S(2)}, u32[]{:S(2)}) collective-permute-start(bf16[104,128]{1,0:T(8,128)(2,1)S(1)} %pack.1.m0), channel_id=1, source_target_pairs={{0,16},{16,32},{32,48},{48,0},{1,17},{17,33},{33,49},{49,1},{2,18}... | collective-permute-start | bytes 79880 | tf_op jit(solution)/shard_map/ppermute | solution.py:253
  14.3 4.1 %collective-permute-done.7.m3 = bf16[104,128]{1,0:T(8,128)(2,1)S(1)} collective-permute-done((bf16[104,128]{1,0:T(8,128)(2,1)S(1)}, bf16[104,128]{1,0:T(8,128)(2,1)S(1)}, u32[]{:S(2)}, u32[]{:S(2)}) %collective-permute-start.7) | collective-permute-done | bytes 26656 | tf_op jit(solution)/shard_map/ppermute | solution.py:253
  18.4 4.9 %collective-permute-done.6.m2 = bf16[104,128]{1,0:T(8,128)(2,1)S(1)} collective-permute-done((bf16[104,128]{1,0:T(8,128)(2,1)S(1)}, bf16[104,128]{1,0:T(8,128)(2,1)S(1)}, u32[]{:S(2)}, u32[]{:S(2)}) %collective-permute-start.6) | collective-permute-done | bytes 26656 | tf_op jit(solution)/shard_map/ppermute | solution.py:253
  23.3 1.9 %collective-permute-done.5.m1 = bf16[104,128]{1,0:T(8,128)(2,1)S(1)} collective-permute-done((bf16[104,128]{1,0:T(8,128)(2,1)S(1)}, bf16[104,128]{1,0:T(8,128)(2,1)S(1)}, u32[]{:S(2)}, u32[]{:S(2)}) %collective-permute-start.5) | collective-permute-done | bytes 26656 | tf_op jit(solution)/shard_map/ppermute | solution.py:253
  25.8 2.8 %collective-permute-start.10 = (bf16[400,128]{1,0:T(8,128)(2,1)S(1)}, bf16[400,128]{1,0:T(8,128)(2,1)S(1)}, u32[]{:S(2)}, u32[]{:S(2)}) collective-permute-start(bf16[400,128]{1,0:T(8,128)(2,1)S(1)} %line.1.s0), channel_id=1, source_target_pairs={{0,192},{64,0},{128,64},{192,128},{1,193},{65,1},{129,65},{193,129... | collective-permute-start | bytes 307208 | tf_op jit(solution)/shard_map/ppermute | solution.py:259
  29.1 1.2 %collective-permute-done.10.s3 = bf16[400,128]{1,0:T(8,128)(2,1)S(1)} collective-permute-done((bf16[400,128]{1,0:T(8,128)(2,1)S(1)}, bf16[400,128]{1,0:T(8,128)(2,1)S(1)}, u32[]{:S(2)}, u32[]{:S(2)}) %collective-permute-start.10) | collective-permute-done | bytes 102432 | tf_op jit(solution)/shard_map/ppermute | solution.py:259
  30.9 3.6 %collective-permute-start.9 = (bf16[400,128]{1,0:T(8,128)(2,1)S(1)}, bf16[400,128]{1,0:T(8,128)(2,1)S(1)}, u32[]{:S(2)}, u32[]{:S(2)}) collective-permute-start(bf16[400,128]{1,0:T(8,128)(2,1)S(1)} %line.1.s0), channel_id=1, source_target_pairs={{0,128},{64,192},{128,0},{192,64},{1,129},{65,193},{129,1},{193,65... | collective-permute-start | bytes 307208 | tf_op jit(solution)/shard_map/ppermute | solution.py:259
  34.5 12.1 %collective-permute-done.9.s2 = bf16[400,128]{1,0:T(8,128)(2,1)S(1)} collective-permute-done((bf16[400,128]{1,0:T(8,128)(2,1)S(1)}, bf16[400,128]{1,0:T(8,128)(2,1)S(1)}, u32[]{:S(2)}, u32[]{:S(2)}) %collective-permute-start.9) | collective-permute-done | bytes 102432 | tf_op jit(solution)/shard_map/ppermute | solution.py:259
  46.7 4.3 %collective-permute-start.11 = (bf16[768,128]{1,0:T(8,128)(2,1)S(1)}, bf16[768,128]{1,0:T(8,128)(2,1)S(1)}, u32[]{:S(2)}, u32[]{:S(2)}) collective-permute-start(bf16[768,128]{1,0:T(8,128)(2,1)S(1)} %slice.8), channel_id=1, source_target_pairs={{0,16},{16,32},{32,48},{48,0},{1,17},{17,33},{33,49},{49,1},{2,18}... | collective-permute-start | bytes 589832 | tf_op jit(solution)/shard_map/ppermute | solution.py:260
  51.0 5.4 %collective-permute-start.12 = (bf16[768,128]{1,0:T(8,128)(2,1)S(1)}, bf16[768,128]{1,0:T(8,128)(2,1)S(1)}, u32[]{:S(2)}, u32[]{:S(2)}) collective-permute-start(bf16[768,128]{1,0:T(8,128)(2,1)S(1)} %slice.9), channel_id=1, source_target_pairs={{0,48},{16,0},{32,16},{48,32},{1,49},{17,1},{33,17},{49,33},{2,50}... | collective-permute-start | bytes 589832 | tf_op jit(solution)/shard_map/ppermute | solution.py:261
  56.4 1.0 copy-done
  57.5 3.0 %build.1 = (bf16[1024,1664]{1,0:T(8,128)(2,1)S(1)}, bf16[1024,1664]{1,0:T(8,128)(2,1)S(1)}, bf16[13,128,128]{2,1,0:T(8,128)(2,1)S(1)}) custom-call(s32[5]{0:T(128)S(1)} %stack.23.sc_ref, bf16[1536,128]{1,0:T(8,128)(2,1)S(1)} %hold.1.t0, bf16[1536,128]{1,0:T(8,128)(2,1)S(1)} %collective-permute-done.1.t1, bf16[1536,128]{1,0:T(8,128)(2,1)S(1)} %collective-permute-done.2.t2, ...), custom_call_target="tpu_custom_call" | custom-call | tf_op jit(solution)/shard_map/build/pallas_call | solution.py:132
  60.5 3.8 %send.1 = f32[4,2,256,256]{3,2,1,0:T(8,128)S(1)} custom-call(s32[5]{0:T(128)S(1)} %stack.23.sc_ref, bf16[1024,1664]{1,0:T(8,128)(2,1)S(1)} %get-tuple-element.16.dy, bf16[1024,1664]{1,0:T(8,128)(2,1)S(1)} %get-tuple-element.17.dz, bf16[13,128,128]{2,1,0:T(8,128)(2,1)S(1)} %get-tuple-element.18.met, bf16[768,128]{1,0:T(8,128)(2,1)S(1)} %collective-permute-done.11.f1, ...), custom_call_target="tpu_custom_call" | custom-call | tf_op jit(solution)/shard_map/send/pallas_call | solution.py:184
  64.3 4.3 %collective-permute-start.13 = (f32[4,2,256,256]{3,2,1,0:T(8,128)S(1)}, f32[4,2,256,256]{3,2,1,0:T(8,128)S(1)}, u32[]{:S(2)}, u32[]{:S(2)}) collective-permute-start(f32[4,2,256,256]{3,2,1,0:T(8,128)S(1)} %send.1), channel_id=1, source_target_pairs={{0,1},{1,0},{2,3},{3,2},{4,5},{5,4},{6,7},{7,6},{8,9},{9,8},{10,11... | collective-permute-start | bytes 6291464 | tf_op jit(solution)/shard_map/ppermute | solution.py:265
  68.6 2.6 %keep.1 = f32[4,2,256,256]{3,2,1,0:T(8,128)S(1)} custom-call(s32[5]{0:T(128)S(1)} %stack.23.sc_ref, bf16[1024,1664]{1,0:T(8,128)(2,1)S(1)} %get-tuple-element.16.dy, bf16[1024,1664]{1,0:T(8,128)(2,1)S(1)} %get-tuple-element.17.dz, bf16[13,128,128]{2,1,0:T(8,128)(2,1)S(1)} %get-tuple-element.18.met, bf16[768,128]{1,0:T(8,128)(2,1)S(1)} %collective-permute-done.11.f1, ...), custom_call_target="tpu_custom_call" | custom-call | tf_op jit(solution)/shard_map/keep/pallas_call | solution.py:184
  71.2 1.2 %collective-permute-done.13.got = f32[4,2,256,256]{3,2,1,0:T(8,128)S(1)} collective-permute-done((f32[4,2,256,256]{3,2,1,0:T(8,128)S(1)}, f32[4,2,256,256]{3,2,1,0:T(8,128)S(1)}, u32[]{:S(2)}, u32[]{:S(2)}) %collective-permute-start.13) | collective-permute-done | bytes 2097184 | tf_op jit(solution)/shard_map/ppermute | solution.py:265
  73.4 2.1 %collective-permute-start.15 = (bf16[256,256]{1,0:T(8,128)(2,1)S(1)}, bf16[256,256]{1,0:T(8,128)(2,1)S(1)}, u32[]{:S(2)}, u32[]{:S(2)}) collective-permute-start(bf16[256,256]{1,0:T(8,128)(2,1)S(1)} %get-tuple-element.21), channel_id=1, source_target_pairs={{0,8},{2,10},{4,12},{6,14},{8,0},{10,2},{12,4},{14,6},{1,9},{3,11}... | collective-permute-start | bytes 393224 | tf_op jit(solution)/shard_map/ppermute | solution.py:269
  75.5 1.4 %collective-permute-start.17 = (bf16[256,256]{1,0:T(8,128)(2,1)S(1)}, bf16[256,256]{1,0:T(8,128)(2,1)S(1)}, u32[]{:S(2)}, u32[]{:S(2)}) collective-permute-start(bf16[256,256]{1,0:T(8,128)(2,1)S(1)} %get-tuple-element.23), channel_id=1, source_target_pairs={{0,2},{2,0},{4,6},{6,4},{8,10},{10,8},{12,14},{14,12},{1,3},{3,1},... | collective-permute-start | bytes 393224 | tf_op jit(solution)/shard_map/ppermute | solution.py:269
  77.0 2.4 %collective-permute-start.18 = (bf16[256,256]{1,0:T(8,128)(2,1)S(1)}, bf16[256,256]{1,0:T(8,128)(2,1)S(1)}, u32[]{:S(2)}, u32[]{:S(2)}) collective-permute-start(bf16[256,256]{1,0:T(8,128)(2,1)S(1)} %get-tuple-element.24), channel_id=1, source_target_pairs={{0,6},{2,4},{4,10},{6,8},{8,14},{10,12},{12,2},{14,0},{1,7},{3,5},... | collective-permute-start | bytes 393224 | tf_op jit(solution)/shard_map/ppermute | solution.py:269
  79.4 0.8 collective-permute-start.19
  80.2 2.3 %collective-permute-start.20 = (bf16[256,256]{1,0:T(8,128)(2,1)S(1)}, bf16[256,256]{1,0:T(8,128)(2,1)S(1)}, u32[]{:S(2)}, u32[]{:S(2)}) collective-permute-start(bf16[256,256]{1,0:T(8,128)(2,1)S(1)} %get-tuple-element.26), channel_id=1, source_target_pairs={{0,14},{2,12},{4,2},{6,0},{8,6},{10,4},{12,10},{14,8},{1,15},{3,13... | collective-permute-start | bytes 393224 | tf_op jit(solution)/shard_map/ppermute | solution.py:269
  82.6 0.8 collective-permute-done.18
  83.4 3.7 %collective-permute-done.19 = bf16[256,256]{1,0:T(8,128)(2,1)S(1)} collective-permute-done((bf16[256,256]{1,0:T(8,128)(2,1)S(1)}, bf16[256,256]{1,0:T(8,128)(2,1)S(1)}, u32[]{:S(2)}, u32[]{:S(2)}) %collective-permute-start.19) | collective-permute-done | bytes 131104 | tf_op jit(solution)/shard_map/ppermute | solution.py:269
  87.1 3.2 %collective-permute-done.20 = bf16[256,256]{1,0:T(8,128)(2,1)S(1)} collective-permute-done((bf16[256,256]{1,0:T(8,128)(2,1)S(1)}, bf16[256,256]{1,0:T(8,128)(2,1)S(1)}, u32[]{:S(2)}, u32[]{:S(2)}) %collective-permute-start.20) | collective-permute-done | bytes 131104 | tf_op jit(solution)/shard_map/ppermute | solution.py:269
  90.5 10.2 %collective-permute-start.21 = (f32[256,256]{1,0:T(8,128)S(1)}, f32[256,256]{1,0:T(8,128)S(1)}, u32[]{:S(2)}, u32[]{:S(2)}) collective-permute-start(f32[256,256]{1,0:T(8,128)S(1)} %convert_add_fusion), channel_id=1, source_target_pairs={{0,0},{1,16},{2,2},{3,48},{4,4},{5,20},{6,66},{7,52},{8,8},{9,24},... | collective-permute-start | bytes 786440 | tf_op jit(solution)/shard_map/ppermute | solution.py:270
  100.6 6.8 %collective-permute-done.21 = f32[256,256]{1,0:T(8,128)S(1)} collective-permute-done((f32[256,256]{1,0:T(8,128)S(1)}, f32[256,256]{1,0:T(8,128)S(1)}, u32[]{:S(2)}, u32[]{:S(2)}) %collective-permute-start.21) | collective-permute-done | bytes 262176 | tf_op jit(solution)/shard_map/ppermute | solution.py:270
  (31 shorter events, 4.6 us)
Async XLA Ops:
  0.0 30.9 %collective-permute-start.4 = (bf16[1536,128]{1,0:T(8,128)(2,1)}, bf16[1536,128]{1,0:T(8,128)(2,1)S(1)}, u32[]{:S(2)}, u32[]{:S(2)}) collective-permute-start(bf16[1536,128]{1,0:T(8,128)(2,1)} %bitcast.7), channel_id=1, source_target_pairs={{0,16},{16,32},{32,48},{48,0},{1,17},{17,33},{33,49},{49,1},{2,18}... | collective-permute-start | bytes 1179656 | tf_op jit(solution)/shard_map/ppermute | solution.py:255
  3.0 31.5 %collective-permute-start = (bf16[1536,128]{1,0:T(8,128)(2,1)}, bf16[1536,128]{1,0:T(8,128)(2,1)S(1)}, u32[]{:S(2)}, u32[]{:S(2)}) collective-permute-start(bf16[1536,128]{1,0:T(8,128)(2,1)} %bitcast.8), channel_id=1, source_target_pairs={{0,48},{16,0},{32,16},{48,32},{1,49},{17,1},{33,17},{49,33},{2,50}... | collective-permute-start | bytes 1179656 | tf_op jit(solution)/shard_map/ppermute | solution.py:256
  5.9 0.7 copy-start.1
  6.6 0.7 copy-start.2
  7.4 11.1 %collective-permute-start.7 = (bf16[104,128]{1,0:T(8,128)(2,1)S(1)}, bf16[104,128]{1,0:T(8,128)(2,1)S(1)}, u32[]{:S(2)}, u32[]{:S(2)}) collective-permute-start(bf16[104,128]{1,0:T(8,128)(2,1)S(1)} %pack.1.m0), channel_id=1, source_target_pairs={{0,48},{16,0},{32,16},{48,32},{1,49},{17,1},{33,17},{49,33},{2,50}... | collective-permute-start | bytes 79880 | tf_op jit(solution)/shard_map/ppermute | solution.py:253
  9.7 13.5 %collective-permute-start.6 = (bf16[104,128]{1,0:T(8,128)(2,1)S(1)}, bf16[104,128]{1,0:T(8,128)(2,1)S(1)}, u32[]{:S(2)}, u32[]{:S(2)}) collective-permute-start(bf16[104,128]{1,0:T(8,128)(2,1)S(1)} %pack.1.m0), channel_id=1, source_target_pairs={{0,32},{16,48},{32,0},{48,16},{1,33},{17,49},{33,1},{49,17},{2,34}... | collective-permute-start | bytes 79880 | tf_op jit(solution)/shard_map/ppermute | solution.py:253
  11.9 13.2 %collective-permute-start.5 = (bf16[104,128]{1,0:T(8,128)(2,1)S(1)}, bf16[104,128]{1,0:T(8,128)(2,1)S(1)}, u32[]{:S(2)}, u32[]{:S(2)}) collective-permute-start(bf16[104,128]{1,0:T(8,128)(2,1)S(1)} %pack.1.m0), channel_id=1, source_target_pairs={{0,16},{16,32},{32,48},{48,0},{1,17},{17,33},{33,49},{49,1},{2,18}... | collective-permute-start | bytes 79880 | tf_op jit(solution)/shard_map/ppermute | solution.py:253
  25.8 4.5 %collective-permute-start.10 = (bf16[400,128]{1,0:T(8,128)(2,1)S(1)}, bf16[400,128]{1,0:T(8,128)(2,1)S(1)}, u32[]{:S(2)}, u32[]{:S(2)}) collective-permute-start(bf16[400,128]{1,0:T(8,128)(2,1)S(1)} %line.1.s0), channel_id=1, source_target_pairs={{0,192},{64,0},{128,64},{192,128},{1,193},{65,1},{129,65},{193,129... | collective-permute-start | bytes 307208 | tf_op jit(solution)/shard_map/ppermute | solution.py:259
  28.6 28.9 %collective-permute-start.3 = (bf16[1536,128]{1,0:T(8,128)(2,1)}, bf16[1536,128]{1,0:T(8,128)(2,1)S(1)}, u32[]{:S(2)}, u32[]{:S(2)}) collective-permute-start(bf16[1536,128]{1,0:T(8,128)(2,1)} %bitcast.9), channel_id=1, source_target_pairs={{0,192},{64,0},{128,64},{192,128},{1,193},{65,1},{129,65},{193,129... | collective-permute-start | bytes 1179656 | tf_op jit(solution)/shard_map/ppermute | solution.py:257
  29.0 28.4 %collective-permute-start.2 = (bf16[1536,128]{1,0:T(8,128)(2,1)}, bf16[1536,128]{1,0:T(8,128)(2,1)S(1)}, u32[]{:S(2)}, u32[]{:S(2)}) collective-permute-start(bf16[1536,128]{1,0:T(8,128)(2,1)} %bitcast.10), channel_id=1, source_target_pairs={{0,128},{64,192},{128,0},{192,64},{1,129},{65,193},{129,1},{193,65... | collective-permute-start | bytes 1179656 | tf_op jit(solution)/shard_map/ppermute | solution.py:257
  30.3 27.2 %collective-permute-start.1 = (bf16[1536,128]{1,0:T(8,128)(2,1)}, bf16[1536,128]{1,0:T(8,128)(2,1)S(1)}, u32[]{:S(2)}, u32[]{:S(2)}) collective-permute-start(bf16[1536,128]{1,0:T(8,128)(2,1)} %bitcast.11), channel_id=1, source_target_pairs={{0,64},{64,128},{128,192},{192,0},{1,65},{65,129},{129,193},{193,1... | collective-permute-start | bytes 1179656 | tf_op jit(solution)/shard_map/ppermute | solution.py:257
  30.9 15.7 %collective-permute-start.9 = (bf16[400,128]{1,0:T(8,128)(2,1)S(1)}, bf16[400,128]{1,0:T(8,128)(2,1)S(1)}, u32[]{:S(2)}, u32[]{:S(2)}) collective-permute-start(bf16[400,128]{1,0:T(8,128)(2,1)S(1)} %line.1.s0), channel_id=1, source_target_pairs={{0,128},{64,192},{128,0},{192,64},{1,129},{65,193},{129,1},{193,65... | collective-permute-start | bytes 307208 | tf_op jit(solution)/shard_map/ppermute | solution.py:259
  34.5 16.5 %collective-permute-start.8 = (bf16[400,128]{1,0:T(8,128)(2,1)S(1)}, bf16[400,128]{1,0:T(8,128)(2,1)S(1)}, u32[]{:S(2)}, u32[]{:S(2)}) collective-permute-start(bf16[400,128]{1,0:T(8,128)(2,1)S(1)} %line.1.s0), channel_id=1, source_target_pairs={{0,64},{64,128},{128,192},{192,0},{1,65},{65,129},{129,193},{193,1... | collective-permute-start | bytes 307208 | tf_op jit(solution)/shard_map/ppermute | solution.py:259
  46.7 13.8 %collective-permute-start.11 = (bf16[768,128]{1,0:T(8,128)(2,1)S(1)}, bf16[768,128]{1,0:T(8,128)(2,1)S(1)}, u32[]{:S(2)}, u32[]{:S(2)}) collective-permute-start(bf16[768,128]{1,0:T(8,128)(2,1)S(1)} %slice.8), channel_id=1, source_target_pairs={{0,16},{16,32},{32,48},{48,0},{1,17},{17,33},{33,49},{49,1},{2,18}... | collective-permute-start | bytes 589832 | tf_op jit(solution)/shard_map/ppermute | solution.py:260
  51.0 9.5 %collective-permute-start.12 = (bf16[768,128]{1,0:T(8,128)(2,1)S(1)}, bf16[768,128]{1,0:T(8,128)(2,1)S(1)}, u32[]{:S(2)}, u32[]{:S(2)}) collective-permute-start(bf16[768,128]{1,0:T(8,128)(2,1)S(1)} %slice.9), channel_id=1, source_target_pairs={{0,48},{16,0},{32,16},{48,32},{1,49},{17,1},{33,17},{49,33},{2,50}... | collective-permute-start | bytes 589832 | tf_op jit(solution)/shard_map/ppermute | solution.py:261
  56.4 1.0 copy-start
  64.3 8.1 %collective-permute-start.13 = (f32[4,2,256,256]{3,2,1,0:T(8,128)S(1)}, f32[4,2,256,256]{3,2,1,0:T(8,128)S(1)}, u32[]{:S(2)}, u32[]{:S(2)}) collective-permute-start(f32[4,2,256,256]{3,2,1,0:T(8,128)S(1)} %send.1), channel_id=1, source_target_pairs={{0,1},{1,0},{2,3},{3,2},{4,5},{5,4},{6,7},{7,6},{8,9},{9,8},{10,11... | collective-permute-start | bytes 6291464 | tf_op jit(solution)/shard_map/ppermute | solution.py:265
  73.1 6.3 %collective-permute-start.14 = (bf16[256,256]{1,0:T(8,128)(2,1)S(1)}, bf16[256,256]{1,0:T(8,128)(2,1)S(1)}, u32[]{:S(2)}, u32[]{:S(2)}) collective-permute-start(bf16[256,256]{1,0:T(8,128)(2,1)S(1)} %get-tuple-element.20), channel_id=1, source_target_pairs={{0,4},{2,6},{4,8},{6,10},{8,12},{10,14},{12,0},{14,2},{1,5},{3,7},... | collective-permute-start | bytes 393224 | tf_op jit(solution)/shard_map/ppermute | solution.py:269
  73.4 6.8 %collective-permute-start.15 = (bf16[256,256]{1,0:T(8,128)(2,1)S(1)}, bf16[256,256]{1,0:T(8,128)(2,1)S(1)}, u32[]{:S(2)}, u32[]{:S(2)}) collective-permute-start(bf16[256,256]{1,0:T(8,128)(2,1)S(1)} %get-tuple-element.21), channel_id=1, source_target_pairs={{0,8},{2,10},{4,12},{6,14},{8,0},{10,2},{12,4},{14,6},{1,9},{3,11}... | collective-permute-start | bytes 393224 | tf_op jit(solution)/shard_map/ppermute | solution.py:269
  75.5 7.0 %collective-permute-start.16 = (bf16[256,256]{1,0:T(8,128)(2,1)S(1)}, bf16[256,256]{1,0:T(8,128)(2,1)S(1)}, u32[]{:S(2)}, u32[]{:S(2)}) collective-permute-start(bf16[256,256]{1,0:T(8,128)(2,1)S(1)} %get-tuple-element.22), channel_id=1, source_target_pairs={{0,12},{2,14},{4,0},{6,2},{8,4},{10,6},{12,8},{14,10},{1,13},{3,15... | collective-permute-start | bytes 393224 | tf_op jit(solution)/shard_map/ppermute | solution.py:269
  75.5 7.0 %collective-permute-start.17 = (bf16[256,256]{1,0:T(8,128)(2,1)S(1)}, bf16[256,256]{1,0:T(8,128)(2,1)S(1)}, u32[]{:S(2)}, u32[]{:S(2)}) collective-permute-start(bf16[256,256]{1,0:T(8,128)(2,1)S(1)} %get-tuple-element.23), channel_id=1, source_target_pairs={{0,2},{2,0},{4,6},{6,4},{8,10},{10,8},{12,14},{14,12},{1,3},{3,1},... | collective-permute-start | bytes 393224 | tf_op jit(solution)/shard_map/ppermute | solution.py:269
  77.0 6.4 %collective-permute-start.18 = (bf16[256,256]{1,0:T(8,128)(2,1)S(1)}, bf16[256,256]{1,0:T(8,128)(2,1)S(1)}, u32[]{:S(2)}, u32[]{:S(2)}) collective-permute-start(bf16[256,256]{1,0:T(8,128)(2,1)S(1)} %get-tuple-element.24), channel_id=1, source_target_pairs={{0,6},{2,4},{4,10},{6,8},{8,14},{10,12},{12,2},{14,0},{1,7},{3,5},... | collective-permute-start | bytes 393224 | tf_op jit(solution)/shard_map/ppermute | solution.py:269
  79.4 7.7 %collective-permute-start.19 = (bf16[256,256]{1,0:T(8,128)(2,1)S(1)}, bf16[256,256]{1,0:T(8,128)(2,1)S(1)}, u32[]{:S(2)}, u32[]{:S(2)}) collective-permute-start(bf16[256,256]{1,0:T(8,128)(2,1)S(1)} %get-tuple-element.25), channel_id=1, source_target_pairs={{0,10},{2,8},{4,14},{6,12},{8,2},{10,0},{12,6},{14,4},{1,11},{3,9}... | collective-permute-start | bytes 393224 | tf_op jit(solution)/shard_map/ppermute | solution.py:269
  80.2 10.2 %collective-permute-start.20 = (bf16[256,256]{1,0:T(8,128)(2,1)S(1)}, bf16[256,256]{1,0:T(8,128)(2,1)S(1)}, u32[]{:S(2)}, u32[]{:S(2)}) collective-permute-start(bf16[256,256]{1,0:T(8,128)(2,1)S(1)} %get-tuple-element.26), channel_id=1, source_target_pairs={{0,14},{2,12},{4,2},{6,0},{8,6},{10,4},{12,10},{14,8},{1,15},{3,13... | collective-permute-start | bytes 393224 | tf_op jit(solution)/shard_map/ppermute | solution.py:269
  90.5 17.0 %collective-permute-start.21 = (f32[256,256]{1,0:T(8,128)S(1)}, f32[256,256]{1,0:T(8,128)S(1)}, u32[]{:S(2)}, u32[]{:S(2)}) collective-permute-start(f32[256,256]{1,0:T(8,128)S(1)} %convert_add_fusion), channel_id=1, source_target_pairs={{0,0},{1,16},{2,2},{3,48},{4,4},{5,20},{6,66},{7,52},{8,8},{9,24},... | collective-permute-start | bytes 786440 | tf_op jit(solution)/shard_map/ppermute | solution.py:270

commit v9 on v8

--- a/solution.py
+++ b/solution.py
@@ -105,7 +105,7 @@
     return small[LIST0:SMALL, :].astype(F32).astype(jnp.int32)
 
 
-def build_kernel(sc_ref, t0, t1, t2, t3, z1, z3, s0, s1, s2, s3, dy, dz, met, lv, ls, sem):
+def build_kernel(sc_ref, t0, t1, t2, t3, z1, z3, f1, f3, s0, s1, s2, s3, dy, dz, met, lv, ls, sem):
     y, zh = sc_ref[0], sc_ref[1]
     for k, s in enumerate((s0, s1, s2, s3)):
         lv[16 * k : 16 * k + 16, :] = read_lists(s)
@@ -125,16 +125,20 @@
     for k, t in ((1, z1), (3, z3)):
         src = back(zh, k)
         fill_block(t, met, ls, NA * src, dz, src * ROWS)
+    src = back(zh, 2)
+    for a, f in enumerate((f1, f3)):
+        fill(f, 0, met, ls, NA * src + a, dz, src * ROWS + a * BS)
 
 
 def build(sc, tiles, zs, smalls):
     dense = jax.ShapeDtypeStruct((4 * ROWS, WIDE), BF16)
     return pl.pallas_call(
         build_kernel,
-        out_shape=(dense, dense, jax.ShapeDtypeStruct((QB + 1, AUXB, AUXB), BF16)),
-        in_specs=[SMEM] + [VMEM] * 10,
-        out_specs=(VMEM,) * 3,
+        out_shape=(dense, dense),
+        in_specs=[SMEM] + [VMEM] * 12,
+        out_specs=(VMEM,) * 2,
         scratch_shapes=[
+            pltpu.VMEM((QB + 1, AUXB, AUXB), BF16),
             pltpu.VMEM((64, 128), jnp.int32),
             pltpu.SMEM((64, 128), jnp.int32),
             pltpu.SemaphoreType.DMA,
@@ -144,57 +148,35 @@
     )(sc, *tiles, *zs, *smalls)
 
 
-def gram_kernel(flip, sc_ref, dy, dz, met, f1, f3, s0, out, far, lv, ls, sem):
+def gram_kernel(flip, sc_ref, dy, dz, out):
     zh, co = sc_ref[1], sc_ref[2]
     parity = 1 - co if flip else co
     opposite = back(zh, 2)
     factor = 1.0 / (QS * 16 * AUXB) ** 0.5
-
-    @pl.when(lax.rem(zh, 2) == parity)
-    def _():
-        lv[...] = read_lists(s0)
-        copy = pltpu.make_async_copy(lv, ls, sem)
-        copy.start()
-        far[...] = jnp.zeros_like(far)
-        copy.wait()
-        fill(f1, 0, met, ls, NA * opposite, far, 0)
-        fill(f3, 0, met, ls, NA * opposite + 1, far, BS)
-
-    def product(h, swapped, block):
-        for q in range(4):
-            row = dy[q * ROWS : (q + 1) * ROWS, 0:USED]
-            pair = (block, row) if swapped else (row, block)
-            prod = lax.dot_general(*pair, (((1,), (1,)), ((), ())), preferred_element_type=F32)
-            out[q, h] = prod * factor
-
     for h in range(2):
         p = 2 * h + parity
-
-        @pl.when(p == opposite)
-        def _():
-            product(h, True, far[:, 0:USED])
-
-        @pl.when(p != opposite)
-        def _():
-            at = pl.multiple_of(p * ROWS, ROWS)
-            product(h, False, dz[pl.ds(at, ROWS), 0:USED])
-
-
-def gram(flip, sc, dy, dz, met, f1, f3, small):
+        block = dz[pl.ds(pl.multiple_of(p * ROWS, ROWS), ROWS), 0:USED]
+
+        def product(swapped):
+            for q in range(4):
+                row = dy[q * ROWS : (q + 1) * ROWS, 0:USED]
+                pair = (block, row) if swapped else (row, block)
+                prod = lax.dot_general(*pair, (((1,), (1,)), ((), ())), preferred_element_type=F32)
+                out[q, h] = prod * factor
+
+        pl.when(p == opposite)(lambda: product(True))
+        pl.when(p != opposite)(lambda: product(False))
+
+
+def gram(flip, sc, dy, dz):
     return pl.pallas_call(
         functools.partial(gram_kernel, flip),
         out_shape=jax.ShapeDtypeStruct((4, 2, ROWS, ROWS), F32),
-        in_specs=[SMEM] + [VMEM] * 6,
-        out_specs=VMEM,
-        scratch_shapes=[
-            pltpu.VMEM((ROWS, WIDE), BF16),
-            pltpu.VMEM((16, 128), jnp.int32),
-            pltpu.SMEM((16, 128), jnp.int32),
-            pltpu.SemaphoreType.DMA,
-        ],
+        in_specs=[SMEM] + [VMEM] * 2,
+        out_specs=VMEM,
         compiler_params=PARAMS,
         name="send" if flip else "keep",
-    )(sc, dy, dz, met, f1, f3, small)
+    )(sc, dy, dz)
 
 
 def hold_kernel(tiles, late, out):
@@ -260,10 +242,11 @@
     f1 = lax.ppermute(z1[:HALF], "zh", ring(4, 1))
     f3 = lax.ppermute(z3[HALF:], "zh", ring(4, 3))
 
-    dy, dz, met = build(sc, [hold(tiles, z3)] + ys[1:], [z1, z3], smalls)
-    send = gram(True, sc, dy, dz, met, f1, f3, small)
+    mine = hold(tiles, part)
+    dy, dz = build(sc, [mine] + ys[1:], [z1, z3, f1, f3], smalls)
+    send = gram(True, sc, dy, dz)
     got = lax.ppermute(send, "co", ring(2, 1))
-    keep = gram(False, sc, dy, dz, met, f1, f3, small)
+    keep = gram(False, sc, dy, dz)
     total, *shares = share(sc, keep, got)
     for (k, w), piece in zip(STEPS[1:], shares):
         total = total + lax.ppermute(piece, ("x", "zl"), hop(k, w)).astype(F32)

time: 108 us -> 113 us (1.046)
  the two profiles are of different devices: /device:TPU:39 before, /device:TPU:56 now
where the time goes in v9:
time: 113 us
  waiting for transfers between devices  62.4 us (55%)
  starting transfers between devices  36.3 us (32%)
  Pallas kernels  10.1 us (9%)
  local copies, waits for them, and re-layouts  3.97 us (4%)
    ppermute x3, waiting for transfers between devices, local(): smalls = [small] + [lax.ppermute(small, 'y', ring(4, k)) for k in (1, 2, 3)]  15.9 us
    ppermute x3, waiting for transfers between devices, local(): parts = [part] + [lax.ppermute(part, 'zh', ring(4, k)) for k in (1, 2, 3)]  14.3 us
    ppermute x7, waiting for transfers between devices, local(): total = total + lax.ppermute(piece, ('x', 'zl'), hop(k, w)).astype(F32)  13.1 us
    ppermute x1, waiting for transfers between devices, local(): return lax.ppermute(total, ('y', 'zh', 'x', 'zl', 'co'), homes())  9.37 us
    ppermute x7, starting transfers between devices, local(): total = total + lax.ppermute(piece, ('x', 'zl'), hop(k, w)).astype(F32)  8.12 us
    ppermute x3, starting transfers between devices, local(): parts = [part] + [lax.ppermute(part, 'zh', ring(4, k)) for k in (1, 2, 3)]  6.75 us
    pallas_call x2, Pallas kernels, gram(): pl.pallas_call(functools.partial(gram_kernel, flip), out_shape=jax.ShapeD...  5.58 us
    ppermute x3, starting transfers between devices, local(): smalls = [small] + [lax.ppermute(small, 'y', ring(4, k)) for k in (1, 2, 3)]  5.52 us
  transfers between devices with their start and end apart: 22, of which 13 were waited for; matrix products, arithmetic and copies ran while one was open for 1% of the time, Pallas kernels for 3%

profile of v9, /device:TPU:56, one launch (start us, length us, event | category | flops | bytes accessed | tf_op | source)
XLA Modules:
  0.0 113.1 jit_solution(5288116835556329740)
XLA Ops:
  0.0 5.4 %collective-permute-start.4 = (bf16[1536,128]{1,0:T(8,128)(2,1)}, bf16[1536,128]{1,0:T(8,128)(2,1)S(1)}, u32[]{:S(2)}, u32[]{:S(2)}) collective-permute-start(bf16[1536,128]{1,0:T(8,128)(2,1)} %bitcast.7), channel_id=1, source_target_pairs={{0,48},{16,0},{32,16},{48,32},{1,49},{17,1},{33,17},{49,33},{2,50}... | collective-permute-start | bytes 1179656 | tf_op jit(solution)/shard_map/ppermute | solution.py:238
  5.4 0.7 copy.5.counts
  6.1 0.7 copy-done.1
  7.6 4.1 %collective-permute-start.9 = (bf16[104,128]{1,0:T(8,128)(2,1)S(1)}, bf16[104,128]{1,0:T(8,128)(2,1)S(1)}, u32[]{:S(2)}, u32[]{:S(2)}) collective-permute-start(bf16[104,128]{1,0:T(8,128)(2,1)S(1)} %pack.1.late.m0), channel_id=1, source_target_pairs={{0,48},{16,0},{32,16},{48,32},{1,49},{17,1},{33,17},{49,33},{2,50}... | collective-permute-start | bytes 79880 | tf_op jit(solution)/shard_map/ppermute | solution.py:235
  11.8 1.4 %collective-permute-start.8 = (bf16[104,128]{1,0:T(8,128)(2,1)S(1)}, bf16[104,128]{1,0:T(8,128)(2,1)S(1)}, u32[]{:S(2)}, u32[]{:S(2)}) collective-permute-start(bf16[104,128]{1,0:T(8,128)(2,1)S(1)} %pack.1.late.m0), channel_id=1, source_target_pairs={{0,32},{16,48},{32,0},{48,16},{1,33},{17,49},{33,1},{49,17},{2,34}... | collective-permute-start | bytes 79880 | tf_op jit(solution)/shard_map/ppermute | solution.py:235
  13.2 1.2 %collective-permute-start.7 = (bf16[104,128]{1,0:T(8,128)(2,1)S(1)}, bf16[104,128]{1,0:T(8,128)(2,1)S(1)}, u32[]{:S(2)}, u32[]{:S(2)}) collective-permute-start(bf16[104,128]{1,0:T(8,128)(2,1)S(1)} %pack.1.late.m0), channel_id=1, source_target_pairs={{0,16},{16,32},{32,48},{48,0},{1,17},{17,33},{33,49},{49,1},{2,18}... | collective-permute-start | bytes 79880 | tf_op jit(solution)/shard_map/ppermute | solution.py:235
  14.5 8.5 %collective-permute-done.9.m3 = bf16[104,128]{1,0:T(8,128)(2,1)S(1)} collective-permute-done((bf16[104,128]{1,0:T(8,128)(2,1)S(1)}, bf16[104,128]{1,0:T(8,128)(2,1)S(1)}, u32[]{:S(2)}, u32[]{:S(2)}) %collective-permute-start.9) | collective-permute-done | bytes 26656 | tf_op jit(solution)/shard_map/ppermute | solution.py:235
  23.3 5.5 %collective-permute-done.7.m1 = bf16[104,128]{1,0:T(8,128)(2,1)S(1)} collective-permute-done((bf16[104,128]{1,0:T(8,128)(2,1)S(1)}, bf16[104,128]{1,0:T(8,128)(2,1)S(1)}, u32[]{:S(2)}, u32[]{:S(2)}) %collective-permute-start.7) | collective-permute-done | bytes 26656 | tf_op jit(solution)/shard_map/ppermute | solution.py:235
  29.4 0.8 collective-permute-start.12
  30.7 3.5 %collective-permute-start.1 = (bf16[1536,128]{1,0:T(8,128)(2,1)}, bf16[1536,128]{1,0:T(8,128)(2,1)S(1)}, u32[]{:S(2)}, u32[]{:S(2)}) collective-permute-start(bf16[1536,128]{1,0:T(8,128)(2,1)} %bitcast.10), channel_id=1, source_target_pairs={{0,128},{64,192},{128,0},{192,64},{1,129},{65,193},{129,1},{193,65... | collective-permute-start | bytes 1179656 | tf_op jit(solution)/shard_map/ppermute | solution.py:239
  34.2 2.3 %collective-permute-done.12.s3 = bf16[400,128]{1,0:T(8,128)(2,1)S(1)} collective-permute-done((bf16[400,128]{1,0:T(8,128)(2,1)S(1)}, bf16[400,128]{1,0:T(8,128)(2,1)S(1)}, u32[]{:S(2)}, u32[]{:S(2)}) %collective-permute-start.12) | collective-permute-done | bytes 102432 | tf_op jit(solution)/shard_map/ppermute | solution.py:241
  36.4 1.6 %collective-permute-start.11 = (bf16[400,128]{1,0:T(8,128)(2,1)S(1)}, bf16[400,128]{1,0:T(8,128)(2,1)S(1)}, u32[]{:S(2)}, u32[]{:S(2)}) collective-permute-start(bf16[400,128]{1,0:T(8,128)(2,1)S(1)} %line.1.s0), channel_id=1, source_target_pairs={{0,128},{64,192},{128,0},{192,64},{1,129},{65,193},{129,1},{193,65... | collective-permute-start | bytes 307208 | tf_op jit(solution)/shard_map/ppermute | solution.py:241
  38.0 3.1 %collective-permute-start.10 = (bf16[400,128]{1,0:T(8,128)(2,1)S(1)}, bf16[400,128]{1,0:T(8,128)(2,1)S(1)}, u32[]{:S(2)}, u32[]{:S(2)}) collective-permute-start(bf16[400,128]{1,0:T(8,128)(2,1)S(1)} %line.1.s0), channel_id=1, source_target_pairs={{0,64},{64,128},{128,192},{192,0},{1,65},{65,129},{129,193},{193,1... | collective-permute-start | bytes 307208 | tf_op jit(solution)/shard_map/ppermute | solution.py:241
  41.2 12.1 %collective-permute-done.11.s2 = bf16[400,128]{1,0:T(8,128)(2,1)S(1)} collective-permute-done((bf16[400,128]{1,0:T(8,128)(2,1)S(1)}, bf16[400,128]{1,0:T(8,128)(2,1)S(1)}, u32[]{:S(2)}, u32[]{:S(2)}) %collective-permute-start.11) | collective-permute-done | bytes 102432 | tf_op jit(solution)/shard_map/ppermute | solution.py:241
  53.8 1.5 %collective-permute-done.10.s1 = bf16[400,128]{1,0:T(8,128)(2,1)S(1)} collective-permute-done((bf16[400,128]{1,0:T(8,128)(2,1)S(1)}, bf16[400,128]{1,0:T(8,128)(2,1)S(1)}, u32[]{:S(2)}, u32[]{:S(2)}) %collective-permute-start.10) | collective-permute-done | bytes 102432 | tf_op jit(solution)/shard_map/ppermute | solution.py:241
  55.3 0.9 collective-permute-start.5
  56.2 1.0 copy-done
  57.3 4.1 %collective-permute-done.6.f3 = bf16[768,128]{1,0:T(8,128)(2,1)S(1)} collective-permute-done((bf16[768,128]{1,0:T(8,128)(2,1)S(1)}, bf16[768,128]{1,0:T(8,128)(2,1)S(1)}, u32[]{:S(2)}, u32[]{:S(2)}) %collective-permute-start.6) | collective-permute-done | bytes 196640 | tf_op jit(solution)/shard_map/ppermute | solution.py:243
  61.4 4.2 %collective-permute-done.5.f1 = bf16[768,128]{1,0:T(8,128)(2,1)S(1)} collective-permute-done((bf16[768,128]{1,0:T(8,128)(2,1)S(1)}, bf16[768,128]{1,0:T(8,128)(2,1)S(1)}, u32[]{:S(2)}, u32[]{:S(2)}) %collective-permute-start.5) | collective-permute-done | bytes 196640 | tf_op jit(solution)/shard_map/ppermute | solution.py:242
  65.6 3.1 %build.1 = (bf16[1024,1664]{1,0:T(8,128)(2,1)S(1)}, bf16[1024,1664]{1,0:T(8,128)(2,1)S(1)}) custom-call(s32[5]{0:T(128)S(1)} %stack.23.sc_ref, bf16[1536,128]{1,0:T(8,128)(2,1)S(1)} %hold.1.t0, bf16[1536,128]{1,0:T(8,128)(2,1)S(1)} %collective-permute-done.t1, bf16[1536,128]{1,0:T(8,128)(2,1)S(1)} %collective-permute-done.1.t2, ...), custom_call_target="tpu_custom_call" | custom-call | tf_op jit(solution)/shard_map/build/pallas_call | solution.py:135
  68.7 2.9 %send.1 = f32[4,2,256,256]{3,2,1,0:T(8,128)S(1)} custom-call(s32[5]{0:T(128)S(1)} %stack.23.sc_ref, bf16[1024,1664]{1,0:T(8,128)(2,1)S(1)} %get-tuple-element.15.dy, bf16[1024,1664]{1,0:T(8,128)(2,1)S(1)} %get-tuple-element.16.dz), custom_call_target="tpu_custom_call" | custom-call | tf_op jit(solution)/shard_map/send/pallas_call | solution.py:172
  71.7 2.7 %keep.1 = f32[4,2,256,256]{3,2,1,0:T(8,128)S(1)} custom-call(s32[5]{0:T(128)S(1)} %stack.23.sc_ref, bf16[1024,1664]{1,0:T(8,128)(2,1)S(1)} %get-tuple-element.15.dy, bf16[1024,1664]{1,0:T(8,128)(2,1)S(1)} %get-tuple-element.16.dz), custom_call_target="tpu_custom_call" | custom-call | tf_op jit(solution)/shard_map/keep/pallas_call | solution.py:172
  74.4 1.4 %collective-permute-done.13.got = f32[4,2,256,256]{3,2,1,0:T(8,128)S(1)} collective-permute-done((f32[4,2,256,256]{3,2,1,0:T(8,128)S(1)}, f32[4,2,256,256]{3,2,1,0:T(8,128)S(1)}, u32[]{:S(2)}, u32[]{:S(2)}) %collective-permute-start.13) | collective-permute-done | bytes 2097184 | tf_op jit(solution)/shard_map/ppermute | solution.py:248
  76.6 1.6 %collective-permute-start.14 = (bf16[256,256]{1,0:T(8,128)(2,1)S(1)}, bf16[256,256]{1,0:T(8,128)(2,1)S(1)}, u32[]{:S(2)}, u32[]{:S(2)}) collective-permute-start(bf16[256,256]{1,0:T(8,128)(2,1)S(1)} %get-tuple-element.18), channel_id=1, source_target_pairs={{0,4},{2,6},{4,8},{6,10},{8,12},{10,14},{12,0},{14,2},{1,5},{3,7},... | collective-permute-start | bytes 393224 | tf_op jit(solution)/shard_map/ppermute | solution.py:252
  78.2 2.7 %collective-permute-start.15 = (bf16[256,256]{1,0:T(8,128)(2,1)S(1)}, bf16[256,256]{1,0:T(8,128)(2,1)S(1)}, u32[]{:S(2)}, u32[]{:S(2)}) collective-permute-start(bf16[256,256]{1,0:T(8,128)(2,1)S(1)} %get-tuple-element.19), channel_id=1, source_target_pairs={{0,8},{2,10},{4,12},{6,14},{8,0},{10,2},{12,4},{14,6},{1,9},{3,11}... | collective-permute-start | bytes 393224 | tf_op jit(solution)/shard_map/ppermute | solution.py:252
  80.9 1.4 %collective-permute-start.16 = (bf16[256,256]{1,0:T(8,128)(2,1)S(1)}, bf16[256,256]{1,0:T(8,128)(2,1)S(1)}, u32[]{:S(2)}, u32[]{:S(2)}) collective-permute-start(bf16[256,256]{1,0:T(8,128)(2,1)S(1)} %get-tuple-element.20), channel_id=1, source_target_pairs={{0,12},{2,14},{4,0},{6,2},{8,4},{10,6},{12,8},{14,10},{1,13},{3,15... | collective-permute-start | bytes 393224 | tf_op jit(solution)/shard_map/ppermute | solution.py:252
  82.4 2.0 %collective-permute-start.18 = (bf16[256,256]{1,0:T(8,128)(2,1)S(1)}, bf16[256,256]{1,0:T(8,128)(2,1)S(1)}, u32[]{:S(2)}, u32[]{:S(2)}) collective-permute-start(bf16[256,256]{1,0:T(8,128)(2,1)S(1)} %get-tuple-element.22), channel_id=1, source_target_pairs={{0,6},{2,4},{4,10},{6,8},{8,14},{10,12},{12,2},{14,0},{1,7},{3,5},... | collective-permute-start | bytes 393224 | tf_op jit(solution)/shard_map/ppermute | solution.py:252
  84.7 7.2 %collective-permute-done.15 = bf16[256,256]{1,0:T(8,128)(2,1)S(1)} collective-permute-done((bf16[256,256]{1,0:T(8,128)(2,1)S(1)}, bf16[256,256]{1,0:T(8,128)(2,1)S(1)}, u32[]{:S(2)}, u32[]{:S(2)}) %collective-permute-start.15) | collective-permute-done | bytes 131104 | tf_op jit(solution)/shard_map/ppermute | solution.py:252
  92.0 2.0 %collective-permute-done.19 = bf16[256,256]{1,0:T(8,128)(2,1)S(1)} collective-permute-done((bf16[256,256]{1,0:T(8,128)(2,1)S(1)}, bf16[256,256]{1,0:T(8,128)(2,1)S(1)}, u32[]{:S(2)}, u32[]{:S(2)}) %collective-permute-start.19) | collective-permute-done | bytes 131104 | tf_op jit(solution)/shard_map/ppermute | solution.py:252
  94.0 3.8 %collective-permute-done.20 = bf16[256,256]{1,0:T(8,128)(2,1)S(1)} collective-permute-done((bf16[256,256]{1,0:T(8,128)(2,1)S(1)}, bf16[256,256]{1,0:T(8,128)(2,1)S(1)}, u32[]{:S(2)}, u32[]{:S(2)}) %collective-permute-start.20) | collective-permute-done | bytes 131104 | tf_op jit(solution)/shard_map/ppermute | solution.py:252
  98.0 5.0 %collective-permute-start.21 = (f32[256,256]{1,0:T(8,128)S(1)}, f32[256,256]{1,0:T(8,128)S(1)}, u32[]{:S(2)}, u32[]{:S(2)}) collective-permute-start(f32[256,256]{1,0:T(8,128)S(1)} %convert_add_fusion), channel_id=1, source_target_pairs={{0,0},{1,16},{2,2},{3,48},{4,4},{5,20},{6,66},{7,52},{8,8},{9,24},... | collective-permute-start | bytes 786440 | tf_op jit(solution)/shard_map/ppermute | solution.py:253
  103.0 9.4 %collective-permute-done.21 = f32[256,256]{1,0:T(8,128)S(1)} collective-permute-done((f32[256,256]{1,0:T(8,128)S(1)}, f32[256,256]{1,0:T(8,128)S(1)}, u32[]{:S(2)}, u32[]{:S(2)}) %collective-permute-start.21) | collective-permute-done | bytes 262176 | tf_op jit(solution)/shard_map/ppermute | solution.py:253
  (31 shorter events, 4.7 us)
Async XLA Ops:
  0.0 36.4 %collective-permute-start.4 = (bf16[1536,128]{1,0:T(8,128)(2,1)}, bf16[1536,128]{1,0:T(8,128)(2,1)S(1)}, u32[]{:S(2)}, u32[]{:S(2)}) collective-permute-start(bf16[1536,128]{1,0:T(8,128)(2,1)} %bitcast.7), channel_id=1, source_target_pairs={{0,48},{16,0},{32,16},{48,32},{1,49},{17,1},{33,17},{49,33},{2,50}... | collective-permute-start | bytes 1179656 | tf_op jit(solution)/shard_map/ppermute | solution.py:238
  5.4 32.6 %collective-permute-start.3 = (bf16[1536,128]{1,0:T(8,128)(2,1)}, bf16[1536,128]{1,0:T(8,128)(2,1)S(1)}, u32[]{:S(2)}, u32[]{:S(2)}) collective-permute-start(bf16[1536,128]{1,0:T(8,128)(2,1)} %bitcast.8), channel_id=1, source_target_pairs={{0,16},{16,32},{32,48},{48,0},{1,17},{17,33},{33,49},{49,1},{2,18}... | collective-permute-start | bytes 1179656 | tf_op jit(solution)/shard_map/ppermute | solution.py:237
  6.1 0.7 copy-start.1
  6.9 0.7 copy-start.2
  7.6 15.4 %collective-permute-start.9 = (bf16[104,128]{1,0:T(8,128)(2,1)S(1)}, bf16[104,128]{1,0:T(8,128)(2,1)S(1)}, u32[]{:S(2)}, u32[]{:S(2)}) collective-permute-start(bf16[104,128]{1,0:T(8,128)(2,1)S(1)} %pack.1.late.m0), channel_id=1, source_target_pairs={{0,48},{16,0},{32,16},{48,32},{1,49},{17,1},{33,17},{49,33},{2,50}... | collective-permute-start | bytes 79880 | tf_op jit(solution)/shard_map/ppermute | solution.py:235
  11.8 11.5 %collective-permute-start.8 = (bf16[104,128]{1,0:T(8,128)(2,1)S(1)}, bf16[104,128]{1,0:T(8,128)(2,1)S(1)}, u32[]{:S(2)}, u32[]{:S(2)}) collective-permute-start(bf16[104,128]{1,0:T(8,128)(2,1)S(1)} %pack.1.late.m0), channel_id=1, source_target_pairs={{0,32},{16,48},{32,0},{48,16},{1,33},{17,49},{33,1},{49,17},{2,34}... | collective-permute-start | bytes 79880 | tf_op jit(solution)/shard_map/ppermute | solution.py:235
  13.2 15.6 %collective-permute-start.7 = (bf16[104,128]{1,0:T(8,128)(2,1)S(1)}, bf16[104,128]{1,0:T(8,128)(2,1)S(1)}, u32[]{:S(2)}, u32[]{:S(2)}) collective-permute-start(bf16[104,128]{1,0:T(8,128)(2,1)S(1)} %pack.1.late.m0), channel_id=1, source_target_pairs={{0,16},{16,32},{32,48},{48,0},{1,17},{17,33},{33,49},{49,1},{2,18}... | collective-permute-start | bytes 79880 | tf_op jit(solution)/shard_map/ppermute | solution.py:235
  29.4 7.0 %collective-permute-start.12 = (bf16[400,128]{1,0:T(8,128)(2,1)S(1)}, bf16[400,128]{1,0:T(8,128)(2,1)S(1)}, u32[]{:S(2)}, u32[]{:S(2)}) collective-permute-start(bf16[400,128]{1,0:T(8,128)(2,1)S(1)} %line.1.s0), channel_id=1, source_target_pairs={{0,192},{64,0},{128,64},{192,128},{1,193},{65,1},{129,65},{193,129... | collective-permute-start | bytes 307208 | tf_op jit(solution)/shard_map/ppermute | solution.py:241
  30.2 27.0 %collective-permute-start.2 = (bf16[1536,128]{1,0:T(8,128)(2,1)}, bf16[1536,128]{1,0:T(8,128)(2,1)S(1)}, u32[]{:S(2)}, u32[]{:S(2)}) collective-permute-start(bf16[1536,128]{1,0:T(8,128)(2,1)} %bitcast.9), channel_id=1, source_target_pairs={{0,192},{64,0},{128,64},{192,128},{1,193},{65,1},{129,65},{193,129... | collective-permute-start | bytes 1179656 | tf_op jit(solution)/shard_map/ppermute | solution.py:239
  30.7 26.6 %collective-permute-start.1 = (bf16[1536,128]{1,0:T(8,128)(2,1)}, bf16[1536,128]{1,0:T(8,128)(2,1)S(1)}, u32[]{:S(2)}, u32[]{:S(2)}) collective-permute-start(bf16[1536,128]{1,0:T(8,128)(2,1)} %bitcast.10), channel_id=1, source_target_pairs={{0,128},{64,192},{128,0},{192,64},{1,129},{65,193},{129,1},{193,65... | collective-permute-start | bytes 1179656 | tf_op jit(solution)/shard_map/ppermute | solution.py:239
  36.4 20.8 %collective-permute-start = (bf16[1536,128]{1,0:T(8,128)(2,1)}, bf16[1536,128]{1,0:T(8,128)(2,1)S(1)}, u32[]{:S(2)}, u32[]{:S(2)}) collective-permute-start(bf16[1536,128]{1,0:T(8,128)(2,1)} %bitcast.11), channel_id=1, source_target_pairs={{0,64},{64,128},{128,192},{192,0},{1,65},{65,129},{129,193},{193,1... | collective-permute-start | bytes 1179656 | tf_op jit(solution)/shard_map/ppermute | solution.py:239
  36.4 16.9 %collective-permute-start.11 = (bf16[400,128]{1,0:T(8,128)(2,1)S(1)}, bf16[400,128]{1,0:T(8,128)(2,1)S(1)}, u32[]{:S(2)}, u32[]{:S(2)}) collective-permute-start(bf16[400,128]{1,0:T(8,128)(2,1)S(1)} %line.1.s0), channel_id=1, source_target_pairs={{0,128},{64,192},{128,0},{192,64},{1,129},{65,193},{129,1},{193,65... | collective-permute-start | bytes 307208 | tf_op jit(solution)/shard_map/ppermute | solution.py:241
  38.0 17.3 %collective-permute-start.10 = (bf16[400,128]{1,0:T(8,128)(2,1)S(1)}, bf16[400,128]{1,0:T(8,128)(2,1)S(1)}, u32[]{:S(2)}, u32[]{:S(2)}) collective-permute-start(bf16[400,128]{1,0:T(8,128)(2,1)S(1)} %line.1.s0), channel_id=1, source_target_pairs={{0,64},{64,128},{128,192},{192,0},{1,65},{65,129},{129,193},{193,1... | collective-permute-start | bytes 307208 | tf_op jit(solution)/shard_map/ppermute | solution.py:241
  53.3 8.1 %collective-permute-start.6 = (bf16[768,128]{1,0:T(8,128)(2,1)S(1)}, bf16[768,128]{1,0:T(8,128)(2,1)S(1)}, u32[]{:S(2)}, u32[]{:S(2)}) collective-permute-start(bf16[768,128]{1,0:T(8,128)(2,1)S(1)} %slice.9), channel_id=1, source_target_pairs={{0,48},{16,0},{32,16},{48,32},{1,49},{17,1},{33,17},{49,33},{2,50}... | collective-permute-start | bytes 589832 | tf_op jit(solution)/shard_map/ppermute | solution.py:243
  55.3 10.3 %collective-permute-start.5 = (bf16[768,128]{1,0:T(8,128)(2,1)S(1)}, bf16[768,128]{1,0:T(8,128)(2,1)S(1)}, u32[]{:S(2)}, u32[]{:S(2)}) collective-permute-start(bf16[768,128]{1,0:T(8,128)(2,1)S(1)} %slice.8), channel_id=1, source_target_pairs={{0,16},{16,32},{32,48},{48,0},{1,17},{17,33},{33,49},{49,1},{2,18}... | collective-permute-start | bytes 589832 | tf_op jit(solution)/shard_map/ppermute | solution.py:242
  56.2 1.0 copy-start
  71.6 4.2 %collective-permute-start.13 = (f32[4,2,256,256]{3,2,1,0:T(8,128)S(1)}, f32[4,2,256,256]{3,2,1,0:T(8,128)S(1)}, u32[]{:S(2)}, u32[]{:S(2)}) collective-permute-start(f32[4,2,256,256]{3,2,1,0:T(8,128)S(1)} %send.1), channel_id=1, source_target_pairs={{0,1},{1,0},{2,3},{3,2},{4,5},{5,4},{6,7},{7,6},{8,9},{9,8},{10,11... | collective-permute-start | bytes 6291464 | tf_op jit(solution)/shard_map/ppermute | solution.py:248
  76.6 7.8 %collective-permute-start.14 = (bf16[256,256]{1,0:T(8,128)(2,1)S(1)}, bf16[256,256]{1,0:T(8,128)(2,1)S(1)}, u32[]{:S(2)}, u32[]{:S(2)}) collective-permute-start(bf16[256,256]{1,0:T(8,128)(2,1)S(1)} %get-tuple-element.18), channel_id=1, source_target_pairs={{0,4},{2,6},{4,8},{6,10},{8,12},{10,14},{12,0},{14,2},{1,5},{3,7},... | collective-permute-start | bytes 393224 | tf_op jit(solution)/shard_map/ppermute | solution.py:252
  78.2 13.8 %collective-permute-start.15 = (bf16[256,256]{1,0:T(8,128)(2,1)S(1)}, bf16[256,256]{1,0:T(8,128)(2,1)S(1)}, u32[]{:S(2)}, u32[]{:S(2)}) collective-permute-start(bf16[256,256]{1,0:T(8,128)(2,1)S(1)} %get-tuple-element.19), channel_id=1, source_target_pairs={{0,8},{2,10},{4,12},{6,14},{8,0},{10,2},{12,4},{14,6},{1,9},{3,11}... | collective-permute-start | bytes 393224 | tf_op jit(solution)/shard_map/ppermute | solution.py:252
  80.9 11.1 %collective-permute-start.16 = (bf16[256,256]{1,0:T(8,128)(2,1)S(1)}, bf16[256,256]{1,0:T(8,128)(2,1)S(1)}, u32[]{:S(2)}, u32[]{:S(2)}) collective-permute-start(bf16[256,256]{1,0:T(8,128)(2,1)S(1)} %get-tuple-element.20), channel_id=1, source_target_pairs={{0,12},{2,14},{4,0},{6,2},{8,4},{10,6},{12,8},{14,10},{1,13},{3,15... | collective-permute-start | bytes 393224 | tf_op jit(solution)/shard_map/ppermute | solution.py:252
  82.4 9.6 %collective-permute-start.17 = (bf16[256,256]{1,0:T(8,128)(2,1)S(1)}, bf16[256,256]{1,0:T(8,128)(2,1)S(1)}, u32[]{:S(2)}, u32[]{:S(2)}) collective-permute-start(bf16[256,256]{1,0:T(8,128)(2,1)S(1)} %get-tuple-element.21), channel_id=1, source_target_pairs={{0,2},{2,0},{4,6},{6,4},{8,10},{10,8},{12,14},{14,12},{1,3},{3,1},... | collective-permute-start | bytes 393224 | tf_op jit(solution)/shard_map/ppermute | solution.py:252
  82.4 9.6 %collective-permute-start.18 = (bf16[256,256]{1,0:T(8,128)(2,1)S(1)}, bf16[256,256]{1,0:T(8,128)(2,1)S(1)}, u32[]{:S(2)}, u32[]{:S(2)}) collective-permute-start(bf16[256,256]{1,0:T(8,128)(2,1)S(1)} %get-tuple-element.22), channel_id=1, source_target_pairs={{0,6},{2,4},{4,10},{6,8},{8,14},{10,12},{12,2},{14,0},{1,7},{3,5},... | collective-permute-start | bytes 393224 | tf_op jit(solution)/shard_map/ppermute | solution.py:252
  84.4 9.6 %collective-permute-start.19 = (bf16[256,256]{1,0:T(8,128)(2,1)S(1)}, bf16[256,256]{1,0:T(8,128)(2,1)S(1)}, u32[]{:S(2)}, u32[]{:S(2)}) collective-permute-start(bf16[256,256]{1,0:T(8,128)(2,1)S(1)} %get-tuple-element.23), channel_id=1, source_target_pairs={{0,10},{2,8},{4,14},{6,12},{8,2},{10,0},{12,6},{14,4},{1,11},{3,9}... | collective-permute-start | bytes 393224 | tf_op jit(solution)/shard_map/ppermute | solution.py:252
  92.0 5.9 %collective-permute-start.20 = (bf16[256,256]{1,0:T(8,128)(2,1)S(1)}, bf16[256,256]{1,0:T(8,128)(2,1)S(1)}, u32[]{:S(2)}, u32[]{:S(2)}) collective-permute-start(bf16[256,256]{1,0:T(8,128)(2,1)S(1)} %get-tuple-element.24), channel_id=1, source_target_pairs={{0,14},{2,12},{4,2},{6,0},{8,6},{10,4},{12,10},{14,8},{1,15},{3,13... | collective-permute-start | bytes 393224 | tf_op jit(solution)/shard_map/ppermute | solution.py:252
  98.0 14.4 %collective-permute-start.21 = (f32[256,256]{1,0:T(8,128)S(1)}, f32[256,256]{1,0:T(8,128)S(1)}, u32[]{:S(2)}, u32[]{:S(2)}) collective-permute-start(f32[256,256]{1,0:T(8,128)S(1)} %convert_add_fusion), channel_id=1, source_target_pairs={{0,0},{1,16},{2,2},{3,48},{4,4},{5,20},{6,66},{7,52},{8,8},{9,24},... | collective-permute-start | bytes 786440 | tf_op jit(solution)/shard_map/ppermute | solution.py:253

commit v10 on v9

--- a/solution.py
+++ b/solution.py
@@ -105,7 +105,7 @@
     return small[LIST0:SMALL, :].astype(F32).astype(jnp.int32)
 
 
-def build_kernel(sc_ref, t0, t1, t2, t3, z1, z3, f1, f3, s0, s1, s2, s3, dy, dz, met, lv, ls, sem):
+def build_kernel(sc_ref, t0, t1, t2, t3, z1, z3, f1, f3, s0, s1, s2, s3, ey, ez, dy, dz, met, lv, ls, sem):
     y, zh = sc_ref[0], sc_ref[1]
     for k, s in enumerate((s0, s1, s2, s3)):
         lv[16 * k : 16 * k + 16, :] = read_lists(s)
@@ -114,8 +114,6 @@
     for k, s in enumerate((s0, s1, s2, s3)):
         at = pl.multiple_of(back(y, k) * 4 * MROWS, 4 * MROWS)
         met[0:QB, pl.ds(at, 4 * MROWS), :] = s[0:LIST0, :].reshape(QB, 4 * MROWS, AUXB)
-    dy[...] = jnp.zeros_like(dy)
-    dz[...] = jnp.zeros_like(dz)
     copy.wait()
     fill_block(t0, met, ls, 8, dy, y * ROWS)
     mine = dy[pl.ds(pl.multiple_of(y * ROWS, ROWS), ROWS), :]
@@ -130,12 +128,12 @@
         fill(f, 0, met, ls, NA * src + a, dz, src * ROWS + a * BS)
 
 
-def build(sc, tiles, zs, smalls):
+def build(sc, tiles, zs, smalls, empty):
     dense = jax.ShapeDtypeStruct((4 * ROWS, WIDE), BF16)
     return pl.pallas_call(
         build_kernel,
         out_shape=(dense, dense),
-        in_specs=[SMEM] + [VMEM] * 12,
+        in_specs=[SMEM] + [VMEM] * 14,
         out_specs=(VMEM,) * 2,
         scratch_shapes=[
             pltpu.VMEM((QB + 1, AUXB, AUXB), BF16),
@@ -143,9 +141,10 @@
             pltpu.SMEM((64, 128), jnp.int32),
             pltpu.SemaphoreType.DMA,
         ],
+        input_output_aliases={13: 0, 14: 1},
         compiler_params=PARAMS,
         name="build",
-    )(sc, *tiles, *zs, *smalls)
+    )(sc, *tiles, *zs, *smalls, *empty)
 
 
 def gram_kernel(flip, sc_ref, dy, dz, out):
@@ -157,15 +156,22 @@
         p = 2 * h + parity
         block = dz[pl.ds(pl.multiple_of(p * ROWS, ROWS), ROWS), 0:USED]
 
-        def product(swapped):
+        @pl.when(p == opposite)
+        def _():
             for q in range(4):
                 row = dy[q * ROWS : (q + 1) * ROWS, 0:USED]
-                pair = (block, row) if swapped else (row, block)
-                prod = lax.dot_general(*pair, (((1,), (1,)), ((), ())), preferred_element_type=F32)
+                prod = lax.dot_general(
+                    block, row, (((1,), (1,)), ((), ())), preferred_element_type=F32
+                )
                 out[q, h] = prod * factor
 
-        pl.when(p == opposite)(lambda: product(True))
-        pl.when(p != opposite)(lambda: product(False))
+        @pl.when(p != opposite)
+        def _():
+            prod = lax.dot_general(
+                dy[:, 0:USED], block, (((1,), (1,)), ((), ())), preferred_element_type=F32
+            )
+            for q in range(4):
+                out[q, h] = prod[q * ROWS : (q + 1) * ROWS, :] * factor
 
 
 def gram(flip, sc, dy, dz):
@@ -179,16 +185,19 @@
     )(sc, dy, dz)
 
 
-def hold_kernel(tiles, late, out):
+def hold_kernel(tiles, late, out, dy, dz):
     out[...] = tiles[...]
+    dy[...] = jnp.zeros_like(dy)
+    dz[...] = jnp.zeros_like(dz)
 
 
 def hold(tiles, late):
+    dense = jax.ShapeDtypeStruct((4 * ROWS, WIDE), BF16)
     return pl.pallas_call(
         hold_kernel,
-        out_shape=jax.ShapeDtypeStruct(tiles.shape, tiles.dtype),
+        out_shape=(jax.ShapeDtypeStruct(tiles.shape, tiles.dtype), dense, dense),
         in_specs=[VMEM] * 2,
-        out_specs=VMEM,
+        out_specs=(VMEM,) * 3,
         compiler_params=PARAMS,
         name="hold",
     )(tiles, late)
@@ -242,8 +251,8 @@
     f1 = lax.ppermute(z1[:HALF], "zh", ring(4, 1))
     f3 = lax.ppermute(z3[HALF:], "zh", ring(4, 3))
 
-    mine = hold(tiles, part)
-    dy, dz = build(sc, [mine] + ys[1:], [z1, z3, f1, f3], smalls)
+    mine, *empty = hold(tiles, part)
+    dy, dz = build(sc, [mine] + ys[1:], [z1, z3, f1, f3], smalls, empty)
     send = gram(True, sc, dy, dz)
     got = lax.ppermute(send, "co", ring(2, 1))
     keep = gram(False, sc, dy, dz)

time: 113 us -> 113 us (level)
  no operation moved by 1% of the time
where the time goes in v10:
time: 113 us
  waiting for transfers between devices  62 us (55%)
  starting transfers between devices  36.3 us (32%)
  Pallas kernels  10.1 us (9%)
  local copies, waits for them, and re-layouts  3.97 us (4%)
    ppermute x3, waiting for transfers between devices, local(): smalls = [small] + [lax.ppermute(small, 'y', ring(4, k)) for k in (1, 2, 3)]  15.9 us
    ppermute x3, waiting for transfers between devices, local(): parts = [part] + [lax.ppermute(part, 'zh', ring(4, k)) for k in (1, 2, 3)]  14.3 us
    ppermute x7, waiting for transfers between devices, local(): total = total + lax.ppermute(piece, ('x', 'zl'), hop(k, w)).astype(F32)  13.1 us
    ppermute x1, waiting for transfers between devices, local(): return lax.ppermute(total, ('y', 'zh', 'x', 'zl', 'co'), homes())  9.37 us
    ppermute x7, starting transfers between devices, local(): total = total + lax.ppermute(piece, ('x', 'zl'), hop(k, w)).astype(F32)  8.11 us
    ppermute x3, starting transfers between devices, local(): parts = [part] + [lax.ppermute(part, 'zh', ring(4, k)) for k in (1, 2, 3)]  6.75 us
    pallas_call x2, Pallas kernels, gram(): pl.pallas_call(functools.partial(gram_kernel, flip), out_shape=jax.ShapeD...  5.53 us
    ppermute x3, starting transfers between devices, local(): smalls = [small] + [lax.ppermute(small, 'y', ring(4, k)) for k in (1, 2, 3)]  5.52 us
  transfers between devices with their start and end apart: 22, of which 13 were waited for; matrix products, arithmetic and copies ran while one was open for 1% of the time, Pallas kernels for 3%

profile of v10, /device:TPU:56, one launch (start us, length us, event | category | flops | bytes accessed | tf_op | source)
XLA Modules:
  0.0 112.6 jit_solution(9130336525491914099)
XLA Ops:
  0.0 5.4 %collective-permute-start.4 = (bf16[1536,128]{1,0:T(8,128)(2,1)}, bf16[1536,128]{1,0:T(8,128)(2,1)S(1)}, u32[]{:S(2)}, u32[]{:S(2)}) collective-permute-start(bf16[1536,128]{1,0:T(8,128)(2,1)} %bitcast.7), channel_id=1, source_target_pairs={{0,48},{16,0},{32,16},{48,32},{1,49},{17,1},{33,17},{49,33},{2,50}... | collective-permute-start | bytes 1179656 | tf_op jit(solution)/shard_map/ppermute | solution.py:247
  5.4 0.7 copy.7.counts
  6.1 0.7 copy-done.1
  7.6 4.1 %collective-permute-start.9 = (bf16[104,128]{1,0:T(8,128)(2,1)S(1)}, bf16[104,128]{1,0:T(8,128)(2,1)S(1)}, u32[]{:S(2)}, u32[]{:S(2)}) collective-permute-start(bf16[104,128]{1,0:T(8,128)(2,1)S(1)} %pack.1.late.m0), channel_id=1, source_target_pairs={{0,48},{16,0},{32,16},{48,32},{1,49},{17,1},{33,17},{49,33},{2,50}... | collective-permute-start | bytes 79880 | tf_op jit(solution)/shard_map/ppermute | solution.py:244
  11.8 1.4 %collective-permute-start.8 = (bf16[104,128]{1,0:T(8,128)(2,1)S(1)}, bf16[104,128]{1,0:T(8,128)(2,1)S(1)}, u32[]{:S(2)}, u32[]{:S(2)}) collective-permute-start(bf16[104,128]{1,0:T(8,128)(2,1)S(1)} %pack.1.late.m0), channel_id=1, source_target_pairs={{0,32},{16,48},{32,0},{48,16},{1,33},{17,49},{33,1},{49,17},{2,34}... | collective-permute-start | bytes 79880 | tf_op jit(solution)/shard_map/ppermute | solution.py:244
  13.2 1.2 %collective-permute-start.7 = (bf16[104,128]{1,0:T(8,128)(2,1)S(1)}, bf16[104,128]{1,0:T(8,128)(2,1)S(1)}, u32[]{:S(2)}, u32[]{:S(2)}) collective-permute-start(bf16[104,128]{1,0:T(8,128)(2,1)S(1)} %pack.1.late.m0), channel_id=1, source_target_pairs={{0,16},{16,32},{32,48},{48,0},{1,17},{17,33},{33,49},{49,1},{2,18}... | collective-permute-start | bytes 79880 | tf_op jit(solution)/shard_map/ppermute | solution.py:244
  14.5 8.5 %collective-permute-done.9.m3 = bf16[104,128]{1,0:T(8,128)(2,1)S(1)} collective-permute-done((bf16[104,128]{1,0:T(8,128)(2,1)S(1)}, bf16[104,128]{1,0:T(8,128)(2,1)S(1)}, u32[]{:S(2)}, u32[]{:S(2)}) %collective-permute-start.9) | collective-permute-done | bytes 26656 | tf_op jit(solution)/shard_map/ppermute | solution.py:244
  23.3 5.5 %collective-permute-done.7.m1 = bf16[104,128]{1,0:T(8,128)(2,1)S(1)} collective-permute-done((bf16[104,128]{1,0:T(8,128)(2,1)S(1)}, bf16[104,128]{1,0:T(8,128)(2,1)S(1)}, u32[]{:S(2)}, u32[]{:S(2)}) %collective-permute-start.7) | collective-permute-done | bytes 26656 | tf_op jit(solution)/shard_map/ppermute | solution.py:244
  29.4 0.8 collective-permute-start.12
  30.7 3.5 %collective-permute-start.1 = (bf16[1536,128]{1,0:T(8,128)(2,1)}, bf16[1536,128]{1,0:T(8,128)(2,1)S(1)}, u32[]{:S(2)}, u32[]{:S(2)}) collective-permute-start(bf16[1536,128]{1,0:T(8,128)(2,1)} %bitcast.10), channel_id=1, source_target_pairs={{0,128},{64,192},{128,0},{192,64},{1,129},{65,193},{129,1},{193,65... | collective-permute-start | bytes 1179656 | tf_op jit(solution)/shard_map/ppermute | solution.py:248
  34.2 2.3 %collective-permute-done.12.s3 = bf16[400,128]{1,0:T(8,128)(2,1)S(1)} collective-permute-done((bf16[400,128]{1,0:T(8,128)(2,1)S(1)}, bf16[400,128]{1,0:T(8,128)(2,1)S(1)}, u32[]{:S(2)}, u32[]{:S(2)}) %collective-permute-start.12) | collective-permute-done | bytes 102432 | tf_op jit(solution)/shard_map/ppermute | solution.py:250
  36.4 1.6 %collective-permute-start.11 = (bf16[400,128]{1,0:T(8,128)(2,1)S(1)}, bf16[400,128]{1,0:T(8,128)(2,1)S(1)}, u32[]{:S(2)}, u32[]{:S(2)}) collective-permute-start(bf16[400,128]{1,0:T(8,128)(2,1)S(1)} %line.1.s0), channel_id=1, source_target_pairs={{0,128},{64,192},{128,0},{192,64},{1,129},{65,193},{129,1},{193,65... | collective-permute-start | bytes 307208 | tf_op jit(solution)/shard_map/ppermute | solution.py:250
  38.0 3.1 %collective-permute-start.10 = (bf16[400,128]{1,0:T(8,128)(2,1)S(1)}, bf16[400,128]{1,0:T(8,128)(2,1)S(1)}, u32[]{:S(2)}, u32[]{:S(2)}) collective-permute-start(bf16[400,128]{1,0:T(8,128)(2,1)S(1)} %line.1.s0), channel_id=1, source_target_pairs={{0,64},{64,128},{128,192},{192,0},{1,65},{65,129},{129,193},{193,1... | collective-permute-start | bytes 307208 | tf_op jit(solution)/shard_map/ppermute | solution.py:250
  41.2 12.1 %collective-permute-done.11.s2 = bf16[400,128]{1,0:T(8,128)(2,1)S(1)} collective-permute-done((bf16[400,128]{1,0:T(8,128)(2,1)S(1)}, bf16[400,128]{1,0:T(8,128)(2,1)S(1)}, u32[]{:S(2)}, u32[]{:S(2)}) %collective-permute-start.11) | collective-permute-done | bytes 102432 | tf_op jit(solution)/shard_map/ppermute | solution.py:250
  53.8 1.5 %collective-permute-done.10.s1 = bf16[400,128]{1,0:T(8,128)(2,1)S(1)} collective-permute-done((bf16[400,128]{1,0:T(8,128)(2,1)S(1)}, bf16[400,128]{1,0:T(8,128)(2,1)S(1)}, u32[]{:S(2)}, u32[]{:S(2)}) %collective-permute-start.10) | collective-permute-done | bytes 102432 | tf_op jit(solution)/shard_map/ppermute | solution.py:250
  55.3 0.9 collective-permute-start.5
  56.2 1.0 copy-done
  57.8 3.6 %collective-permute-done.6.f3 = bf16[768,128]{1,0:T(8,128)(2,1)S(1)} collective-permute-done((bf16[768,128]{1,0:T(8,128)(2,1)S(1)}, bf16[768,128]{1,0:T(8,128)(2,1)S(1)}, u32[]{:S(2)}, u32[]{:S(2)}) %collective-permute-start.6) | collective-permute-done | bytes 196640 | tf_op jit(solution)/shard_map/ppermute | solution.py:252
  61.4 4.2 %collective-permute-done.5.f1 = bf16[768,128]{1,0:T(8,128)(2,1)S(1)} collective-permute-done((bf16[768,128]{1,0:T(8,128)(2,1)S(1)}, bf16[768,128]{1,0:T(8,128)(2,1)S(1)}, u32[]{:S(2)}, u32[]{:S(2)}) %collective-permute-start.5) | collective-permute-done | bytes 196640 | tf_op jit(solution)/shard_map/ppermute | solution.py:251
  65.6 2.6 %build.1 = (bf16[1024,1664]{1,0:T(8,128)(2,1)S(1)}, bf16[1024,1664]{1,0:T(8,128)(2,1)S(1)}) custom-call(s32[5]{0:T(128)S(1)} %stack.23.sc_ref, bf16[1536,128]{1,0:T(8,128)(2,1)S(1)} %get-tuple-element.18.t0, bf16[1536,128]{1,0:T(8,128)(2,1)S(1)} %collective-permute-done.t1, ...), custom_call_target="tpu_custom_call", output_to_operand_aliasing={{0}: (13, {}), {1}: (14, {})} | custom-call | tf_op jit(solution)/shard_map/build/pallas_call | solution.py:133
  68.3 2.8 %send.1 = f32[4,2,256,256]{3,2,1,0:T(8,128)S(1)} custom-call(s32[5]{0:T(128)S(1)} %stack.23.sc_ref, bf16[1024,1664]{1,0:T(8,128)(2,1)S(1)} %get-tuple-element.21.dy, bf16[1024,1664]{1,0:T(8,128)(2,1)S(1)} %get-tuple-element.22.dz), custom_call_target="tpu_custom_call" | custom-call | tf_op jit(solution)/shard_map/send/pallas_call | solution.py:178
  71.2 2.7 %keep.1 = f32[4,2,256,256]{3,2,1,0:T(8,128)S(1)} custom-call(s32[5]{0:T(128)S(1)} %stack.23.sc_ref, bf16[1024,1664]{1,0:T(8,128)(2,1)S(1)} %get-tuple-element.21.dy, bf16[1024,1664]{1,0:T(8,128)(2,1)S(1)} %get-tuple-element.22.dz), custom_call_target="tpu_custom_call" | custom-call | tf_op jit(solution)/shard_map/keep/pallas_call | solution.py:178
  73.9 1.5 %collective-permute-done.13.got = f32[4,2,256,256]{3,2,1,0:T(8,128)S(1)} collective-permute-done((f32[4,2,256,256]{3,2,1,0:T(8,128)S(1)}, f32[4,2,256,256]{3,2,1,0:T(8,128)S(1)}, u32[]{:S(2)}, u32[]{:S(2)}) %collective-permute-start.13) | collective-permute-done | bytes 2097184 | tf_op jit(solution)/shard_map/ppermute | solution.py:257
  76.1 1.6 %collective-permute-start.14 = (bf16[256,256]{1,0:T(8,128)(2,1)S(1)}, bf16[256,256]{1,0:T(8,128)(2,1)S(1)}, u32[]{:S(2)}, u32[]{:S(2)}) collective-permute-start(bf16[256,256]{1,0:T(8,128)(2,1)S(1)} %get-tuple-element.24), channel_id=1, source_target_pairs={{0,4},{2,6},{4,8},{6,10},{8,12},{10,14},{12,0},{14,2},{1,5},{3,7},... | collective-permute-start | bytes 393224 | tf_op jit(solution)/shard_map/ppermute | solution.py:261
  77.7 2.7 %collective-permute-start.15 = (bf16[256,256]{1,0:T(8,128)(2,1)S(1)}, bf16[256,256]{1,0:T(8,128)(2,1)S(1)}, u32[]{:S(2)}, u32[]{:S(2)}) collective-permute-start(bf16[256,256]{1,0:T(8,128)(2,1)S(1)} %get-tuple-element.25), channel_id=1, source_target_pairs={{0,8},{2,10},{4,12},{6,14},{8,0},{10,2},{12,4},{14,6},{1,9},{3,11}... | collective-permute-start | bytes 393224 | tf_op jit(solution)/shard_map/ppermute | solution.py:261
  80.4 1.4 %collective-permute-start.16 = (bf16[256,256]{1,0:T(8,128)(2,1)S(1)}, bf16[256,256]{1,0:T(8,128)(2,1)S(1)}, u32[]{:S(2)}, u32[]{:S(2)}) collective-permute-start(bf16[256,256]{1,0:T(8,128)(2,1)S(1)} %get-tuple-element.26), channel_id=1, source_target_pairs={{0,12},{2,14},{4,0},{6,2},{8,4},{10,6},{12,8},{14,10},{1,13},{3,15... | collective-permute-start | bytes 393224 | tf_op jit(solution)/shard_map/ppermute | solution.py:261
  81.9 2.0 %collective-permute-start.18 = (bf16[256,256]{1,0:T(8,128)(2,1)S(1)}, bf16[256,256]{1,0:T(8,128)(2,1)S(1)}, u32[]{:S(2)}, u32[]{:S(2)}) collective-permute-start(bf16[256,256]{1,0:T(8,128)(2,1)S(1)} %get-tuple-element.28), channel_id=1, source_target_pairs={{0,6},{2,4},{4,10},{6,8},{8,14},{10,12},{12,2},{14,0},{1,7},{3,5},... | collective-permute-start | bytes 393224 | tf_op jit(solution)/shard_map/ppermute | solution.py:261
  84.2 7.2 %collective-permute-done.15 = bf16[256,256]{1,0:T(8,128)(2,1)S(1)} collective-permute-done((bf16[256,256]{1,0:T(8,128)(2,1)S(1)}, bf16[256,256]{1,0:T(8,128)(2,1)S(1)}, u32[]{:S(2)}, u32[]{:S(2)}) %collective-permute-start.15) | collective-permute-done | bytes 131104 | tf_op jit(solution)/shard_map/ppermute | solution.py:261
  91.5 2.0 %collective-permute-done.19 = bf16[256,256]{1,0:T(8,128)(2,1)S(1)} collective-permute-done((bf16[256,256]{1,0:T(8,128)(2,1)S(1)}, bf16[256,256]{1,0:T(8,128)(2,1)S(1)}, u32[]{:S(2)}, u32[]{:S(2)}) %collective-permute-start.19) | collective-permute-done | bytes 131104 | tf_op jit(solution)/shard_map/ppermute | solution.py:261
  93.5 3.8 %collective-permute-done.20 = bf16[256,256]{1,0:T(8,128)(2,1)S(1)} collective-permute-done((bf16[256,256]{1,0:T(8,128)(2,1)S(1)}, bf16[256,256]{1,0:T(8,128)(2,1)S(1)}, u32[]{:S(2)}, u32[]{:S(2)}) %collective-permute-start.20) | collective-permute-done | bytes 131104 | tf_op jit(solution)/shard_map/ppermute | solution.py:261
  97.5 5.0 %collective-permute-start.21 = (f32[256,256]{1,0:T(8,128)S(1)}, f32[256,256]{1,0:T(8,128)S(1)}, u32[]{:S(2)}, u32[]{:S(2)}) collective-permute-start(f32[256,256]{1,0:T(8,128)S(1)} %convert_add_fusion), channel_id=1, source_target_pairs={{0,0},{1,16},{2,2},{3,48},{4,4},{5,20},{6,66},{7,52},{8,8},{9,24},... | collective-permute-start | bytes 786440 | tf_op jit(solution)/shard_map/ppermute | solution.py:262
  102.5 9.4 %collective-permute-done.21 = f32[256,256]{1,0:T(8,128)S(1)} collective-permute-done((f32[256,256]{1,0:T(8,128)S(1)}, f32[256,256]{1,0:T(8,128)S(1)}, u32[]{:S(2)}, u32[]{:S(2)}) %collective-permute-start.21) | collective-permute-done | bytes 262176 | tf_op jit(solution)/shard_map/ppermute | solution.py:262
  (31 shorter events, 5.2 us)
Async XLA Ops:
  0.0 36.4 %collective-permute-start.4 = (bf16[1536,128]{1,0:T(8,128)(2,1)}, bf16[1536,128]{1,0:T(8,128)(2,1)S(1)}, u32[]{:S(2)}, u32[]{:S(2)}) collective-permute-start(bf16[1536,128]{1,0:T(8,128)(2,1)} %bitcast.7), channel_id=1, source_target_pairs={{0,48},{16,0},{32,16},{48,32},{1,49},{17,1},{33,17},{49,33},{2,50}... | collective-permute-start | bytes 1179656 | tf_op jit(solution)/shard_map/ppermute | solution.py:247
  5.4 32.6 %collective-permute-start.3 = (bf16[1536,128]{1,0:T(8,128)(2,1)}, bf16[1536,128]{1,0:T(8,128)(2,1)S(1)}, u32[]{:S(2)}, u32[]{:S(2)}) collective-permute-start(bf16[1536,128]{1,0:T(8,128)(2,1)} %bitcast.8), channel_id=1, source_target_pairs={{0,16},{16,32},{32,48},{48,0},{1,17},{17,33},{33,49},{49,1},{2,18}... | collective-permute-start | bytes 1179656 | tf_op jit(solution)/shard_map/ppermute | solution.py:246
  6.1 0.7 copy-start.1
  6.9 0.7 copy-start.2
  7.6 15.4 %collective-permute-start.9 = (bf16[104,128]{1,0:T(8,128)(2,1)S(1)}, bf16[104,128]{1,0:T(8,128)(2,1)S(1)}, u32[]{:S(2)}, u32[]{:S(2)}) collective-permute-start(bf16[104,128]{1,0:T(8,128)(2,1)S(1)} %pack.1.late.m0), channel_id=1, source_target_pairs={{0,48},{16,0},{32,16},{48,32},{1,49},{17,1},{33,17},{49,33},{2,50}... | collective-permute-start | bytes 79880 | tf_op jit(solution)/shard_map/ppermute | solution.py:244
  11.8 11.5 %collective-permute-start.8 = (bf16[104,128]{1,0:T(8,128)(2,1)S(1)}, bf16[104,128]{1,0:T(8,128)(2,1)S(1)}, u32[]{:S(2)}, u32[]{:S(2)}) collective-permute-start(bf16[104,128]{1,0:T(8,128)(2,1)S(1)} %pack.1.late.m0), channel_id=1, source_target_pairs={{0,32},{16,48},{32,0},{48,16},{1,33},{17,49},{33,1},{49,17},{2,34}... | collective-permute-start | bytes 79880 | tf_op jit(solution)/shard_map/ppermute | solution.py:244
  13.2 15.6 %collective-permute-start.7 = (bf16[104,128]{1,0:T(8,128)(2,1)S(1)}, bf16[104,128]{1,0:T(8,128)(2,1)S(1)}, u32[]{:S(2)}, u32[]{:S(2)}) collective-permute-start(bf16[104,128]{1,0:T(8,128)(2,1)S(1)} %pack.1.late.m0), channel_id=1, source_target_pairs={{0,16},{16,32},{32,48},{48,0},{1,17},{17,33},{33,49},{49,1},{2,18}... | collective-permute-start | bytes 79880 | tf_op jit(solution)/shard_map/ppermute | solution.py:244
  29.4 7.0 %collective-permute-start.12 = (bf16[400,128]{1,0:T(8,128)(2,1)S(1)}, bf16[400,128]{1,0:T(8,128)(2,1)S(1)}, u32[]{:S(2)}, u32[]{:S(2)}) collective-permute-start(bf16[400,128]{1,0:T(8,128)(2,1)S(1)} %line.1.s0), channel_id=1, source_target_pairs={{0,192},{64,0},{128,64},{192,128},{1,193},{65,1},{129,65},{193,129... | collective-permute-start | bytes 307208 | tf_op jit(solution)/shard_map/ppermute | solution.py:250
  30.2 27.5 %collective-permute-start.2 = (bf16[1536,128]{1,0:T(8,128)(2,1)}, bf16[1536,128]{1,0:T(8,128)(2,1)S(1)}, u32[]{:S(2)}, u32[]{:S(2)}) collective-permute-start(bf16[1536,128]{1,0:T(8,128)(2,1)} %bitcast.9), channel_id=1, source_target_pairs={{0,192},{64,0},{128,64},{192,128},{1,193},{65,1},{129,65},{193,129... | collective-permute-start | bytes 1179656 | tf_op jit(solution)/shard_map/ppermute | solution.py:248
  30.7 27.1 %collective-permute-start.1 = (bf16[1536,128]{1,0:T(8,128)(2,1)}, bf16[1536,128]{1,0:T(8,128)(2,1)S(1)}, u32[]{:S(2)}, u32[]{:S(2)}) collective-permute-start(bf16[1536,128]{1,0:T(8,128)(2,1)} %bitcast.10), channel_id=1, source_target_pairs={{0,128},{64,192},{128,0},{192,64},{1,129},{65,193},{129,1},{193,65... | collective-permute-start | bytes 1179656 | tf_op jit(solution)/shard_map/ppermute | solution.py:248
  36.4 21.3 %collective-permute-start = (bf16[1536,128]{1,0:T(8,128)(2,1)}, bf16[1536,128]{1,0:T(8,128)(2,1)S(1)}, u32[]{:S(2)}, u32[]{:S(2)}) collective-permute-start(bf16[1536,128]{1,0:T(8,128)(2,1)} %bitcast.11), channel_id=1, source_target_pairs={{0,64},{64,128},{128,192},{192,0},{1,65},{65,129},{129,193},{193,1... | collective-permute-start | bytes 1179656 | tf_op jit(solution)/shard_map/ppermute | solution.py:248
  36.4 16.9 %collective-permute-start.11 = (bf16[400,128]{1,0:T(8,128)(2,1)S(1)}, bf16[400,128]{1,0:T(8,128)(2,1)S(1)}, u32[]{:S(2)}, u32[]{:S(2)}) collective-permute-start(bf16[400,128]{1,0:T(8,128)(2,1)S(1)} %line.1.s0), channel_id=1, source_target_pairs={{0,128},{64,192},{128,0},{192,64},{1,129},{65,193},{129,1},{193,65... | collective-permute-start | bytes 307208 | tf_op jit(solution)/shard_map/ppermute | solution.py:250
  38.0 17.3 %collective-permute-start.10 = (bf16[400,128]{1,0:T(8,128)(2,1)S(1)}, bf16[400,128]{1,0:T(8,128)(2,1)S(1)}, u32[]{:S(2)}, u32[]{:S(2)}) collective-permute-start(bf16[400,128]{1,0:T(8,128)(2,1)S(1)} %line.1.s0), channel_id=1, source_target_pairs={{0,64},{64,128},{128,192},{192,0},{1,65},{65,129},{129,193},{193,1... | collective-permute-start | bytes 307208 | tf_op jit(solution)/shard_map/ppermute | solution.py:250
  53.3 8.1 %collective-permute-start.6 = (bf16[768,128]{1,0:T(8,128)(2,1)S(1)}, bf16[768,128]{1,0:T(8,128)(2,1)S(1)}, u32[]{:S(2)}, u32[]{:S(2)}) collective-permute-start(bf16[768,128]{1,0:T(8,128)(2,1)S(1)} %slice.9), channel_id=1, source_target_pairs={{0,48},{16,0},{32,16},{48,32},{1,49},{17,1},{33,17},{49,33},{2,50}... | collective-permute-start | bytes 589832 | tf_op jit(solution)/shard_map/ppermute | solution.py:252
  55.3 10.3 %collective-permute-start.5 = (bf16[768,128]{1,0:T(8,128)(2,1)S(1)}, bf16[768,128]{1,0:T(8,128)(2,1)S(1)}, u32[]{:S(2)}, u32[]{:S(2)}) collective-permute-start(bf16[768,128]{1,0:T(8,128)(2,1)S(1)} %slice.8), channel_id=1, source_target_pairs={{0,16},{16,32},{32,48},{48,0},{1,17},{17,33},{33,49},{49,1},{2,18}... | collective-permute-start | bytes 589832 | tf_op jit(solution)/shard_map/ppermute | solution.py:251
  56.2 1.0 copy-start
  71.1 4.2 %collective-permute-start.13 = (f32[4,2,256,256]{3,2,1,0:T(8,128)S(1)}, f32[4,2,256,256]{3,2,1,0:T(8,128)S(1)}, u32[]{:S(2)}, u32[]{:S(2)}) collective-permute-start(f32[4,2,256,256]{3,2,1,0:T(8,128)S(1)} %send.1), channel_id=1, source_target_pairs={{0,1},{1,0},{2,3},{3,2},{4,5},{5,4},{6,7},{7,6},{8,9},{9,8},{10,11... | collective-permute-start | bytes 6291464 | tf_op jit(solution)/shard_map/ppermute | solution.py:257
  76.1 7.8 %collective-permute-start.14 = (bf16[256,256]{1,0:T(8,128)(2,1)S(1)}, bf16[256,256]{1,0:T(8,128)(2,1)S(1)}, u32[]{:S(2)}, u32[]{:S(2)}) collective-permute-start(bf16[256,256]{1,0:T(8,128)(2,1)S(1)} %get-tuple-element.24), channel_id=1, source_target_pairs={{0,4},{2,6},{4,8},{6,10},{8,12},{10,14},{12,0},{14,2},{1,5},{3,7},... | collective-permute-start | bytes 393224 | tf_op jit(solution)/shard_map/ppermute | solution.py:261
  77.7 13.8 %collective-permute-start.15 = (bf16[256,256]{1,0:T(8,128)(2,1)S(1)}, bf16[256,256]{1,0:T(8,128)(2,1)S(1)}, u32[]{:S(2)}, u32[]{:S(2)}) collective-permute-start(bf16[256,256]{1,0:T(8,128)(2,1)S(1)} %get-tuple-element.25), channel_id=1, source_target_pairs={{0,8},{2,10},{4,12},{6,14},{8,0},{10,2},{12,4},{14,6},{1,9},{3,11}... | collective-permute-start | bytes 393224 | tf_op jit(solution)/shard_map/ppermute | solution.py:261
  80.4 11.1 %collective-permute-start.16 = (bf16[256,256]{1,0:T(8,128)(2,1)S(1)}, bf16[256,256]{1,0:T(8,128)(2,1)S(1)}, u32[]{:S(2)}, u32[]{:S(2)}) collective-permute-start(bf16[256,256]{1,0:T(8,128)(2,1)S(1)} %get-tuple-element.26), channel_id=1, source_target_pairs={{0,12},{2,14},{4,0},{6,2},{8,4},{10,6},{12,8},{14,10},{1,13},{3,15... | collective-permute-start | bytes 393224 | tf_op jit(solution)/shard_map/ppermute | solution.py:261
  81.9 9.6 %collective-permute-start.17 = (bf16[256,256]{1,0:T(8,128)(2,1)S(1)}, bf16[256,256]{1,0:T(8,128)(2,1)S(1)}, u32[]{:S(2)}, u32[]{:S(2)}) collective-permute-start(bf16[256,256]{1,0:T(8,128)(2,1)S(1)} %get-tuple-element.27), channel_id=1, source_target_pairs={{0,2},{2,0},{4,6},{6,4},{8,10},{10,8},{12,14},{14,12},{1,3},{3,1},... | collective-permute-start | bytes 393224 | tf_op jit(solution)/shard_map/ppermute | solution.py:261
  81.9 9.6 %collective-permute-start.18 = (bf16[256,256]{1,0:T(8,128)(2,1)S(1)}, bf16[256,256]{1,0:T(8,128)(2,1)S(1)}, u32[]{:S(2)}, u32[]{:S(2)}) collective-permute-start(bf16[256,256]{1,0:T(8,128)(2,1)S(1)} %get-tuple-element.28), channel_id=1, source_target_pairs={{0,6},{2,4},{4,10},{6,8},{8,14},{10,12},{12,2},{14,0},{1,7},{3,5},... | collective-permute-start | bytes 393224 | tf_op jit(solution)/shard_map/ppermute | solution.py:261
  83.9 9.6 %collective-permute-start.19 = (bf16[256,256]{1,0:T(8,128)(2,1)S(1)}, bf16[256,256]{1,0:T(8,128)(2,1)S(1)}, u32[]{:S(2)}, u32[]{:S(2)}) collective-permute-start(bf16[256,256]{1,0:T(8,128)(2,1)S(1)} %get-tuple-element.29), channel_id=1, source_target_pairs={{0,10},{2,8},{4,14},{6,12},{8,2},{10,0},{12,6},{14,4},{1,11},{3,9}... | collective-permute-start | bytes 393224 | tf_op jit(solution)/shard_map/ppermute | solution.py:261
  91.5 5.9 %collective-permute-start.20 = (bf16[256,256]{1,0:T(8,128)(2,1)S(1)}, bf16[256,256]{1,0:T(8,128)(2,1)S(1)}, u32[]{:S(2)}, u32[]{:S(2)}) collective-permute-start(bf16[256,256]{1,0:T(8,128)(2,1)S(1)} %get-tuple-element.30), channel_id=1, source_target_pairs={{0,14},{2,12},{4,2},{6,0},{8,6},{10,4},{12,10},{14,8},{1,15},{3,13... | collective-permute-start | bytes 393224 | tf_op jit(solution)/shard_map/ppermute | solution.py:261
  97.5 14.4 %collective-permute-start.21 = (f32[256,256]{1,0:T(8,128)S(1)}, f32[256,256]{1,0:T(8,128)S(1)}, u32[]{:S(2)}, u32[]{:S(2)}) collective-permute-start(f32[256,256]{1,0:T(8,128)S(1)} %convert_add_fusion), channel_id=1, source_target_pairs={{0,0},{1,16},{2,2},{3,48},{4,4},{5,20},{6,66},{7,52},{8,8},{9,24},... | collective-permute-start | bytes 786440 | tf_op jit(solution)/shard_map/ppermute | solution.py:262
